TPU v7x, 256 devices: a whole 4x4x8 slice. The times are simulated.
256 devices in a mesh: ctx: 32 (over y, x, core), ch: 8 (over z).
Axes of the slice: x: 4, y: 4, z: 8, core: 2. Of those that a mesh axis runs over, the one named last changes fastest.
Arguments:
- hidden: bfloat16 [8192, 32768], P('ch', 'ctx'), may hold values from -24 to 24
- cotangent: bfloat16 [8192, 32768], P('ch', 'ctx'), may hold values from -24 to 24
- norm_gain: float32 [8192], P('ch'), may hold values from 0.5 to 1.5
- mr_filter: bfloat16 [512, 128], P('ch'), may hold values from -0.5 to 0.5
- residue: float32 [512, 16], P('ch'), may hold values from -1.5 to 1.5
- decay_rate: float32 [512, 16], P('ch'), may hold values from 4.7683716e-07 to 0.033
- skip_weight: float32 [8192], P('ch'), may hold values from -3 to 3
Outputs:
- grad_hidden: bfloat16 [8192, 32768], P('ch', 'ctx')
- grad_gain: float32 [8192], P('ch')
- grad_mr: float32 [512, 128], P('ch')
- grad_residue: float32 [512, 16], P('ch')
- grad_log_rate: float32 [512, 16], P('ch')
- grad_skip: float32 [8192], P('ch')
- grad_inv_rms: float32 [32768], P('ctx')
All inputs are finite; a program needn't handle non-finite values.
Results may differ from a plain program's by a relative error of at most 0.005.
Values may be sent and summed in bfloat16 or wider, within the bound.
No kernel may reach another device: no remote copies, remote signals or barrier semaphores. Data moves between devices by JAX's collectives and lax.ppermute only.
A program may use at most 192 MiB of HBM per device.

v0:
```python
import functools

import jax
import jax.numpy as jnp
from jax import lax
from jax.experimental import pallas as pl
from jax.experimental.pallas import tpu as pltpu
from jax.sharding import PartitionSpec as P

eps_norm = 1e-06
B = 128
GB = 8
f32 = jnp.float32
bf16 = jnp.bfloat16

NN = (((1,), (0,)), ((), ()))
NT = (((1,), (1,)), ((), ()))
TN = (((0,), (0,)), ((), ()))


def mm(a, b, dims):
    return lax.dot_general(a, b, dims, preferred_element_type=f32)


def split(x):
    hi = x.astype(bf16)
    lo = (x - hi.astype(f32)).astype(bf16)
    return hi, lo


def iotas(shape):
    return (
        lax.broadcasted_iota(jnp.int32, shape, 0),
        lax.broadcasted_iota(jnp.int32, shape, 1),
    )


def toeplitz(row):
    full = jnp.broadcast_to(row, (B, B))
    return pltpu.roll(full, 0, 1, stride=1, stride_axis=0)


def lag_sums(square):
    total = square[:8]
    for a in range(8, B, 8):
        total = total + pltpu.roll(square[a : a + 8], B - a, 1)
    row = lax.broadcasted_iota(jnp.int32, (8, B), 0)
    for bit in (1, 2, 4):
        total = jnp.where((row & bit) != 0, pltpu.roll(total, B - bit, 1), total)
    return jnp.sum(total, axis=0, keepdims=True)


def grads_kernel(nb, ct_ref, ctn_ref, e0_ref, g_ref, k_ref, d_ref, skip_ref, gml_ref, aft_ref):
    row, lane = iotas((B, B))
    upper = lane >= row
    step_lane = lax.broadcasted_iota(jnp.int32, (16, B), 1)
    steps = step_lane.astype(f32)
    third = (step_lane >= 32) & (step_lane < 48)
    zeros = jnp.zeros((16, B), f32)
    for g in range(GB):
        rows = pl.ds(16 * g, 16)
        blocks = [ct_ref[rows, pl.ds(B * b, B)] for b in range(nb)] + [ctn_ref[rows, :]]
        lhs = jnp.concatenate(blocks, axis=0)
        toe = jnp.where(upper, toeplitz(k_ref[pl.ds(g, 1), :]), 0.0)
        e0 = e0_ref[g]
        weights = jnp.concatenate([toe, e0, e0 * steps, e0, e0, zeros, zeros, zeros, zeros], axis=0)
        hi, lo = split(weights)
        out = mm(jnp.concatenate([lhs, lhs], axis=1), jnp.concatenate([hi, lo], axis=1), NT)
        near = out[:, :B]
        states = out[:, B:]
        decay = jnp.broadcast_to(d_ref[pl.ds(g, 1), :], (16, B))
        after = zeros
        found = [after]
        for b in range(nb, 0, -1):
            state = states[16 * b : 16 * b + 16]
            state = jnp.where(third, state * float(B * b), state)
            after = state + decay * after
            found.append(after)
        after_all = jnp.concatenate(found[::-1], axis=0)
        aft_ref[g] = after_all
        a_hi, a_lo = split(after_all)
        g_hi, g_lo = split(g_ref[g])
        none = jnp.zeros((16, B), bf16)
        far_w = jnp.concatenate(
            [g_hi, none, none, g_lo] + [none] * 4 + [g_hi] + [none] * 7, axis=0
        )
        far = mm(jnp.concatenate([a_hi, a_lo], axis=1), far_w, NN)
        skip = skip_ref[rows, :]
        direct = jnp.concatenate([skip] * (nb + 1), axis=0) * lhs.astype(f32)
        gml_ref[g] = near + far + direct


def moments_kernel(
    nb, h_ref, hp_ref, inv_ref, gain_ref, ct_ref, w_ref, ee_ref, d_ref, aft_ref,
    x_ref, skip_ref, corr_ref, mom_ref, end_ref,
):
    row, lane = iotas((B, B))
    upper = lane >= row
    step_lane = lax.broadcasted_iota(jnp.int32, (16, B), 1)
    togo = (B - step_lane).astype(f32)
    second = (step_lane >= 16) & (step_lane < 32)
    zeros = jnp.zeros((16, B), f32)
    for g in range(GB):
        rows = pl.ds(16 * g, 16)
        gain = gain_ref[rows, :]
        units = []
        for b in range(nb + 1):
            h = hp_ref[rows, :] if b == 0 else h_ref[rows, pl.ds(B * (b - 1), B)]
            inv = jnp.broadcast_to(inv_ref[pl.ds(b, 1), :], (16, B))
            units.append((h.astype(f32) * inv * gain).astype(bf16))
        x_all = jnp.concatenate(units, axis=0)
        x_ref[g] = x_all
        lhs = jnp.concatenate([x_all[: 16 * nb], x_all[16:]], axis=1)
        taps = toeplitz(w_ref[pl.ds(g, 1), :])
        cur = jnp.where(upper, taps, 0.0).astype(bf16)
        prev = jnp.where(upper, 0.0, taps).astype(bf16)
        mixed = mm(lhs, jnp.concatenate([prev, cur], axis=0), NN).astype(bf16)
        ct = jnp.concatenate([ct_ref[rows, pl.ds(B * b, B)] for b in range(nb)], axis=0)
        direct = ct.astype(f32) * mixed.astype(f32)
        total = direct[:16]
        for b in range(1, nb):
            total = total + direct[16 * b : 16 * b + 16]
        skip_ref[rows, :] = total
        pairs = mm(mixed, ct, TN)
        corr_ref[pl.ds(g, 1), :] = lag_sums(jnp.where(upper, pairs, 0.0))
        ee = ee_ref[g]
        weights = jnp.concatenate([ee, ee, ee, ee * togo, zeros, zeros, zeros, zeros], axis=0)
        hi, lo = split(weights)
        lifted = mm(
            jnp.concatenate([mixed, mixed], axis=1), jnp.concatenate([hi, lo], axis=1), NT
        )
        after = aft_ref[g]
        decay = jnp.broadcast_to(d_ref[pl.ds(g, 1), :], (16, B))
        plain = zeros
        scaled = zeros
        end = zeros
        for b in range(nb):
            lift = lifted[16 * b : 16 * b + 16]
            prod = lift * after[16 * b : 16 * b + 16]
            plain = plain + prod
            scaled = scaled + prod * float(B * (b + 1))
            end = decay * (end + jnp.where(second, lift * float(B * (nb - b)), lift))
        mom_ref[g] = jnp.concatenate(
            [plain[:8] + plain[8:], scaled[:8] + scaled[8:]], axis=0
        )
        end_ref[g] = end


def inputs_kernel(
    nb, gml_ref, a_ref, g_ref, dq_ref, h_ref, inv_ref, gain_ref, w_ref, x_ref,
    ig_ref, row_ref, gain_out_ref, tap_ref,
):
    row, lane = iotas((B, B))
    upper = lane >= row
    lower = row >= lane

    @pl.when(pl.program_id(0) == 0)
    def _():
        row_ref[...] = jnp.zeros_like(row_ref)

    sums = [row_ref[pl.ds(8 * b, 8), :] for b in range(nb)]
    for g in range(GB):
        rows = pl.ds(16 * g, 16)
        q = g % 4
        if q == 0:
            decay = jnp.broadcast_to(dq_ref[g // 4], (16, B))
            after = a_ref[g // 4]
            found = [after]
            for b in range(nb):
                after = after * decay
                found.append(after)
            after_all = jnp.concatenate(found[::-1], axis=0)
            a_hi, a_lo = split(after_all)
            a_lhs = jnp.concatenate([a_hi, a_lo, a_hi], axis=1)
        g_hi, g_lo = split(g_ref[g])
        none = jnp.zeros((16, B), bf16)
        pad = [none] * (2 * q)
        end = [none] * (7 - 2 * q)
        far_w = jnp.concatenate(
            pad + [g_hi] + end + pad + [g_hi] + end + pad + [g_lo] + end, axis=0
        )
        grad = (gml_ref[g] + mm(a_lhs, far_w, NN)).astype(bf16)
        taps = toeplitz(w_ref[pl.ds(g, 1), :])
        cur = jnp.where(upper, taps, 0.0).astype(bf16)
        prev = jnp.where(upper, 0.0, taps).astype(bf16)
        lhs = jnp.concatenate([grad[: 16 * nb], grad[16:]], axis=1)
        ig = mm(lhs, jnp.concatenate([cur, prev], axis=1), NT)
        ig_ref[g] = ig
        gain = gain_ref[rows, :]
        part = jnp.zeros((16, B), f32)
        for b in range(nb):
            h = h_ref[rows, pl.ds(B * b, B)].astype(f32)
            prod = ig[16 * b : 16 * b + 16] * h
            inv = jnp.broadcast_to(inv_ref[pl.ds(b + 1, 1), :], (16, B))
            part = part + prod * inv
            prod = prod * gain
            sums[b] = sums[b] + (prod[:8] + prod[8:])
        gain_out_ref[rows, :] = part
        x_all = x_ref[g]
        x_pair = jnp.concatenate([x_all[16:], x_all[: 16 * nb]], axis=1)
        pairs = mm(grad[: 16 * nb], x_pair, TN)
        tap_ref[pl.ds(g, 1), :] = lag_sums(jnp.where(lower, pairs[:, :B], pairs[:, B:]))
    for b in range(nb):
        row_ref[pl.ds(8 * b, 8), :] = sums[b]


def final_kernel(nb, width, ig_ref, h_ref, inv_ref, gain_ref, raw_ref, out_ref):
    for g in range(GB):
        rows = pl.ds(16 * g, 16)
        gain = gain_ref[rows, :]
        for b in range(nb):
            cols = pl.ds(B * b, B)
            inv = inv_ref[pl.ds(b + 1, 1), :]
            pull = raw_ref[pl.ds(b, 1), :] * inv * inv * (1.0 / width)
            h = h_ref[rows, cols].astype(f32)
            ig = ig_ref[g, pl.ds(16 * b, 16), :]
            out_ref[rows, cols] = (inv * (ig * gain - h * pull)).astype(bf16)


def scan_kernel(count, span, s_ref, r_ref, out_ref):
    lane = lax.broadcasted_iota(jnp.int32, (8, B), 1)
    ones = (lane % 32) >= 16
    decay = jnp.exp(jnp.broadcast_to(r_ref[...], (8, B)) * (-float(span)))
    x = jnp.zeros((8, B), f32)
    found = [None] * count
    found[count - 1] = x
    for i in range(count - 2, -1, -1):
        x = s_ref[i + 1] + decay * x
        found[i] = x
    v = jnp.zeros((8, B), f32)
    out_ref[count - 1] = x * 0.0
    for i in range(count - 2, -1, -1):
        v = decay * (v + float(span) * pltpu.roll(found[i + 1], 16, 1))
        out_ref[i] = found[i] + jnp.where(ones, v, 0.0)


def call(kernel, name, grid, ins, outs, args, flops=0, moved=0):
    return pl.pallas_call(
        kernel,
        name=name,
        grid=grid,
        in_specs=ins,
        out_specs=outs[0],
        out_shape=outs[1],
        compiler_params=pltpu.CompilerParams(vmem_limit_bytes=40 * 1024 * 1024),
        cost_estimate=pl.CostEstimate(flops=flops, bytes_accessed=moved, transcendentals=0),
    )(*args)


def ch_sum(x, count):
    seen = [x] + [
        lax.ppermute(x, "ch", [(i, i ^ k) for i in range(count)]) for k in range(1, count)
    ]
    while len(seen) > 1:
        seen = [seen[i] + seen[i + 1] for i in range(0, len(seen), 2)]
    return seen[0]


def ctx_sum(x, count):
    parts = lax.all_to_all(x.reshape(count, -1), "ctx", 0, 0, tiled=True)
    mine = jnp.sum(parts, axis=0, keepdims=True)
    return lax.all_to_all(
        jnp.broadcast_to(mine, parts.shape), "ctx", 0, 0, tiled=True
    ).reshape(x.shape)


def local(hidden, cotangent, norm_gain, mr_filter, residue, decay_rate, skip_weight):
    channels, tokens = hidden.shape
    groups, taps = mr_filter.shape
    modes = residue.shape[1]
    n_ctx = lax.axis_size("ctx")
    n_ch = lax.axis_size("ch")
    width = channels * n_ch
    scale = (tokens * n_ctx) ** (-0.5)
    nb = tokens // B
    grid = (groups // GB,)

    h_prev = lax.ppermute(hidden[:, tokens - B :], "ctx", [(i, i + 1) for i in range(n_ctx - 1)])
    ct_next = lax.ppermute(cotangent[:, :B], "ctx", [(i, i - 1) for i in range(1, n_ctx)])

    own_sq = jnp.sum(jnp.square(hidden.astype(f32)), axis=0).reshape(nb, B)
    edge_sq = jnp.sum(jnp.square(h_prev.astype(f32)), axis=0).reshape(1, B)
    squares = ch_sum(jnp.concatenate([edge_sq, own_sq], axis=0), n_ch)
    inverse = lax.rsqrt(squares / width + eps_norm)

    steps = jnp.arange(B, dtype=f32)
    amplitude = residue * jnp.sqrt(2.0 * decay_rate)
    e0 = jnp.exp(-decay_rate[:, :, None] * steps)
    ee = jnp.exp(-decay_rate[:, :, None] * (B - steps))
    g_table = amplitude[:, :, None] * ee
    k_table = jnp.sum(amplitude[:, :, None] * e0, axis=1)
    block_decay = jnp.exp(-decay_rate * B)
    d_table = jnp.tile(block_decay, (1, 8))
    dq_table = jnp.concatenate([block_decay, block_decay], axis=1).reshape(groups // 4, 1, B)
    gain_wide = jnp.broadcast_to(norm_gain[:, None], (channels, B))
    skip_wide = jnp.broadcast_to(skip_weight[:, None], (channels, B))

    wide = pl.BlockSpec((16 * GB, tokens), lambda i: (i, 0))
    thin = pl.BlockSpec((16 * GB, B), lambda i: (i, 0))
    per_mode = pl.BlockSpec((GB, 16, B), lambda i: (i, 0, 0))
    vector = pl.BlockSpec((GB, B), lambda i: (i, 0))
    tall = pl.BlockSpec((GB, 16 * (nb + 1), B), lambda i: (i, 0, 0))
    body = pl.BlockSpec((GB, 16 * nb, B), lambda i: (i, 0, 0))
    quad = pl.BlockSpec((GB // 4, 16, B), lambda i: (i, 0, 0))
    quad_row = pl.BlockSpec((GB // 4, 1, B), lambda i: (i, 0, 0))
    inv_spec = pl.BlockSpec((nb + 1, B), lambda i: (0, 0))
    row_spec = pl.BlockSpec((8 * nb, B), lambda i: (0, 0))
    raw_spec = pl.BlockSpec((nb, B), lambda i: (0, 0))
    shape = jax.ShapeDtypeStruct
    tall_f32 = shape((groups, 16 * (nb + 1), B), f32)

    grad_local, after_local = call(
        functools.partial(grads_kernel, nb),
        "grads",
        grid,
        [wide, thin, per_mode, per_mode, vector, vector, thin],
        ([tall, tall], [tall_f32, tall_f32]),
        (cotangent, ct_next, e0, g_table, k_table, d_table, skip_wide),
        flops=groups * 2 * 144 * 256 * 384,
        moved=14 * 2**20,
    )

    head = after_local[:, :16, :]
    state_zero = head[:, :, :16]
    state_one = head[:, :, 16:32] + head[:, :, 32:48] - B * state_zero
    packed = jnp.concatenate([state_zero, state_one], axis=2)
    packed = packed.reshape(groups // 4, 4, 16, 32).transpose(0, 2, 1, 3).reshape(n_ctx, 8, B)
    arrived = lax.all_to_all(packed, "ctx", 0, 0, tiled=True)
    rate_rows = jnp.concatenate([decay_rate, decay_rate], axis=1).reshape(groups // 4, B)
    my_rates = lax.dynamic_slice_in_dim(rate_rows, lax.axis_index("ctx") // 2, 1, 0)
    whole = pl.BlockSpec((n_ctx, 8, B), lambda: (0, 0, 0))
    scanned = call(
        functools.partial(scan_kernel, n_ctx, tokens),
        "scan",
        (),
        [whole, pl.BlockSpec((1, B), lambda: (0, 0))],
        (whole, shape((n_ctx, 8, B), f32)),
        (arrived, my_rates),
        moved=2**18,
    )
    after = lax.all_to_all(scanned, "ctx", 0, 0, tiled=True).reshape(groups // 4, 16, B)

    units, skip_part, corr, mom, ends = call(
        functools.partial(moments_kernel, nb),
        "moments",
        grid,
        [wide, thin, inv_spec, thin, wide, vector, per_mode, vector, tall],
        (
            [tall, thin, vector, per_mode, per_mode],
            [
                shape((groups, 16 * (nb + 1), B), bf16),
                shape((channels, B), f32),
                shape((groups, B), f32),
                shape((groups, 16, B), f32),
                shape((groups, 16, B), f32),
            ],
        ),
        (
            hidden, h_prev, inverse, gain_wide, cotangent, mr_filter.astype(f32), ee, d_table,
            after_local,
        ),
        flops=groups * 2 * 128 * 256 * 384,
        moved=14 * 2**20,
    )

    ig, row_part, gain_part, tap_part = call(
        functools.partial(inputs_kernel, nb),
        "inputs",
        grid,
        [tall, quad, per_mode, quad_row, wide, inv_spec, thin, vector, tall],
        (
            [body, row_spec, thin, vector],
            [
                shape((groups, 16 * nb, B), f32),
                shape((8 * nb, B), f32),
                shape((channels, B), f32),
                shape((groups, B), f32),
            ],
        ),
        (
            grad_local, after, g_table, dq_table, hidden, inverse, gain_wide,
            mr_filter.astype(f32), units,
        ),
        flops=groups * 2 * 144 * 256 * 512,
        moved=14 * 2**20,
    )

    raw = ch_sum(jnp.sum(row_part.reshape(nb, 8, B), axis=1), n_ch)
    grad_hidden = call(
        functools.partial(final_kernel, nb, width),
        "final",
        grid,
        [body, wide, inv_spec, thin, raw_spec],
        (wide, shape((channels, tokens), bf16)),
        (ig, hidden, inverse, gain_wide, raw),
        moved=8 * 2**20,
    )
    grad_inv_rms = (raw * width ** (-0.5)).reshape(tokens)

    after_g = after.reshape(groups // 4, 16, 4, 32).transpose(0, 2, 1, 3).reshape(groups, 16, 32)
    a_zero, a_one = after_g[:, :, :16], after_g[:, :, 16:]
    end_zero = ends[:, :, :16]
    end_one = ends[:, :, 16:32] + ends[:, :, 48:64]
    plain = jnp.sum(mom[:, :8], axis=1)
    scaled = jnp.sum(mom[:, 8:], axis=1)
    near = corr[:, None, :] * e0
    first = jnp.sum(near, axis=2) + plain[:, :16] + jnp.sum(end_zero * a_zero, axis=1)
    second = (
        jnp.sum(near * steps, axis=2)
        + plain[:, 16:32] + plain[:, 32:48] + plain[:, 48:64] - scaled[:, :16]
        + jnp.sum(end_one * a_zero + end_zero * a_one, axis=1)
    )
    flipped = jnp.concatenate([tap_part[:, :1], tap_part[:, :0:-1]], axis=1)
    payload = jnp.concatenate(
        [
            flipped.reshape(-1),
            jnp.sum(gain_part, axis=1),
            jnp.sum(skip_part, axis=1),
            first.reshape(-1),
            second.reshape(-1),
        ]
    )
    total = ctx_sum(payload, n_ctx)
    cuts = [groups * taps, channels, channels, groups * modes, groups * modes]
    pieces = []
    start = 0
    for size in cuts:
        pieces.append(total[start : start + size])
        start += size
    first_total = pieces[3].reshape(groups, modes)
    second_total = pieces[4].reshape(groups, modes)
    root_rate = jnp.sqrt(2.0 * decay_rate)
    return (
        grad_hidden,
        pieces[1] * scale,
        pieces[0].reshape(groups, taps) * scale,
        root_rate * first_total * scale,
        residue * root_rate * (0.5 * first_total - decay_rate * second_total) * scale,
        pieces[2] * scale,
        grad_inv_rms,
    )


def solution(mesh):
    return jax.shard_map(
        local,
        mesh=mesh,
        in_specs=(
            P("ch", "ctx"),
            P("ch", "ctx"),
            P("ch"),
            P("ch", None),
            P("ch", None),
            P("ch", None),
            P("ch"),
        ),
        out_specs=(
            P("ch", "ctx"),
            P("ch"),
            P("ch", None),
            P("ch", None),
            P("ch", None),
            P("ch"),
            P("ctx"),
        ),
        check_vma=False,
    )
```

profile of v0, /device:TPU:1, one launch (start us, length us, event | category | flops | bytes accessed | tf_op | source)
XLA Modules:
  0.0 181.1 jit_solution(4016327124778276369)
XLA Ops:
  0.7 1.8 %slice.83 = bf16[1024,128]{1,0:T(8,128)(2,1)} slice(bf16[1024,1024]{1,0:T(8,128)(2,1)} %ct_ref.3), slice={[0:1024], [0:128]} | slice | bytes 524288 | tf_op jit(solution)/shard_map/slice | solution.py:279
  2.5 5.1 %collective-permute-start = (bf16[1024,128]{1,0:T(8,128)(2,1)}, bf16[1024,128]{1,0:T(8,128)(2,1)}, u32[]{:S(2)}, u32[]{:S(2)}) collective-permute-start(bf16[1024,128]{1,0:T(8,128)(2,1)} %slice.83), channel_id=1, source_target_pairs={{8,0},{16,8},{24,16},{32,24},{40,32},{48,40},{56,48},{64,56},{72,6... | collective-permute-start | bytes 786440 | tf_op jit(solution)/shard_map/ppermute | solution.py:279
  7.6 1.7 slice.87
  9.3 1.9 %collective-permute-start.1 = (bf16[1024,128]{1,0:T(8,128)(2,1)}, bf16[1024,128]{1,0:T(8,128)(2,1)S(1)}, u32[]{:S(2)}, u32[]{:S(2)}) collective-permute-start(bf16[1024,128]{1,0:T(8,128)(2,1)} %slice.87), channel_id=1, source_target_pairs={{0,8},{8,16},{16,24},{24,32},{32,40},{40,48},{48,56},{56,64},{64,7... | collective-permute-start | bytes 786440 | tf_op jit(solution)/shard_map/ppermute | solution.py:278
  11.2 2.7 %multiply_reduce_fusion = f32[1024]{0:T(1024)} fusion(bf16[1024,1024]{1,0:T(8,128)(2,1)} %h_ref.5), kind=kLoop, calls=%fused_computation | loop fusion | flops 3144704 | bytes 2101248 | tf_op jit(solution)/shard_map/reduce_sum | solution.py:281
  14.8 1.1 multiply_reduce_fusion.4
  17.3 0.8 copy.79
  18.2 1.3 convert_element_type.12.w_ref
  19.7 1.3 pad_maximum_fusion.3
  21.0 5.4 %collective-permute-start.7 = (f32[9,128]{1,0:T(8,128)}, f32[9,128]{1,0:T(8,128)S(1)}, u32[]{:S(2)}, u32[]{:S(2)}) collective-permute-start(f32[9,128]{1,0:T(8,128)} %pad_maximum_fusion.3), channel_id=1, source_target_pairs={{0,6},{1,7},{2,4},{3,5},{4,2},{5,3},{6,0},{7,1},{8,14},{9,15},{10,... | collective-permute-start | bytes 13832 | tf_op jit(solution)/shard_map/ppermute | solution.py:252
  26.4 4.0 %collective-permute-start.5 = (f32[9,128]{1,0:T(8,128)}, f32[9,128]{1,0:T(8,128)}, u32[]{:S(2)}, u32[]{:S(2)}) collective-permute-start(f32[9,128]{1,0:T(8,128)} %pad_maximum_fusion.3), channel_id=1, source_target_pairs={{0,4},{1,5},{2,6},{3,7},{4,0},{5,1},{6,2},{7,3},{8,12},{9,13},{10,... | collective-permute-start | bytes 13832 | tf_op jit(solution)/shard_map/ppermute | solution.py:252
  30.4 1.4 collective-permute-start.6
  32.5 0.9 broadcast_in_dim.6.skip_ref
  33.4 16.9 %grads.1 = (f32[64,144,128]{2,1,0:T(8,128)S(1)}, f32[64,144,128]{2,1,0:T(8,128)S(1)}) custom-call(bf16[1024,1024]{1,0:T(8,128)(2,1)S(1)} %copy-done.6, bf16[1024,128]{1,0:T(8,128)(2,1)} %collective-permute-done.ctn_ref, f32[64,16,128]{2,1,0:T(8,128)S(1)} %get-tuple-element.76.e0_ref, f32[64,16,128]{2,1,0:T(8,128)S(1)} %get-tuple-element.70.g_ref, ...), custom_call_target="tpu_custom_call" | custom-call | flops 1811939328 | bytes 14680064 | tf_op jit(solution)/shard_map/grads/pallas_call | solution.py:238
  50.3 2.1 %copy-done.3 = f32[64,144,128]{2,1,0:T(8,128)} copy-done((f32[64,144,128]{2,1,0:T(8,128)}, f32[64,144,128]{2,1,0:T(8,128)S(1)}, u32[]{:S(2)}) %copy-start.3) | copy-done | bytes 4718616
  52.9 2.2 %copy-done.1 = f32[64,144,128]{2,1,0:T(8,128)} copy-done((f32[64,144,128]{2,1,0:T(8,128)}, f32[64,144,128]{2,1,0:T(8,128)S(1)}, u32[]{:S(2)}) %copy-start.1) | copy-done | bytes 4718616
  55.0 1.6 collective-permute-start.4
  57.4 0.9 reshape.91
  58.3 9.0 %all-to-all-start = ((f32[32,8,128]{2,1,0:T(8,128)}), f32[32,8,128]{2,1,0:T(8,128)S(1)}, u32[]{:S(2)}, u32[]{:S(2)}) async-start(f32[32,8,128]{2,1,0:T(8,128)} %reshape.91), calls=%async_computation | async-start | bytes 262144 | tf_op jit(solution)/shard_map/all_to_all | solution.py:328
  67.4 0.8 add_rsqrt_fusion.inv_ref
  68.2 0.9 broadcast_in_dim.7.gain_ref
  69.1 2.3 %copy-done.2 = f32[64,144,128]{2,1,0:T(8,128)S(1)} copy-done((f32[64,144,128]{2,1,0:T(8,128)S(1)}, f32[64,144,128]{2,1,0:T(8,128)}, u32[]{:S(2)}) %copy-start.2) | copy-done | bytes 4718616
  71.4 1.6 copy-done.7
  73.0 1.0 copy-done.12
  75.6 17.4 %moments.1 = (bf16[64,144,128]{2,1,0:T(8,128)(2,1)S(1)}, f32[1024,128]{1,0:T(8,128)S(1)}, f32[64,128]{1,0:T(8,128)S(1)}, f32[64,16,128]{2,1,0:T(8,128)S(1)}, f32[64,16,128]{2,1,0:T(8,128)S(1)}) custom-call(bf16[1024,1024]{1,0:T(8,128)(2,1)S(1)} %copy-done, bf16[1024,128]{1,0:T(8,128)(2,1)S(1)} %collective-permute-done.1.hp_ref, ...), custom_call_target="tpu_custom_call" | custom-call | flops 1610612736 | bytes 14680064 | tf_op jit(solution)/shard_map/moments/pallas_call | solution.py:238
  93.0 1.4 copy-done.8
  97.3 0.8 scan.1
  98.1 7.4 %all-to-all-start.1 = ((f32[32,8,128]{2,1,0:T(8,128)}), f32[32,8,128]{2,1,0:T(8,128)S(1)}, u32[]{:S(2)}, u32[]{:S(2)}) async-start(f32[32,8,128]{2,1,0:T(8,128)} %scan.1), calls=%async_computation.1 | async-start | bytes 262144 | tf_op jit(solution)/shard_map/all_to_all | solution.py:341
  105.5 1.3 multiply_reduce_fusion.1
  106.8 1.8 %reduce_sum.122 = f32[1024]{0:T(1024)} reduce(f32[1024,128]{1,0:T(8,128)} %copy-done.14, f32[]{:T(128)} %constant.16.clone.1), dimensions={1}, to_apply=%region_5.6 | reduce | flops 130048 | bytes 528388 | tf_op jit(solution)/shard_map/reduce_sum | solution.py:418
  108.6 1.2 slice_reduce_fusion
  109.8 3.3 %all-to-all-done.1 = f32[32,8,128]{2,1,0:T(8,128)S(1)} async-done(((f32[32,8,128]{2,1,0:T(8,128)}), f32[32,8,128]{2,1,0:T(8,128)S(1)}, u32[]{:S(2)}, u32[]{:S(2)}) %all-to-all-start.1) | async-done | bytes 131104 | tf_op jit(solution)/shard_map/all_to_all | solution.py:341
  113.1 1.7 copy-done.9
  114.8 1.0 copy-done.11
  116.6 19.0 %inputs.1 = (f32[64,128,128]{2,1,0:T(8,128)S(1)}, f32[64,128]{1,0:T(8,128)S(1)}, f32[1024,128]{1,0:T(8,128)S(1)}, f32[64,128]{1,0:T(8,128)S(1)}) custom-call(f32[64,144,128]{2,1,0:T(8,128)} %copy-done.3, f32[16,16,128]{2,1,0:T(8,128)S(1)} %bitcast.24, f32[64,16,128]{2,1,0:T(8,128)S(1)} %copy-done.11, f32[16,1,128]{2,1,0:T(1,128)S(1)} %bitcast.26, ...), custom_call_target="tpu_custom_call" | custom-call | flops 2415919104 | bytes 14680064 | tf_op jit(solution)/shard_map/inputs/pallas_call | solution.py:238
  135.6 1.9 %copy-done.4 = f32[64,128,128]{2,1,0:T(8,128)} copy-done((f32[64,128,128]{2,1,0:T(8,128)}, f32[64,128,128]{2,1,0:T(8,128)S(1)}, u32[]{:S(2)}) %copy-start.4) | copy-done | bytes 4194328
  138.4 1.3 reduce_sum.121
  139.7 1.1 reshape_reshape.3
  140.8 1.1 copy.82
  145.7 4.1 %all-to-all-start.2 = ((f32[32,1,384]{2,1,0:T(1,128)}), f32[32,1,384]{2,1,0:T(1,128)S(1)}, u32[]{:S(2)}, u32[]{:S(2)}) async-start(f32[32,1,384]{2,1,0:T(1,128)} %bitcast.12), calls=%async_computation.2 | async-start | bytes 98304 | tf_op jit(solution)/shard_map/all_to_all | solution.py:260
  149.8 3.7 %collective-permute-start.14 = (f32[8,128]{1,0:T(8,128)S(1)}, f32[8,128]{1,0:T(8,128)S(1)}, u32[]{:S(2)}, u32[]{:S(2)}) collective-permute-start(f32[8,128]{1,0:T(8,128)S(1)} %bitcast_reduce_fusion), channel_id=1, source_target_pairs={{0,6},{1,7},{2,4},{3,5},{4,2},{5,3},{6,0},{7,1},{8,14},{9,15},{10,... | collective-permute-start | bytes 12296 | tf_op jit(solution)/shard_map/ppermute | solution.py:252
  153.4 4.0 %collective-permute-start.12 = (f32[8,128]{1,0:T(8,128)S(1)}, f32[8,128]{1,0:T(8,128)S(1)}, u32[]{:S(2)}, u32[]{:S(2)}) collective-permute-start(f32[8,128]{1,0:T(8,128)S(1)} %bitcast_reduce_fusion), channel_id=1, source_target_pairs={{0,4},{1,5},{2,6},{3,7},{4,0},{5,1},{6,2},{7,3},{8,12},{9,13},{10,... | collective-permute-start | bytes 12296 | tf_op jit(solution)/shard_map/ppermute | solution.py:252
  157.4 1.5 collective-permute-start.13
  159.6 1.6 collective-permute-start.11
  162.3 9.2 %all-to-all-start.3 = ((f32[32,1,384]{2,1,0:T(1,128)}), f32[32,1,384]{2,1,0:T(1,128)S(1)}, u32[]{:S(2)}, u32[]{:S(2)}) async-start(f32[32,1,384]{2,1,0:T(1,128)} %broadcast_in_dim.8), calls=%async_computation.3 | async-start | bytes 98304 | tf_op jit(solution)/shard_map/all_to_all | solution.py:262
  172.2 2.2 %copy-done.5 = f32[64,128,128]{2,1,0:T(8,128)S(1)} copy-done((f32[64,128,128]{2,1,0:T(8,128)S(1)}, f32[64,128,128]{2,1,0:T(8,128)}, u32[]{:S(2)}) %copy-start.5) | copy-done | bytes 4194328
  174.4 3.5 %final.1 = bf16[1024,1024]{1,0:T(8,128)(2,1)} custom-call(f32[64,128,128]{2,1,0:T(8,128)S(1)} %copy-done.5, bf16[1024,1024]{1,0:T(8,128)(2,1)S(1)} %copy-done, f32[9,128]{1,0:T(8,128)S(1)} %add_rsqrt_fusion.inv_ref, f32[1024,128]{1,0:T(8,128)S(1)} %broadcast_in_dim.7.gain_ref, f32[8,128]{1,0:T(8,128)S(1)} %get-tuple-element.64.raw_ref), custom_call_target="tpu_custom_call" | custom-call | bytes 8388608 | tf_op jit(solution)/shard_map/final/pallas_call | solution.py:238
  177.8 1.0 all-to-all-done.3
  (113 shorter events, 18.9 us)
Async XLA Ops:
  0.6 32.7 %copy-start.6 = (bf16[1024,1024]{1,0:T(8,128)(2,1)S(1)}, bf16[1024,1024]{1,0:T(8,128)(2,1)}, u32[]{:S(2)}) copy-start(bf16[1024,1024]{1,0:T(8,128)(2,1)} %ct_ref.3) | copy-start | bytes 6291460
  0.6 15.3 %copy-start.23 = (f32[64,16]{0,1:T(8,128)S(1)}, f32[64,16]{0,1:T(8,128)}, u32[]{:S(2)}) copy-start(f32[64,16]{0,1:T(8,128)} %param.12) | copy-start | bytes 12292
  2.5 29.3 %collective-permute-start = (bf16[1024,128]{1,0:T(8,128)(2,1)}, bf16[1024,128]{1,0:T(8,128)(2,1)}, u32[]{:S(2)}, u32[]{:S(2)}) collective-permute-start(bf16[1024,128]{1,0:T(8,128)(2,1)} %slice.83), channel_id=1, source_target_pairs={{8,0},{16,8},{24,16},{32,24},{40,32},{48,40},{56,48},{64,56},{72,6... | collective-permute-start | bytes 786440 | tf_op jit(solution)/shard_map/ppermute | solution.py:279
  9.3 10.3 %collective-permute-start.1 = (bf16[1024,128]{1,0:T(8,128)(2,1)}, bf16[1024,128]{1,0:T(8,128)(2,1)S(1)}, u32[]{:S(2)}, u32[]{:S(2)}) collective-permute-start(bf16[1024,128]{1,0:T(8,128)(2,1)} %slice.87), channel_id=1, source_target_pairs={{0,8},{8,16},{16,24},{24,32},{32,40},{40,48},{48,56},{56,64},{64,7... | collective-permute-start | bytes 786440 | tf_op jit(solution)/shard_map/ppermute | solution.py:278
  14.8 2.5 %copy-start.22 = (f32[64,16]{1,0:T(8,128)}, f32[64,16]{1,0:T(8,128)S(1)}, u32[]{:S(2)}) copy-start(f32[64,16]{1,0:T(8,128)S(1)} %copy.74) | copy-start | bytes 12292
  15.9 36.9 %copy-start.10 = (f32[64,16,128]{2,1,0:T(8,128)}, f32[64,16,128]{2,1,0:T(8,128)S(1)}, u32[]{:S(2)}) copy-start(f32[64,16,128]{2,1,0:T(8,128)S(1)} %get-tuple-element.70.g_ref) | copy-start | bytes 1572868
  17.3 35.5 %copy-start.18 = (f32[64,128]{1,0:T(8,128)}, f32[64,128]{1,0:T(8,128)S(1)}, u32[]{:S(2)}) copy-start(f32[64,128]{1,0:T(8,128)S(1)} %copy.76.d_ref) | copy-start | bytes 98308
  21.0 34.1 %collective-permute-start.7 = (f32[9,128]{1,0:T(8,128)}, f32[9,128]{1,0:T(8,128)S(1)}, u32[]{:S(2)}, u32[]{:S(2)}) collective-permute-start(f32[9,128]{1,0:T(8,128)} %pad_maximum_fusion.3), channel_id=1, source_target_pairs={{0,6},{1,7},{2,4},{3,5},{4,2},{5,3},{6,0},{7,1},{8,14},{9,15},{10,... | collective-permute-start | bytes 13832 | tf_op jit(solution)/shard_map/ppermute | solution.py:252
  26.4 30.3 %collective-permute-start.8 = (f32[9,128]{1,0:T(8,128)}, f32[9,128]{1,0:T(8,128)S(1)}, u32[]{:S(2)}, u32[]{:S(2)}) collective-permute-start(f32[9,128]{1,0:T(8,128)} %pad_maximum_fusion.3), channel_id=1, source_target_pairs={{0,7},{1,6},{2,5},{3,4},{4,3},{5,2},{6,1},{7,0},{8,15},{9,14},{10,... | collective-permute-start | bytes 13832 | tf_op jit(solution)/shard_map/ppermute | solution.py:252
  26.4 41.0 %collective-permute-start.5 = (f32[9,128]{1,0:T(8,128)}, f32[9,128]{1,0:T(8,128)}, u32[]{:S(2)}, u32[]{:S(2)}) collective-permute-start(f32[9,128]{1,0:T(8,128)} %pad_maximum_fusion.3), channel_id=1, source_target_pairs={{0,4},{1,5},{2,6},{3,7},{4,0},{5,1},{6,2},{7,3},{8,12},{9,13},{10,... | collective-permute-start | bytes 13832 | tf_op jit(solution)/shard_map/ppermute | solution.py:252
  30.4 36.9 %collective-permute-start.6 = (f32[9,128]{1,0:T(8,128)}, f32[9,128]{1,0:T(8,128)}, u32[]{:S(2)}, u32[]{:S(2)}) collective-permute-start(f32[9,128]{1,0:T(8,128)} %pad_maximum_fusion.3), channel_id=1, source_target_pairs={{0,5},{1,4},{2,7},{3,6},{4,1},{5,0},{6,3},{7,2},{8,13},{9,12},{10,... | collective-permute-start | bytes 13832 | tf_op jit(solution)/shard_map/ppermute | solution.py:252
  31.7 35.6 %collective-permute-start.3 = (f32[9,128]{1,0:T(8,128)}, f32[9,128]{1,0:T(8,128)}, u32[]{:S(2)}, u32[]{:S(2)}) collective-permute-start(f32[9,128]{1,0:T(8,128)} %pad_maximum_fusion.3), channel_id=1, source_target_pairs={{0,2},{1,3},{2,0},{3,1},{4,6},{5,7},{6,4},{7,5},{8,10},{9,11},{10,... | collective-permute-start | bytes 13832 | tf_op jit(solution)/shard_map/ppermute | solution.py:252
  50.3 2.1 %copy-start.3 = (f32[64,144,128]{2,1,0:T(8,128)}, f32[64,144,128]{2,1,0:T(8,128)S(1)}, u32[]{:S(2)}) copy-start(f32[64,144,128]{2,1,0:T(8,128)S(1)} %get-tuple-element.18.gml_ref) | copy-start | bytes 14155780
  52.5 14.9 %copy-start.25 = (f32[1024]{0:T(1024)S(1)}, f32[1024]{0:T(1024)}, u32[]{:S(2)}) copy-start(f32[1024]{0:T(1024)} %multiply_reduce_fusion) | copy-start | bytes 12292
  52.5 16.6 %copy-start = (bf16[1024,1024]{1,0:T(8,128)(2,1)S(1)}, bf16[1024,1024]{1,0:T(8,128)(2,1)}, u32[]{:S(2)}) copy-start(bf16[1024,1024]{1,0:T(8,128)(2,1)} %h_ref.5) | copy-start | bytes 6291460
  52.8 2.2 %copy-start.1 = (f32[64,144,128]{2,1,0:T(8,128)}, f32[64,144,128]{2,1,0:T(8,128)S(1)}, u32[]{:S(2)}) copy-start(f32[64,144,128]{2,1,0:T(8,128)S(1)} %get-tuple-element.19.aft_ref) | copy-start | bytes 14155780
  55.0 2.3 %copy-start.28 = (f32[9,128]{1,0:T(8,128)}, f32[9,128]{1,0:T(8,128)S(1)}, u32[]{:S(2)}) copy-start(f32[9,128]{1,0:T(8,128)S(1)} %collective-permute-done.7) | copy-start | bytes 13828
  55.0 12.3 %collective-permute-start.4 = (f32[9,128]{1,0:T(8,128)}, f32[9,128]{1,0:T(8,128)}, u32[]{:S(2)}, u32[]{:S(2)}) collective-permute-start(f32[9,128]{1,0:T(8,128)} %pad_maximum_fusion.3), channel_id=1, source_target_pairs={{0,3},{1,2},{2,1},{3,0},{4,7},{5,6},{6,5},{7,4},{8,11},{9,10},{10,... | collective-permute-start | bytes 13832 | tf_op jit(solution)/shard_map/ppermute | solution.py:252
  56.7 0.7 copy-start.29
  56.7 10.7 %collective-permute-start.2 = (f32[9,128]{1,0:T(8,128)}, f32[9,128]{1,0:T(8,128)}, u32[]{:S(2)}, u32[]{:S(2)}) collective-permute-start(f32[9,128]{1,0:T(8,128)} %pad_maximum_fusion.3), channel_id=1, source_target_pairs={{0,1},{1,0},{2,3},{3,2},{4,5},{5,4},{6,7},{7,6},{8,9},{9,8},{10,11... | collective-permute-start | bytes 13832 | tf_op jit(solution)/shard_map/ppermute | solution.py:252
  58.3 38.3 %all-to-all-start = ((f32[32,8,128]{2,1,0:T(8,128)}), f32[32,8,128]{2,1,0:T(8,128)S(1)}, u32[]{:S(2)}, u32[]{:S(2)}) async-start(f32[32,8,128]{2,1,0:T(8,128)} %reshape.91), calls=%async_computation | async-start | bytes 262144 | tf_op jit(solution)/shard_map/all_to_all | solution.py:328
  69.1 2.3 %copy-start.2 = (f32[64,144,128]{2,1,0:T(8,128)S(1)}, f32[64,144,128]{2,1,0:T(8,128)}, u32[]{:S(2)}) copy-start(f32[64,144,128]{2,1,0:T(8,128)} %copy-done.1) | copy-start | bytes 14155780
  71.4 1.6 copy-start.7
  73.0 1.0 copy-start.12
  74.1 0.8 copy-start.16
  74.8 0.8 copy-start.19
  93.0 1.4 copy-start.8
  94.4 0.8 copy-start.13
  95.2 0.8 copy-start.14
  98.1 15.0 %all-to-all-start.1 = ((f32[32,8,128]{2,1,0:T(8,128)}), f32[32,8,128]{2,1,0:T(8,128)S(1)}, u32[]{:S(2)}, u32[]{:S(2)}) async-start(f32[32,8,128]{2,1,0:T(8,128)} %scan.1), calls=%async_computation.1 | async-start | bytes 262144 | tf_op jit(solution)/shard_map/all_to_all | solution.py:341
  113.1 1.7 copy-start.9
  114.8 1.0 copy-start.11
  115.8 0.8 copy-start.17
  135.5 1.9 %copy-start.4 = (f32[64,128,128]{2,1,0:T(8,128)}, f32[64,128,128]{2,1,0:T(8,128)S(1)}, u32[]{:S(2)}) copy-start(f32[64,128,128]{2,1,0:T(8,128)S(1)} %get-tuple-element.21.ig_ref) | copy-start | bytes 12582916
  137.5 0.8 copy-start.15
  138.3 5.6 %copy-start.27 = (f32[1024]{0:T(1024)S(1)}, f32[1024]{0:T(1024)}, u32[]{:S(2)}) copy-start(f32[1024]{0:T(1024)} %reduce_sum.122) | copy-start | bytes 12292
  145.7 15.9 %all-to-all-start.2 = ((f32[32,1,384]{2,1,0:T(1,128)}), f32[32,1,384]{2,1,0:T(1,128)S(1)}, u32[]{:S(2)}, u32[]{:S(2)}) async-start(f32[32,1,384]{2,1,0:T(1,128)} %bitcast.12), calls=%async_computation.2 | async-start | bytes 98304 | tf_op jit(solution)/shard_map/all_to_all | solution.py:260
  149.8 9.8 %collective-permute-start.14 = (f32[8,128]{1,0:T(8,128)S(1)}, f32[8,128]{1,0:T(8,128)S(1)}, u32[]{:S(2)}, u32[]{:S(2)}) collective-permute-start(f32[8,128]{1,0:T(8,128)S(1)} %bitcast_reduce_fusion), channel_id=1, source_target_pairs={{0,6},{1,7},{2,4},{3,5},{4,2},{5,3},{6,0},{7,1},{8,14},{9,15},{10,... | collective-permute-start | bytes 12296 | tf_op jit(solution)/shard_map/ppermute | solution.py:252
  153.4 7.7 %collective-permute-start.15 = (f32[8,128]{1,0:T(8,128)S(1)}, f32[8,128]{1,0:T(8,128)S(1)}, u32[]{:S(2)}, u32[]{:S(2)}) collective-permute-start(f32[8,128]{1,0:T(8,128)S(1)} %bitcast_reduce_fusion), channel_id=1, source_target_pairs={{0,7},{1,6},{2,5},{3,4},{4,3},{5,2},{6,1},{7,0},{8,15},{9,14},{10,... | collective-permute-start | bytes 12296 | tf_op jit(solution)/shard_map/ppermute | solution.py:252
  153.4 18.1 %collective-permute-start.12 = (f32[8,128]{1,0:T(8,128)S(1)}, f32[8,128]{1,0:T(8,128)S(1)}, u32[]{:S(2)}, u32[]{:S(2)}) collective-permute-start(f32[8,128]{1,0:T(8,128)S(1)} %bitcast_reduce_fusion), channel_id=1, source_target_pairs={{0,4},{1,5},{2,6},{3,7},{4,0},{5,1},{6,2},{7,3},{8,12},{9,13},{10,... | collective-permute-start | bytes 12296 | tf_op jit(solution)/shard_map/ppermute | solution.py:252
  157.4 14.1 %collective-permute-start.13 = (f32[8,128]{1,0:T(8,128)S(1)}, f32[8,128]{1,0:T(8,128)S(1)}, u32[]{:S(2)}, u32[]{:S(2)}) collective-permute-start(f32[8,128]{1,0:T(8,128)S(1)} %bitcast_reduce_fusion), channel_id=1, source_target_pairs={{0,5},{1,4},{2,7},{3,6},{4,1},{5,0},{6,3},{7,2},{8,13},{9,12},{10,... | collective-permute-start | bytes 12296 | tf_op jit(solution)/shard_map/ppermute | solution.py:252
  158.9 12.6 %collective-permute-start.10 = (f32[8,128]{1,0:T(8,128)S(1)}, f32[8,128]{1,0:T(8,128)S(1)}, u32[]{:S(2)}, u32[]{:S(2)}) collective-permute-start(f32[8,128]{1,0:T(8,128)S(1)} %bitcast_reduce_fusion), channel_id=1, source_target_pairs={{0,2},{1,3},{2,0},{3,1},{4,6},{5,7},{6,4},{7,5},{8,10},{9,11},{10,... | collective-permute-start | bytes 12296 | tf_op jit(solution)/shard_map/ppermute | solution.py:252
  159.6 12.0 %collective-permute-start.11 = (f32[8,128]{1,0:T(8,128)S(1)}, f32[8,128]{1,0:T(8,128)S(1)}, u32[]{:S(2)}, u32[]{:S(2)}) collective-permute-start(f32[8,128]{1,0:T(8,128)S(1)} %bitcast_reduce_fusion), channel_id=1, source_target_pairs={{0,3},{1,2},{2,1},{3,0},{4,7},{5,6},{6,5},{7,4},{8,11},{9,10},{10,... | collective-permute-start | bytes 12296 | tf_op jit(solution)/shard_map/ppermute | solution.py:252
  161.2 10.4 %collective-permute-start.9 = (f32[8,128]{1,0:T(8,128)S(1)}, f32[8,128]{1,0:T(8,128)S(1)}, u32[]{:S(2)}, u32[]{:S(2)}) collective-permute-start(f32[8,128]{1,0:T(8,128)S(1)} %bitcast_reduce_fusion), channel_id=1, source_target_pairs={{0,1},{1,0},{2,3},{3,2},{4,5},{5,4},{6,7},{7,6},{8,9},{9,8},{10,11... | collective-permute-start | bytes 12296 | tf_op jit(solution)/shard_map/ppermute | solution.py:252
  162.3 16.5 %all-to-all-start.3 = ((f32[32,1,384]{2,1,0:T(1,128)}), f32[32,1,384]{2,1,0:T(1,128)S(1)}, u32[]{:S(2)}, u32[]{:S(2)}) async-start(f32[32,1,384]{2,1,0:T(1,128)} %broadcast_in_dim.8), calls=%async_computation.3 | async-start | bytes 98304 | tf_op jit(solution)/shard_map/all_to_all | solution.py:262
  172.2 2.2 %copy-start.5 = (f32[64,128,128]{2,1,0:T(8,128)S(1)}, f32[64,128,128]{2,1,0:T(8,128)}, u32[]{:S(2)}) copy-start(f32[64,128,128]{2,1,0:T(8,128)} %copy-done.4) | copy-start | bytes 12582916
  174.4 6.1 %copy-start.24 = (f32[64,16]{0,1:T(8,128)S(1)}, f32[64,16]{0,1:T(8,128)}, u32[]{:S(2)}) copy-start(f32[64,16]{0,1:T(8,128)} %param.12) | copy-start | bytes 12292
  174.4 6.1 %copy-start.26 = (f32[64,16]{0,1:T(8,128)S(1)}, f32[64,16]{0,1:T(8,128)}, u32[]{:S(2)}) copy-start(f32[64,16]{0,1:T(8,128)} %param.11) | copy-start | bytes 12292
  (2 other events, 1.3 us)
where the time goes:
time: 183 us; the launch traced here: 181 us
  starting transfers between devices  61.9 us (34%)
  Pallas kernels  57.6 us (31%)
  local copies, waits for them, and re-layouts  37.4 us (20%)
  other arithmetic  18.8 us (10%)
  waiting for transfers between devices  4.35 us (2%)
    pallas_call x5, Pallas kernels, call(): pl.pallas_call(kernel, name=name, grid=grid, in_specs=ins, out_specs=outs...  57.6 us
    unnamed x65, local copies, waits for them, and re-layouts  25.4 us
    ppermute x14, starting transfers between devices, ch_sum(): lax.ppermute(x, 'ch', [(i, i ^ k) for i in range(count)])  25.2 us
    all_to_all x1, starting transfers between devices, ctx_sum(): lax.all_to_all(jnp.broadcast_to(mine, parts.shape), 'ctx', 0, 0, tiled=True)  9.24 us
    all_to_all x1, starting transfers between devices, local(): arrived = lax.all_to_all(packed, 'ctx', 0, 0, tiled=True)  9.01 us
    all_to_all x1, starting transfers between devices, local(): lax.all_to_all(scanned, 'ctx', 0, 0, tiled=True).reshape(groups // 4, 16, B)  7.39 us
    ppermute x1, starting transfers between devices, local(): lax.ppermute(cotangent[:, :B], 'ctx', [(i, i - 1) for i in range(1, n_ctx)])  5.14 us
    all_to_all x1, starting transfers between devices, ctx_sum(): parts = lax.all_to_all(x.reshape(count, -1), 'ctx', 0, 0, tiled=True)  4.06 us
  transfers between devices with their start and end apart: 20, of which 2 were waited for; matrix products, arithmetic and copies ran while one was open for 12% of the time, Pallas kernels for 21%

commit v1 on v0

v1 whole, which is shorter than its diff:
```python
import functools

import jax
import jax.numpy as jnp
from jax import lax
from jax.experimental import pallas as pl
from jax.experimental.pallas import tpu as pltpu
from jax.sharding import PartitionSpec as P

eps_norm = 1e-06
B = 128
GB = 8
VMEM = 16 * 1024 * 1024
f32 = jnp.float32
bf16 = jnp.bfloat16

NN = (((1,), (0,)), ((), ()))
NT = (((1,), (1,)), ((), ()))
TN = (((0,), (0,)), ((), ()))


def mm(a, b, dims):
    return lax.dot_general(a, b, dims, preferred_element_type=f32)


def split(x):
    hi = x.astype(bf16)
    lo = (x - hi.astype(f32)).astype(bf16)
    return hi, lo


def iotas(shape):
    return (
        lax.broadcasted_iota(jnp.int32, shape, 0),
        lax.broadcasted_iota(jnp.int32, shape, 1),
    )


def spread(row):
    return jnp.transpose(jnp.broadcast_to(row, (B, B)))


def fine(x):
    hi, mid = split(x)
    low = (x - hi.astype(f32) - mid.astype(f32)).astype(bf16)
    return jnp.concatenate([hi, mid, low], axis=1)


def lane_sums(x):
    return mm(jnp.ones((8, 3 * B), bf16), fine(x), NT)[:1]


def toeplitz(row):
    full = jnp.broadcast_to(row, (B, B))
    return pltpu.roll(full, 0, 1, stride=1, stride_axis=0)


def lag_sums(square):
    total = square[:8]
    for a in range(8, B, 8):
        total = total + pltpu.roll(square[a : a + 8], B - a, 1)
    row = lax.broadcasted_iota(jnp.int32, (8, B), 0)
    for bit in (1, 2, 4):
        total = jnp.where((row & bit) != 0, pltpu.roll(total, B - bit, 1), total)
    return jnp.sum(total, axis=0, keepdims=True)


def prep_kernel(h_ref, ct_ref, tail_ref, head_ref, sq_ref, acc_ref):
    tokens = h_ref.shape[1]

    @pl.when(pl.program_id(0) == 0)
    def _():
        acc_ref[...] = jnp.zeros_like(acc_ref)

    h = h_ref[...].astype(f32)
    acc_ref[...] += jnp.sum(jnp.square(h).reshape(h.shape[0] // 8, 8, tokens), axis=0)
    tail_ref[...] = h_ref[:, tokens - B :]
    head_ref[...] = ct_ref[...]

    @pl.when(pl.program_id(0) == pl.num_programs(0) - 1)
    def _():
        row = jnp.sum(acc_ref[...], axis=0, keepdims=True)
        for b in range(tokens // B):
            sq_ref[pl.ds(b, 1), :] = row[:, B * b : B * b + B]


def edge_kernel(nb, h_ref, sq_ref, out_ref):
    h = h_ref[...].astype(f32)
    part = jnp.sum(jnp.square(h).reshape(h.shape[0] // 8, 8, B), axis=0)
    edge = jnp.sum(part, axis=0, keepdims=True)
    rows = jnp.concatenate([edge, sq_ref[...], jnp.zeros((7, B), f32)], axis=0)
    for i in range(out_ref.shape[0]):
        out_ref[i] = rows


def inverse_rows(sq_ref, width):
    total = sq_ref[0]
    for i in range(1, sq_ref.shape[0]):
        total = total + sq_ref[i]
    return lax.rsqrt(total / width + eps_norm)


def grads_kernel(
    nb, ct_ref, ctn_ref, rate_ref, res_ref, four_ref, skip_ref, gml_ref, aft_ref, pack_ref
):
    step = pl.program_id(0)
    row, lane = iotas((B, B))
    upper = lane <= row
    back = ((B - lane) % B).astype(f32)
    below = row.astype(f32)
    slot = lane % 64
    first_half = lane < 64
    step_lane = lax.broadcasted_iota(jnp.int32, (16, B), 1)
    step_slot = step_lane % 64
    third = (step_slot >= 32) & (step_slot < 48)
    zeros = jnp.zeros((16, B), f32)
    none = jnp.zeros((16, B), bf16)
    rates = spread(rate_ref[pl.ds(step, 1), :])
    amps = spread(res_ref[pl.ds(step, 1), :]) * jnp.sqrt(2.0 * rates)
    reach = amps * jnp.exp(-rates * (float(B) - lane.astype(f32)))
    lags = amps * jnp.exp(-rates * back)
    skips = spread(skip_ref[pl.ds(step, 1), :])

    def near_part(g, fall):
        rows = pl.ds(16 * g, 16)
        sub = slice(16 * g, 16 * g + 16)
        blocks = [ct_ref[rows, pl.ds(B * b, B)] for b in range(nb)] + [ctn_ref[rows, :]]
        lhs = jnp.concatenate(blocks, axis=0)
        kernel_row = jnp.sum(lags[sub], axis=0, keepdims=True)
        toe = jnp.where(upper, toeplitz(kernel_row), 0.0)
        mine = jnp.where(first_half if g % 2 == 0 else ~first_half, fall, 0.0)
        hi, lo = split(jnp.concatenate([toe, mine], axis=1))
        out = mm(jnp.concatenate([lhs, lhs], axis=1), jnp.concatenate([hi, lo], axis=0), NN)
        direct = jnp.concatenate([skips[sub]] * (nb + 1), axis=0) * lhs.astype(f32)
        gml_ref[g] = out[:, :B] + direct
        return out[:, B:]

    def first_stage(p):
        pair_rates = four_ref[pl.ds(4 * step + p, 1), :]
        fall = jnp.exp(-pair_rates * below)
        fall = jnp.where((slot >= 16) & (slot < 32), fall * below, fall)
        return near_part(2 * p, fall) + near_part(2 * p + 1, fall), pair_rates

    def second_stage(p, states, pair_rates):
        decay = jnp.broadcast_to(jnp.exp(-pair_rates * float(B)), (16, B))
        after = zeros
        found = [after]
        for b in range(nb, 0, -1):
            state = states[16 * b : 16 * b + 16]
            state = jnp.where(third, state * float(B * b), state)
            after = state + decay * after
            found.append(after)
        after_all = jnp.concatenate(found[::-1], axis=0)
        aft_ref[p] = after_all
        one = after + pltpu.roll(after, B - 16, 1) - float(B) * pltpu.roll(after, 16, 1)
        tile = jnp.where(step_slot < 16, after, jnp.where(step_slot < 32, one, 0.0))
        tile = tile + pltpu.roll(tile, B - 32, 1)
        tile = jnp.where(step_lane < 64, tile, 0.0)
        a_hi, a_lo = split(after_all)
        halves = []
        for h in range(2):
            g = 2 * p + h
            g_hi, g_lo = split(reach[16 * g : 16 * g + 16])
            upper_rows = [g_hi, none, none, g_lo]
            lower_rows = [g_hi, none, none, none]
            gap = [none] * 4
            if h == 0:
                parts = upper_rows + gap + lower_rows + gap
            else:
                parts = gap + upper_rows + gap + lower_rows
            halves.append(jnp.concatenate(parts, axis=0))
        far = mm(
            jnp.concatenate([a_hi, a_lo], axis=1), jnp.concatenate(halves, axis=1), NN
        )
        gml_ref[2 * p] += far[:, :B]
        gml_ref[2 * p + 1] += far[:, B:]
        return tile

    held = first_stage(0)
    tiles = []
    for p in range(GB // 2):
        ahead = first_stage(p + 1) if p + 1 < GB // 2 else None
        tiles.append(second_stage(p, *held))
        held = ahead
    for k in range(GB // 4):
        pack_ref[k] = tiles[2 * k] + pltpu.roll(tiles[2 * k + 1], 64, 1)


def squeeze(tile):
    lane = lax.broadcasted_iota(jnp.int32, tile.shape, 1)
    tile = jnp.where(lane % 64 < 32, tile, 0.0)
    return jnp.where(lane < 64, tile + pltpu.roll(tile, B - 32, 1), 0.0)


def moments_kernel(
    nb, width, offset, h_ref, hp_ref, sq_ref, gain_ref, ct_ref, w_ref, rate_ref, four_ref,
    aft_ref, *refs,
):
    x_ref, part_ref, end_ref, w_scratch = refs[-4:]
    step = pl.program_id(0) + offset

    @pl.when(step == offset)
    def _():
        w_scratch[...] = w_ref[...].astype(f32)

    row, lane = iotas((B, B))
    upper = lane >= row
    ahead = lane.astype(f32)
    togo = float(B) - row.astype(f32)
    slot = lane % 64
    first_half = lane < 64
    step_slot = lax.broadcasted_iota(jnp.int32, (16, B), 1) % 64
    low = step_slot < 16
    half = step_slot < 32
    second = half & (step_slot >= 16)
    zeros = jnp.zeros((16, B), f32)
    inverse = inverse_rows(sq_ref, width)
    gains = spread(gain_ref[pl.ds(step, 1), :])

    def mix(g):
        rows = pl.ds(16 * g, 16)
        sub = slice(16 * g, 16 * g + 16)
        units = []
        for b in range(nb + 1):
            h = hp_ref[rows, :] if b == 0 else h_ref[rows, pl.ds(B * (b - 1), B)]
            units.append((h.astype(f32) * inverse[b : b + 1] * gains[sub]).astype(bf16))
        x_all = jnp.concatenate(units, axis=0)
        x_ref[g] = x_all
        lhs = jnp.concatenate([x_all[: 16 * nb], x_all[16:]], axis=1)
        taps = toeplitz(w_scratch[pl.ds(GB * step + g, 1), :])
        cur = jnp.where(upper, taps, 0.0).astype(bf16)
        prev = jnp.where(upper, 0.0, taps).astype(bf16)
        return mm(lhs, jnp.concatenate([prev, cur], axis=0), NN).astype(bf16)

    def first_stage(p):
        pair_rates = four_ref[pl.ds(4 * step + p, 1), :]
        rise = jnp.exp(-pair_rates * togo)
        rise = jnp.where(slot >= 48, rise * togo, rise)
        hi, lo = split(
            jnp.concatenate(
                [jnp.where(first_half, rise, 0.0), jnp.where(first_half, 0.0, rise)], axis=0
            )
        )
        mixes = [mix(2 * p), mix(2 * p + 1)]
        lifted = mm(
            jnp.concatenate(mixes, axis=1), jnp.concatenate([hi, lo], axis=1), NN
        )
        return mixes, lifted[:, :B] + lifted[:, B:], pair_rates

    skip_parts = []
    corrs = []

    def second_stage(p, mixes, lifted, pair_rates):
        for h in range(2):
            rows = pl.ds(16 * (2 * p + h), 16)
            mixed = mixes[h]
            ct = jnp.concatenate([ct_ref[rows, pl.ds(B * b, B)] for b in range(nb)], axis=0)
            pairs = mm(mixed, ct, TN)
            direct = ct.astype(f32) * mixed.astype(f32)
            total = direct[:16]
            for b in range(1, nb):
                total = total + direct[16 * b : 16 * b + 16]
            skip_parts.append(total)
            corrs.append(lag_sums(jnp.where(upper, pairs, 0.0)))
        after = aft_ref[p]
        decay = jnp.broadcast_to(jnp.exp(-pair_rates * float(B)), (16, B))
        plain = zeros
        scaled = zeros
        end = zeros
        for b in range(nb):
            lift = lifted[16 * b : 16 * b + 16]
            prod = lift * after[16 * b : 16 * b + 16]
            plain = plain + prod
            scaled = scaled + prod * float(B * (b + 1))
            end = decay * (end + jnp.where(second, lift * float(B * (nb - b)), lift))
        plain = plain[:8] + plain[8:]
        scaled = scaled[:8] + scaled[8:]
        after_one = (
            plain + pltpu.roll(plain, B - 16, 1) + pltpu.roll(plain, B - 32, 1)
            - pltpu.roll(scaled, 16, 1)
        )
        found = squeeze(jnp.where(low[:8], plain, after_one))
        ends_zero = squeeze(jnp.where(low, end, pltpu.roll(end, B - 16, 1)))
        ends_one = squeeze(
            jnp.where(low, pltpu.roll(end, B - 16, 1) + pltpu.roll(end, B - 48, 1), 0.0)
        )
        return found, ends_zero, ends_one

    held = first_stage(0)
    tiles = []
    for p in range(GB // 2):
        nxt = first_stage(p + 1) if p + 1 < GB // 2 else None
        tiles.append(second_stage(p, *held))
        held = nxt
    quads = []
    for k in range(GB // 4):
        left, right = tiles[2 * k], tiles[2 * k + 1]
        joined = [a + pltpu.roll(b, 64, 1) for a, b in zip(left, right)]
        quads.append(jnp.sum(joined[0], axis=0, keepdims=True))
        end_ref[k] = jnp.concatenate(joined[1:], axis=0)
    skip_row = lane_sums(jnp.concatenate(skip_parts, axis=0))
    corr = jnp.concatenate(corrs, axis=0)
    fall = jnp.exp(-spread(rate_ref[pl.ds(step, 1), :]) * ahead)
    table = []
    for g in range(GB):
        table += [fall[16 * g : 16 * g + 16], fall[16 * g : 16 * g + 16] * ahead[:16]]
    t_hi, t_lo = split(jnp.concatenate(table, axis=0))
    c_hi, c_lo = split(corr)
    near = mm(
        jnp.concatenate([c_hi, c_lo, c_hi], axis=1),
        jnp.concatenate([t_hi, t_hi, t_lo], axis=1),
        NT,
    )
    n_row, n_lane = iotas((GB, 32 * GB))
    near = jnp.sum(jnp.where(n_lane // 32 == n_row, near, 0.0), axis=0, keepdims=True)
    blank = jnp.zeros((1, B), f32)
    part_ref[...] = jnp.concatenate(
        [blank] * 6 + [skip_row] + [blank] * 3 + [quads[0] + near[:, :B]]
        + [blank] * 3 + [quads[1] + near[:, B:]] + [blank],
        axis=0,
    )


def mirror_matrix():
    row, lane = iotas((B, B))
    return jnp.where((row + lane) % B == 0, 1.0, 0.0).astype(bf16)


def inputs_kernel(
    nb, width, gml_ref, a_ref, rate_ref, res_ref, pair_ref, h_ref, sq_ref, gain_ref, w_ref,
    part_ref, end_ref, ig_ref, row_ref, pay_ref, grad_ref, acc_ref, w_scratch,
):
    step = pl.program_id(0)

    @pl.when(step == 0)
    def _():
        w_scratch[...] = mm(w_ref[...], mirror_matrix(), NN)
        acc_ref[...] = jnp.zeros_like(acc_ref)

    row, lane = iotas((B, B))
    upper = lane <= row
    none = jnp.zeros((16, B), bf16)
    ones = (lax.broadcasted_iota(jnp.int32, (16, B), 1) % 32) >= 16
    inverse = inverse_rows(sq_ref, width)
    gains = spread(gain_ref[pl.ds(step, 1), :])
    rates = spread(rate_ref[pl.ds(step, 1), :])
    amps = spread(res_ref[pl.ds(step, 1), :]) * jnp.sqrt(2.0 * rates)
    reach = amps * jnp.exp(-rates * (float(B) - lane.astype(f32)))
    sums = [acc_ref[pl.ds(8 * b, 8), :] for b in range(nb)]
    gain_parts = []
    quads = []
    lhs_of = {}

    def cross(k):
        decay = jnp.exp(jnp.broadcast_to(pair_ref[k], (16, B)) * (-float(B)))
        after = a_ref[k]
        ends = end_ref[k]
        first = jnp.sum(ends[:16] * after, axis=0, keepdims=True)
        other = jnp.sum(ends[16:] * after, axis=0, keepdims=True)
        quads.append(first + pltpu.roll(jnp.broadcast_to(other, (8, B)), 16, 1)[:1])
        after = jnp.where(ones, pltpu.roll(after, 16, 1), after)
        found = [after]
        for b in range(nb):
            after = after * decay
            found.append(after)
        a_hi, a_lo = split(jnp.concatenate(found[::-1], axis=0))
        return jnp.concatenate([a_hi, a_lo], axis=1)

    def first_stage(p):
        k = p // 2
        if k not in lhs_of:
            lhs_of[k] = cross(k)
        halves = []
        for h in range(2):
            g = 2 * p + h
            q = g % 4
            g_hi, g_lo = split(reach[16 * g : 16 * g + 16])
            pad = [none] * (2 * q)
            end = [none] * (6 - 2 * q)
            halves.append(
                jnp.concatenate(pad + [g_hi, g_lo] + end + pad + [g_hi, none] + end, axis=0)
            )
        far = mm(lhs_of[k], jnp.concatenate(halves, axis=1), NN)
        grads = []
        for h in range(2):
            g = 2 * p + h
            grad = (gml_ref[g] + far[:, B * h : B * h + B]).astype(bf16)
            grad_ref[g] = grad[: 16 * nb]
            grads.append(grad)
        return grads

    def second_stage(p, grads):
        for h in range(2):
            g = 2 * p + h
            rows = pl.ds(16 * g, 16)
            sub = slice(16 * g, 16 * g + 16)
            grad = grads[h]
            taps = toeplitz(w_scratch[pl.ds(GB * step + g, 1), :])
            cur = jnp.where(upper, taps, 0.0).astype(bf16)
            prev = jnp.where(upper, 0.0, taps).astype(bf16)
            lhs = jnp.concatenate([grad[: 16 * nb], grad[16:]], axis=1)
            ig = mm(lhs, jnp.concatenate([cur, prev], axis=0), NN)
            ig_ref[g] = ig
            part = jnp.zeros((16, B), f32)
            for b in range(nb):
                prod = ig[16 * b : 16 * b + 16] * h_ref[rows, pl.ds(B * b, B)].astype(f32)
                part = part + prod * inverse[b + 1 : b + 2]
                prod = prod * gains[sub]
                sums[b] = sums[b] + (prod[:8] + prod[8:])
            gain_parts.append(part)

    held = first_stage(0)
    for p in range(GB // 2):
        nxt = first_stage(p + 1) if p + 1 < GB // 2 else None
        second_stage(p, held)
        held = nxt
    for b in range(nb):
        acc_ref[pl.ds(8 * b, 8), :] = sums[b]
    gain_row = lane_sums(jnp.concatenate(gain_parts, axis=0))
    blank = jnp.zeros((1, B), f32)
    pay_ref[...] = part_ref[...] + jnp.concatenate(
        [blank, blank, gain_row] + [blank] * 7 + [quads[0]] + [blank] * 3 + [quads[1], blank],
        axis=0,
    )

    @pl.when(step == pl.num_programs(0) - 1)
    def _():
        raw = jnp.concatenate(
            [jnp.sum(sums[b], axis=0, keepdims=True) for b in range(nb)], axis=0
        )
        for i in range(row_ref.shape[0]):
            row_ref[i] = raw


def taps_kernel(nb, grad_ref, x_ref, pay_ref, out_ref):
    row, lane = iotas((B, B))
    lower = row >= lane

    def product(g):
        x_all = x_ref[g]
        x_pair = jnp.concatenate([x_all[16:], x_all[: 16 * nb]], axis=1)
        return mm(grad_ref[g], x_pair, TN)

    rows = []
    held = product(0)
    for g in range(GB):
        nxt = product(g + 1) if g + 1 < GB else None
        rows.append(lag_sums(jnp.where(lower, held[:, :B], held[:, B:])))
        held = nxt
    mirror = jnp.concatenate([mirror_matrix()] * 3, axis=0)
    taps = mm(fine(jnp.concatenate(rows, axis=0)), mirror, NN)
    blank = jnp.zeros((2, B), f32)
    out_ref[...] = pay_ref[...] + jnp.concatenate(
        [taps[0:2], blank, taps[2:4], blank, taps[4:6], blank, taps[6:8], blank], axis=0
    )


def final_kernel(nb, width, ig_ref, h_ref, sq_ref, gain_ref, raw_ref, out_ref, rms_ref):
    step = pl.program_id(0)
    inverse = inverse_rows(sq_ref, width)
    gains = spread(gain_ref[pl.ds(step, 1), :])
    raw = raw_ref[0]
    for i in range(1, raw_ref.shape[0]):
        raw = raw + raw_ref[i]
    rms_ref[...] = raw * width ** (-0.5)
    inv = [inverse[b + 1 : b + 2] for b in range(nb)]
    pull = [raw[b : b + 1] * inv[b] * inv[b] * (1.0 / width) for b in range(nb)]
    for g in range(GB):
        rows = pl.ds(16 * g, 16)
        gain = gains[16 * g : 16 * g + 16]
        for b in range(nb):
            cols = pl.ds(B * b, B)
            h = h_ref[rows, cols].astype(f32)
            ig = ig_ref[g, pl.ds(16 * b, 16), :]
            out_ref[rows, cols] = (inv[b] * (ig * gain - h * pull[b])).astype(bf16)


def scan_kernel(count, span, s_ref, r_ref, out_ref):
    lane = lax.broadcasted_iota(jnp.int32, (8, B), 1)
    ones = (lane % 32) >= 16
    rates = r_ref[pl.ds(lax.axis_index("ctx") // 2, 1), :]
    decay = jnp.exp(jnp.broadcast_to(rates, (8, B)) * (-float(span)))
    x = jnp.zeros((8, B), f32)
    found = [None] * count
    found[count - 1] = x
    for i in range(count - 2, -1, -1):
        x = s_ref[i + 1] + decay * x
        found[i] = x
    v = jnp.zeros((8, B), f32)
    out_ref[count - 1] = v
    for i in range(count - 2, -1, -1):
        v = decay * (v + float(span) * pltpu.roll(found[i + 1], 16, 1))
        out_ref[i] = found[i] + jnp.where(ones, v, 0.0)


def sum_kernel(in_ref, out_ref):
    total = in_ref[0]
    for i in range(1, in_ref.shape[0]):
        total = total + in_ref[i]
    for i in range(out_ref.shape[0]):
        out_ref[i] = total


def outs_kernel(scale, in_ref, tap_ref, gain_ref, skip_ref, mom_ref):
    owners = tap_ref.shape[0] // 2
    steps = gain_ref.shape[0]
    for r in range(2):
        tap_ref[pl.ds(r, owners, stride=2), :] = in_ref[pl.ds(r, owners, stride=4), :] * scale
    gain_ref[...] = in_ref[pl.ds(2, steps, stride=16), :] * scale
    skip_ref[...] = in_ref[pl.ds(6, steps, stride=16), :] * scale
    for r in range(2):
        mom_ref[pl.ds(r, steps, stride=2), :] = (
            in_ref[pl.ds(10 + 4 * r, steps, stride=16), :] * scale
        )


def call(kernel, name, grid, ins, outs, args, flops=0, moved=0, scratch=(), aliases={}):
    return pl.pallas_call(
        kernel,
        name=name,
        grid=grid,
        in_specs=ins,
        out_specs=outs[0],
        out_shape=outs[1],
        scratch_shapes=scratch,
        input_output_aliases=aliases,
        compiler_params=pltpu.CompilerParams(vmem_limit_bytes=VMEM),
        cost_estimate=pl.CostEstimate(flops=flops, bytes_accessed=moved, transcendentals=0),
    )(*args)


def exchange(x, axis):
    return lax.all_to_all(x, axis, 0, 0, tiled=True)


def local(hidden, cotangent, norm_gain, mr_filter, residue, decay_rate, skip_weight):
    channels, tokens = hidden.shape
    groups, taps = mr_filter.shape
    modes = residue.shape[1]
    n_ctx = lax.axis_size("ctx")
    n_ch = lax.axis_size("ch")
    width = channels * n_ch
    scale = (tokens * n_ctx) ** (-0.5)
    nb = tokens // B
    steps = groups // GB
    grid = (steps,)
    shape = jax.ShapeDtypeStruct
    hidden, cotangent, mr_filter = (
        pltpu.with_memory_space_constraint(x, pltpu.HBM) for x in (hidden, cotangent, mr_filter)
    )

    wide = pl.BlockSpec((16 * GB, tokens), lambda i: (i, 0))
    thin = pl.BlockSpec((16 * GB, B), lambda i: (i, 0))
    tall = pl.BlockSpec((GB, 16 * (nb + 1), B), lambda i: (i, 0, 0))
    pair_tall = pl.BlockSpec((GB // 2, 16 * (nb + 1), B), lambda i: (i, 0, 0))
    body = pl.BlockSpec((GB, 16 * nb, B), lambda i: (i, 0, 0))
    quad = pl.BlockSpec((GB // 4, 16, B), lambda i: (i, 0, 0))
    quad_two = pl.BlockSpec((GB // 4, 32, B), lambda i: (i, 0, 0))
    quad_row = pl.BlockSpec((GB // 4, 1, B), lambda i: (i, 0, 0))
    pay = pl.BlockSpec((16, B), lambda i: (i, 0))

    def full(*dims):
        return pl.BlockSpec(dims, lambda *i: (0,) * len(dims))

    tail, head, own_sq = call(
        prep_kernel,
        "prep",
        grid,
        [wide, thin],
        (
            [thin, thin, full(nb, B)],
            [shape((channels, B), bf16), shape((channels, B), bf16), shape((nb, B), f32)],
        ),
        (hidden, cotangent),
        moved=3 * 2**20,
        scratch=[pltpu.VMEM((8, tokens), f32)],
    )
    ct_next = lax.ppermute(head, "ctx", [(i, i - 1) for i in range(1, n_ctx)])
    h_prev = lax.ppermute(tail, "ctx", [(i, i + 1) for i in range(n_ctx - 1)])
    edge = call(
        functools.partial(edge_kernel, nb),
        "edge",
        (),
        [full(channels, B), full(nb, B)],
        (full(n_ch, 16, B), shape((n_ch, 16, B), f32)),
        (h_prev, own_sq),
        moved=2**18,
    )
    edge, ct_next = lax.optimization_barrier((edge, ct_next))
    squares = exchange(edge, "ch")

    rate_flat = decay_rate.reshape(steps, B)
    res_flat = residue.reshape(steps, B)
    rate_four = jnp.tile(decay_rate, (1, 4)).reshape(groups // 2, B)
    rate_pair = jnp.concatenate([decay_rate, decay_rate], axis=1).reshape(groups // 4, B)
    gain_flat = norm_gain.reshape(steps, B)
    skip_flat = skip_weight.reshape(steps, B)
    flat = full(steps, B)

    grad_local, after_local, packed = call(
        functools.partial(grads_kernel, nb),
        "grads",
        grid,
        [wide, thin, flat, flat, full(groups // 2, B), flat],
        (
            [tall, pair_tall, quad],
            [
                shape((groups, 16 * (nb + 1), B), f32),
                shape((groups // 2, 16 * (nb + 1), B), f32),
                shape((groups // 4, 16, B), f32),
            ],
        ),
        (cotangent, ct_next, rate_flat, res_flat, rate_four, skip_flat),
        flops=groups * 2 * 144 * 256 * 384,
        moved=14 * 2**20,
    )

    def moments(offset, before, x_next):
        def at(spec):
            return pl.BlockSpec(
                spec.block_shape, lambda i: (i + offset,) + spec.index_map(i)[1:]
            )

        held = [pl.BlockSpec(memory_space=pl.ANY)] * len(before)
        return call(
            functools.partial(moments_kernel, nb, width, offset),
            "moments",
            (steps // 2,),
            [
                at(wide), at(thin), full(n_ch, 16, B), flat, at(wide), full(groups, B), flat,
                full(groups // 2, B), at(pair_tall),
            ]
            + held,
            (
                [at(tall), at(pay), at(quad_two)],
                [
                    shape((groups, 16 * (nb + 1), B), bf16),
                    shape((16 * steps, B), f32),
                    shape((groups // 4, 32, B), f32),
                ],
            ),
            (
                hidden, x_next, squares, gain_flat, cotangent, mr_filter, rate_flat, rate_four,
                after_local, *before,
            ),
            flops=groups * 128 * 256 * 384,
            moved=7 * 2**20,
            scratch=[pltpu.VMEM((groups, B), f32)],
            aliases={9 + i: i for i in range(len(before))},
        )

    arrived = exchange(packed.reshape(n_ctx, 8, B), "ctx")
    early = moments(0, (), h_prev)
    arrived, early = lax.optimization_barrier((arrived, tuple(early)))
    scanned = call(
        functools.partial(scan_kernel, n_ctx, tokens),
        "scan",
        (),
        [full(n_ctx, 8, B), full(groups // 4, B)],
        (full(n_ctx, 8, B), shape((n_ctx, 8, B), f32)),
        (arrived, rate_pair),
        moved=2**18,
    )
    scanned, edge_rows = lax.optimization_barrier((scanned, h_prev))
    after = exchange(scanned, "ctx").reshape(groups // 4, 16, B)
    units, part, ends = moments(steps // 2, early, edge_rows)

    ig, row_part, mostly, grad_mixed = call(
        functools.partial(inputs_kernel, nb, width),
        "inputs",
        grid,
        [
            tall, quad, flat, flat, quad_row, wide, full(n_ch, 16, B), flat, full(groups, B),
            pay, quad_two,
        ],
        (
            [body, full(n_ch, nb, B), pay, body],
            [
                shape((groups, 16 * nb, B), f32),
                shape((n_ch, nb, B), f32),
                shape((16 * steps, B), f32),
                shape((groups, 16 * nb, B), bf16),
            ],
        ),
        (
            grad_local, after, rate_flat, res_flat, rate_pair.reshape(groups // 4, 1, B), hidden,
            squares, gain_flat, mr_filter, part, ends,
        ),
        flops=groups * 2 * 144 * 256 * 512,
        moved=14 * 2**20,
        scratch=[pltpu.VMEM((8 * nb, B), f32), pltpu.VMEM((groups, B), f32)],
    )

    raw = exchange(row_part, "ch")
    payload = call(
        functools.partial(taps_kernel, nb),
        "taps",
        grid,
        [body, tall, pay],
        (pay, shape((16 * steps, B), f32)),
        (grad_mixed, units, mostly),
        flops=groups * 2 * 128 * 128 * 256,
        moved=5 * 2**20,
    )
    raw, payload = lax.optimization_barrier((raw, payload))
    landed = exchange(payload.reshape(n_ctx, 4, B), "ctx")
    grad_hidden, grad_inv_rms = call(
        functools.partial(final_kernel, nb, width),
        "final",
        grid,
        [body, wide, full(n_ch, 16, B), flat, full(n_ch, nb, B)],
        (
            [wide, full(nb, B)],
            [shape((channels, tokens), bf16), shape((nb, B), f32)],
        ),
        (ig, hidden, squares, gain_flat, raw),
        moved=8 * 2**20,
    )
    landed, grad_inv_rms = lax.optimization_barrier((landed, grad_inv_rms))
    chunk = full(n_ctx, 4, B)
    summed = call(
        sum_kernel, "sum", (), [chunk], (chunk, shape((n_ctx, 4, B), f32)), (landed,),
        moved=2**17,
    )
    total = exchange(summed, "ctx").reshape(4 * n_ctx, B)
    grad_mr, grad_gain, grad_skip, both = call(
        functools.partial(outs_kernel, scale),
        "outs",
        (),
        [full(4 * n_ctx, B)],
        (
            [full(groups, taps), full(steps, B), full(steps, B), full(groups // 4, B)],
            [
                shape((groups, taps), f32),
                shape((steps, B), f32),
                shape((steps, B), f32),
                shape((groups // 4, B), f32),
            ],
        ),
        (total,),
        moved=2**17,
    )
    both = both.reshape(groups, 2 * modes)
    first, second = both[:, :modes], both[:, modes:]
    root_rate = jnp.sqrt(2.0 * decay_rate)
    return (
        grad_hidden,
        grad_gain.reshape(channels),
        grad_mr,
        root_rate * first,
        residue * root_rate * (0.5 * first - decay_rate * second),
        grad_skip.reshape(channels),
        grad_inv_rms.reshape(tokens),
    )


def solution(mesh):
    return jax.shard_map(
        local,
        mesh=mesh,
        in_specs=(
            P("ch", "ctx"),
            P("ch", "ctx"),
            P("ch"),
            P("ch", None),
            P("ch", None),
            P("ch", None),
            P("ch"),
        ),
        out_specs=(
            P("ch", "ctx"),
            P("ch"),
            P("ch", None),
            P("ch", None),
            P("ch", None),
            P("ch"),
            P("ctx"),
        ),
        check_vma=False,
    )
```

time: 183 us -> 134 us (0.73)
  local copies, waits for them, and re-layouts: 37.4 us -> 17.3 us
  other arithmetic: 18.8 us -> 0.65 us
  starting transfers between devices: 61.9 us -> 45.1 us
  blocking collectives: 0 us -> 14.5 us
  Pallas kernels: 57.6 us -> 50.1 us
    ppermute x16 -> x2, starting transfers between devices: 32.2 us -> 6.45 us  [the longest x1 4.51 us: local(): h_prev = lax.ppermute(tail, 'ctx', [(i, i + 1) for i in range(n_ctx - 1)])]
    all_to_all x0 -> x1, blocking collectives: none -> 14.5 us  [exchange(): return lax.all_to_all(x, axis, 0, 0, tiled=True)]
    reduce_sum x10 -> x0, other arithmetic: 10.1 us -> none  [the longest x1 2.66 us: local(): own_sq = jnp.sum(jnp.square(hidden.astype(f32)), axis=0).reshape(nb, B)]
    all_to_all x4 -> x5, starting transfers between devices: 29.7 us -> 38.6 us  [exchange(): return lax.all_to_all(x, axis, 0, 0, tiled=True)]
    unnamed x65 -> x30, local copies, waits for them, and re-layouts: 25.4 us -> 16.6 us
    pallas_call x5 -> x11, Pallas kernels: 57.6 us -> 50.1 us  [call(): pl.pallas_call(kernel, name=name, grid=grid, in_specs=ins, out_specs=outs...]
    ppermute x16 -> x2, waiting for transfers between devices: 0.04 us -> 4.48 us  [the longest x1 3.63 us: local(): ct_next = lax.ppermute(head, 'ctx', [(i, i - 1) for i in range(1, n_ctx)])]
    all_to_all x4 -> x5, waiting for transfers between devices: 4.3 us -> 0.01 us  [exchange(): return lax.all_to_all(x, axis, 0, 0, tiled=True)]
  transfers between devices with their start and end apart: 20 -> 7, of which waited for: 2 -> 2; matrix products, arithmetic and copies ran while one was open for 12% -> 1% of each run, Pallas kernels for 21% -> 27%
where the time goes in v1:
time: 134 us; the launch traced here: 133 us
  Pallas kernels  50.1 us (37%)
  starting transfers between devices  45.1 us (34%)
  local copies, waits for them, and re-layouts  17.3 us (13%)
  blocking collectives  14.5 us (11%)
  waiting for transfers between devices  4.49 us (3%)
    pallas_call x11, Pallas kernels, call(): pl.pallas_call(kernel, name=name, grid=grid, in_specs=ins, out_specs=outs...  50.1 us
    all_to_all x5, starting transfers between devices, exchange(): return lax.all_to_all(x, axis, 0, 0, tiled=True)  38.6 us
    unnamed x30, local copies, waits for them, and re-layouts  16.6 us
    all_to_all x1, blocking collectives, exchange(): return lax.all_to_all(x, axis, 0, 0, tiled=True)  14.5 us
    ppermute x1, starting transfers between devices, local(): h_prev = lax.ppermute(tail, 'ctx', [(i, i + 1) for i in range(n_ctx - 1)])  4.51 us
    ppermute x1, waiting for transfers between devices, local(): ct_next = lax.ppermute(head, 'ctx', [(i, i - 1) for i in range(1, n_ctx)])  3.63 us
  transfers between devices with their start and end apart: 7, of which 2 were waited for; matrix products, arithmetic and copies ran while one was open for 1% of the time, Pallas kernels for 27%

profile of v1, /device:TPU:1, one launch (start us, length us, event | category | flops | bytes accessed | tf_op | source)
XLA Modules:
  0.0 133.0 jit_solution(851230038580434295)
XLA Ops:
  0.7 4.1 %prep.1 = (bf16[1024,128]{1,0:T(8,128)(2,1)S(1)}, bf16[1024,128]{1,0:T(8,128)(2,1)S(1)}, f32[8,128]{1,0:T(8,128)S(1)}) custom-call(bf16[1024,1024]{1,0:T(8,128)(2,1)} %h_ref.9, bf16[1024,1024]{1,0:T(8,128)(2,1)} %ct_ref.7), custom_call_target="tpu_custom_call" | custom-call | bytes 3145728 | tf_op jit(solution)/shard_map/prep/pallas_call | solution.py:518
  4.8 4.5 %collective-permute-start = (bf16[1024,128]{1,0:T(8,128)(2,1)S(1)}, bf16[1024,128]{1,0:T(8,128)(2,1)S(1)}, u32[]{:S(2)}, u32[]{:S(2)}) collective-permute-start(bf16[1024,128]{1,0:T(8,128)(2,1)S(1)} %get-tuple-element.41), channel_id=1, source_target_pairs={{0,8},{8,16},{16,24},{24,32},{32,40},{40,48},{48,56},{56,64},{64,7... | collective-permute-start | bytes 786440 | tf_op jit(solution)/shard_map/ppermute | solution.py:579
  9.3 1.9 %collective-permute-start.1 = (bf16[1024,128]{1,0:T(8,128)(2,1)S(1)}, bf16[1024,128]{1,0:T(8,128)(2,1)S(1)}, u32[]{:S(2)}, u32[]{:S(2)}) collective-permute-start(bf16[1024,128]{1,0:T(8,128)(2,1)S(1)} %get-tuple-element.43), channel_id=1, source_target_pairs={{8,0},{16,8},{24,16},{32,24},{40,32},{48,40},{56,48},{64,56},{72,6... | collective-permute-start | bytes 786440 | tf_op jit(solution)/shard_map/ppermute | solution.py:578
  11.3 0.1 copy.35
  11.4 0.1 reshape.57.rate_ref
  11.4 0.1 copy.36
  11.5 0.1 reshape.58.res_ref
  11.6 0.1 tile.9.four_ref
  11.8 0.8 collective-permute-done.h_ref.hp_ref
  12.6 0.8 edge.1
  13.4 3.6 %collective-permute-done.1.ctn_ref = bf16[1024,128]{1,0:T(8,128)(2,1)S(1)} collective-permute-done((bf16[1024,128]{1,0:T(8,128)(2,1)S(1)}, bf16[1024,128]{1,0:T(8,128)(2,1)S(1)}, u32[]{:S(2)}, u32[]{:S(2)}) %collective-permute-start.1) | collective-permute-done | bytes 262176 | tf_op jit(solution)/shard_map/ppermute | solution.py:578
  17.0 8.2 %all-to-all-start.1 = ((f32[8,16,128]{2,1,0:T(8,128)}), f32[8,16,128]{2,1,0:T(8,128)S(1)}, u32[]{:S(2)}, u32[]{:S(2)}) async-start(f32[8,16,128]{2,1,0:T(8,128)} %edge.1), calls=%async_computation.1 | async-start | bytes 131072 | tf_op jit(solution)/shard_map/all_to_all | solution.py:533
  25.2 0.0 copy-start.7
  25.2 9.1 %grads.1 = (f32[64,144,128]{2,1,0:T(8,128)S(1)}, f32[32,144,128]{2,1,0:T(8,128)S(1)}, f32[16,16,128]{2,1,0:T(8,128)}) custom-call(bf16[1024,1024]{1,0:T(8,128)(2,1)} %ct_ref.7, bf16[1024,128]{1,0:T(8,128)(2,1)S(1)} %collective-permute-done.1.ctn_ref, f32[8,128]{1,0:T(8,128)S(1)} %reshape.57.rate_ref, f32[8,128]{1,0:T(8,128)S(1)} %reshape.58.res_ref, ...), custom_call_target="tpu_custom_call" | custom-call | flops 1811939328 | bytes 14680064 | tf_op jit(solution)/shard_map/grads/pallas_call | solution.py:518
  34.3 1.5 %copy-done = f32[32,144,128]{2,1,0:T(8,128)} copy-done((f32[32,144,128]{2,1,0:T(8,128)}, f32[32,144,128]{2,1,0:T(8,128)S(1)}, u32[]{:S(2)}) %copy-start) | copy-done | bytes 2359320
  35.8 2.1 %copy-done.9 = f32[64,144,128]{2,1,0:T(8,128)} copy-done((f32[64,144,128]{2,1,0:T(8,128)}, f32[64,144,128]{2,1,0:T(8,128)S(1)}, u32[]{:S(2)}) %copy-start.9) | copy-done | bytes 4718616
  37.9 0.0 all-to-all-done.1.sq_ref
  37.9 8.7 %all-to-all-start = ((f32[32,8,128]{2,1,0:T(8,128)}), f32[32,8,128]{2,1,0:T(8,128)S(1)}, u32[]{:S(2)}, u32[]{:S(2)}) async-start(f32[32,8,128]{2,1,0:T(8,128)} %bitcast.1), calls=%async_computation | async-start | bytes 262144 | tf_op jit(solution)/shard_map/all_to_all | solution.py:533
  46.7 0.1 copy.38
  46.8 0.1 reshape.62.r_ref
  46.8 1.7 %copy-done.1 = f32[32,144,128]{2,1,0:T(8,128)S(1)} copy-done((f32[32,144,128]{2,1,0:T(8,128)S(1)}, f32[32,144,128]{2,1,0:T(8,128)}, u32[]{:S(2)}) %copy-start.1) | copy-done | bytes 2359320
  48.5 6.8 %moments.2 = (bf16[64,144,128]{2,1,0:T(8,128)(2,1)S(1)}, f32[128,128]{1,0:T(8,128)S(1)}, f32[16,32,128]{2,1,0:T(8,128)S(1)}) custom-call(bf16[1024,1024]{1,0:T(8,128)(2,1)} %h_ref.9, bf16[1024,128]{1,0:T(8,128)(2,1)S(1)} %collective-permute-done.h_ref.hp_ref, f32[8,16,128]{2,1,0:T(8,128)S(1)} %all-to-all-done.1.sq_ref, f32[8,128]{1,0:T(8,128)S(1)} %bitcast.12, ...), custom_call_target="tpu_custom_call" | custom-call | flops 805306368 | bytes 7340032 | tf_op jit(solution)/shard_map/moments/pallas_call | solution.py:518
  55.3 0.0 all-to-all-done.s_ref
  55.3 0.8 scan.1
  56.1 7.4 %all-to-all-start.2 = ((f32[32,8,128]{2,1,0:T(8,128)}), f32[32,8,128]{2,1,0:T(8,128)S(1)}, u32[]{:S(2)}, u32[]{:S(2)}) async-start(f32[32,8,128]{2,1,0:T(8,128)} %scan.1), calls=%async_computation.2 | async-start | bytes 262144 | tf_op jit(solution)/shard_map/all_to_all | solution.py:533
  63.5 0.1 reshape_reshape.3
  63.6 1.7 %copy-done.2 = f32[32,144,128]{2,1,0:T(8,128)S(1)} copy-done((f32[32,144,128]{2,1,0:T(8,128)S(1)}, f32[32,144,128]{2,1,0:T(8,128)}, u32[]{:S(2)}) %copy-start.2) | copy-done | bytes 2359320
  65.3 6.8 %moments.3 = (bf16[64,144,128]{2,1,0:T(8,128)(2,1)S(1)}, f32[128,128]{1,0:T(8,128)S(1)}, f32[16,32,128]{2,1,0:T(8,128)S(1)}) custom-call(bf16[1024,1024]{1,0:T(8,128)(2,1)} %h_ref.9, bf16[1024,128]{1,0:T(8,128)(2,1)S(1)} %collective-permute-done.h_ref.hp_ref, ...), custom_call_target="tpu_custom_call", output_to_operand_aliasing={{0}: (9, {}), {1}: (10, {}), {2}: (11, {})} | custom-call | flops 805306368 | bytes 7340032 | tf_op jit(solution)/shard_map/moments/pallas_call | solution.py:518
  72.1 0.0 all-to-all-done.2
  72.1 2.3 %copy-done.10 = f32[64,144,128]{2,1,0:T(8,128)S(1)} copy-done((f32[64,144,128]{2,1,0:T(8,128)S(1)}, f32[64,144,128]{2,1,0:T(8,128)}, u32[]{:S(2)}) %copy-start.10) | copy-done | bytes 4718616
  74.4 8.5 %inputs.1 = (f32[64,128,128]{2,1,0:T(8,128)S(1)}, f32[8,8,128]{2,1,0:T(8,128)}, f32[128,128]{1,0:T(8,128)S(1)}, bf16[64,128,128]{2,1,0:T(8,128)(2,1)S(1)}) custom-call(f32[64,144,128]{2,1,0:T(8,128)S(1)} %copy-done.10, f32[16,16,128]{2,1,0:T(8,128)S(1)} %bitcast.11, f32[8,128]{1,0:T(8,128)S(1)} %reshape.57.rate_ref, f32[8,128]{1,0:T(8,128)S(1)} %reshape.58.res_ref, ...), custom_call_target="tpu_custom_call" | custom-call | flops 2415919104 | bytes 14680064 | tf_op jit(solution)/shard_map/inputs/pallas_call | solution.py:518
  83.0 2.0 %copy-done.3 = f32[64,128,128]{2,1,0:T(8,128)} copy-done((f32[64,128,128]{2,1,0:T(8,128)}, f32[64,128,128]{2,1,0:T(8,128)S(1)}, u32[]{:S(2)}) %copy-start.3) | copy-done | bytes 4194328
  84.9 1.3 copy-done.5
  86.2 6.6 %all-to-all-start.3 = ((f32[8,8,128]{2,1,0:T(8,128)}), f32[8,8,128]{2,1,0:T(8,128)S(1)}, u32[]{:S(2)}, u32[]{:S(2)}) async-start(f32[8,8,128]{2,1,0:T(8,128)} %get-tuple-element.61), calls=%async_computation.3 | async-start | bytes 65536 | tf_op jit(solution)/shard_map/all_to_all | solution.py:533
  92.9 1.6 %copy-done.6 = bf16[64,128,128]{2,1,0:T(8,128)(2,1)S(1)} copy-done((bf16[64,128,128]{2,1,0:T(8,128)(2,1)S(1)}, bf16[64,128,128]{2,1,0:T(8,128)(2,1)}, u32[]{:S(2)}) %copy-start.6) | copy-done | bytes 2097176
  94.5 6.5 %taps.1 = f32[128,128]{1,0:T(8,128)} custom-call(bf16[64,128,128]{2,1,0:T(8,128)(2,1)S(1)} %copy-done.6, bf16[64,144,128]{2,1,0:T(8,128)(2,1)S(1)} %get-tuple-element.63.x_ref, f32[128,128]{1,0:T(8,128)S(1)} %get-tuple-element.64.pay_ref), custom_call_target="tpu_custom_call" | custom-call | flops 536870912 | bytes 5242880 | tf_op jit(solution)/shard_map/taps/pallas_call | solution.py:518
  100.9 0.0 all-to-all-done.3.raw_ref
  100.9 7.7 %all-to-all-start.4 = ((f32[32,4,128]{2,1,0:T(4,128)}), f32[32,4,128]{2,1,0:T(4,128)S(1)}, u32[]{:S(2)}, u32[]{:S(2)}) async-start(f32[32,4,128]{2,1,0:T(4,128)} %bitcast.5), calls=%async_computation.4 | async-start | bytes 131072 | tf_op jit(solution)/shard_map/all_to_all | solution.py:533
  108.6 2.2 %copy-done.4 = f32[64,128,128]{2,1,0:T(8,128)S(1)} copy-done((f32[64,128,128]{2,1,0:T(8,128)S(1)}, f32[64,128,128]{2,1,0:T(8,128)}, u32[]{:S(2)}) %copy-start.4) | copy-done | bytes 4194328
  110.8 6.1 %final.1 = (bf16[1024,1024]{1,0:T(8,128)(2,1)}, f32[8,128]{1,0:T(8,128)}) custom-call(f32[64,128,128]{2,1,0:T(8,128)S(1)} %copy-done.4, bf16[1024,1024]{1,0:T(8,128)(2,1)} %h_ref.9, f32[8,16,128]{2,1,0:T(8,128)S(1)} %all-to-all-done.1.sq_ref, f32[8,128]{1,0:T(8,128)S(1)} %bitcast.15, f32[8,8,128]{2,1,0:T(8,128)S(1)} %all-to-all-done.3.raw_ref), custom_call_target="tpu_custom_call" | custom-call | bytes 8388608 | tf_op jit(solution)/shard_map/final/pallas_call | solution.py:518
  116.9 0.0 all-to-all-done.4.in_ref
  116.9 14.5 %all_to_all.30 = f32[32,4,128]{2,1,0:T(4,128)S(1)} all-to-all(f32[32,4,128]{2,1,0:T(4,128)S(1)} %sum.1), channel_id=1, replica_groups=mesh['ctx'=32,'ch'=8] {'ctx'}, dimensions={0} | all-to-all | bytes 131072 | tf_op jit(solution)/shard_map/all_to_all | solution.py:533
  131.4 0.6 outs.1
  132.0 0.1 reshape.67
  132.1 0.1 fusion.1
  132.2 0.1 copy.44
  132.3 0.1 copy.43
  132.3 0.6 subtract_multiply_fusion
  (19 shorter events, 0.1 us)
Async XLA Ops:
  0.6 10.6 %copy-start.11 = (f32[64,16]{0,1:T(8,128)S(1)}, f32[64,16]{0,1:T(8,128)}, u32[]{:S(2)}) copy-start(f32[64,16]{0,1:T(8,128)} %param.12) | copy-start | bytes 12292
  0.6 10.8 %copy-start.12 = (f32[64,16]{0,1:T(8,128)S(1)}, f32[64,16]{0,1:T(8,128)}, u32[]{:S(2)}) copy-start(f32[64,16]{0,1:T(8,128)} %param.11) | copy-start | bytes 12292
  0.7 24.5 %copy-start.8 = (f32[1024]{0:T(1024)S(1)}, f32[1024]{0:T(1024)}, u32[]{:S(2)}) copy-start(f32[1024]{0:T(1024)} %param.13) | copy-start | bytes 12292
  4.8 7.8 %collective-permute-start = (bf16[1024,128]{1,0:T(8,128)(2,1)S(1)}, bf16[1024,128]{1,0:T(8,128)(2,1)S(1)}, u32[]{:S(2)}, u32[]{:S(2)}) collective-permute-start(bf16[1024,128]{1,0:T(8,128)(2,1)S(1)} %get-tuple-element.41), channel_id=1, source_target_pairs={{0,8},{8,16},{16,24},{24,32},{32,40},{40,48},{48,56},{56,64},{64,7... | collective-permute-start | bytes 786440 | tf_op jit(solution)/shard_map/ppermute | solution.py:579
  9.3 7.7 %collective-permute-start.1 = (bf16[1024,128]{1,0:T(8,128)(2,1)S(1)}, bf16[1024,128]{1,0:T(8,128)(2,1)S(1)}, u32[]{:S(2)}, u32[]{:S(2)}) collective-permute-start(bf16[1024,128]{1,0:T(8,128)(2,1)S(1)} %get-tuple-element.43), channel_id=1, source_target_pairs={{8,0},{16,8},{24,16},{32,24},{40,32},{48,40},{56,48},{64,56},{72,6... | collective-permute-start | bytes 786440 | tf_op jit(solution)/shard_map/ppermute | solution.py:578
  17.0 20.9 %all-to-all-start.1 = ((f32[8,16,128]{2,1,0:T(8,128)}), f32[8,16,128]{2,1,0:T(8,128)S(1)}, u32[]{:S(2)}, u32[]{:S(2)}) async-start(f32[8,16,128]{2,1,0:T(8,128)} %edge.1), calls=%async_computation.1 | async-start | bytes 131072 | tf_op jit(solution)/shard_map/all_to_all | solution.py:533
  25.2 21.6 %copy-start.7 = (f32[1024]{0:T(1024)S(1)}, f32[1024]{0:T(1024)}, u32[]{:S(2)}) copy-start(f32[1024]{0:T(1024)} %param.9) | copy-start | bytes 12292
  34.3 1.5 %copy-start = (f32[32,144,128]{2,1,0:T(8,128)}, f32[32,144,128]{2,1,0:T(8,128)S(1)}, u32[]{:S(2)}) copy-start(f32[32,144,128]{2,1,0:T(8,128)S(1)} %get-tuple-element.48.aft_ref) | copy-start | bytes 7077892
  35.8 2.1 %copy-start.9 = (f32[64,144,128]{2,1,0:T(8,128)}, f32[64,144,128]{2,1,0:T(8,128)S(1)}, u32[]{:S(2)}) copy-start(f32[64,144,128]{2,1,0:T(8,128)S(1)} %get-tuple-element.45.gml_ref) | copy-start | bytes 14155780
  37.9 17.4 %all-to-all-start = ((f32[32,8,128]{2,1,0:T(8,128)}), f32[32,8,128]{2,1,0:T(8,128)S(1)}, u32[]{:S(2)}, u32[]{:S(2)}) async-start(f32[32,8,128]{2,1,0:T(8,128)} %bitcast.1), calls=%async_computation | async-start | bytes 262144 | tf_op jit(solution)/shard_map/all_to_all | solution.py:533
  46.8 1.7 %copy-start.1 = (f32[32,144,128]{2,1,0:T(8,128)S(1)}, f32[32,144,128]{2,1,0:T(8,128)}, u32[]{:S(2)}) copy-start(f32[32,144,128]{2,1,0:T(8,128)} %copy-done) | copy-start | bytes 7077892
  56.1 15.9 %all-to-all-start.2 = ((f32[32,8,128]{2,1,0:T(8,128)}), f32[32,8,128]{2,1,0:T(8,128)S(1)}, u32[]{:S(2)}, u32[]{:S(2)}) async-start(f32[32,8,128]{2,1,0:T(8,128)} %scan.1), calls=%async_computation.2 | async-start | bytes 262144 | tf_op jit(solution)/shard_map/all_to_all | solution.py:533
  63.6 1.7 %copy-start.2 = (f32[32,144,128]{2,1,0:T(8,128)S(1)}, f32[32,144,128]{2,1,0:T(8,128)}, u32[]{:S(2)}) copy-start(f32[32,144,128]{2,1,0:T(8,128)} %copy-done) | copy-start | bytes 7077892
  72.1 2.3 %copy-start.10 = (f32[64,144,128]{2,1,0:T(8,128)S(1)}, f32[64,144,128]{2,1,0:T(8,128)}, u32[]{:S(2)}) copy-start(f32[64,144,128]{2,1,0:T(8,128)} %copy-done.9) | copy-start | bytes 14155780
  83.0 2.0 %copy-start.3 = (f32[64,128,128]{2,1,0:T(8,128)}, f32[64,128,128]{2,1,0:T(8,128)S(1)}, u32[]{:S(2)}) copy-start(f32[64,128,128]{2,1,0:T(8,128)S(1)} %get-tuple-element.60.ig_ref) | copy-start | bytes 12582916
  84.9 1.3 copy-start.5
  86.2 14.7 %all-to-all-start.3 = ((f32[8,8,128]{2,1,0:T(8,128)}), f32[8,8,128]{2,1,0:T(8,128)S(1)}, u32[]{:S(2)}, u32[]{:S(2)}) async-start(f32[8,8,128]{2,1,0:T(8,128)} %get-tuple-element.61), calls=%async_computation.3 | async-start | bytes 65536 | tf_op jit(solution)/shard_map/all_to_all | solution.py:533
  92.9 1.6 %copy-start.6 = (bf16[64,128,128]{2,1,0:T(8,128)(2,1)S(1)}, bf16[64,128,128]{2,1,0:T(8,128)(2,1)}, u32[]{:S(2)}) copy-start(bf16[64,128,128]{2,1,0:T(8,128)(2,1)} %copy-done.5) | copy-start | bytes 6291460
  100.9 15.9 %all-to-all-start.4 = ((f32[32,4,128]{2,1,0:T(4,128)}), f32[32,4,128]{2,1,0:T(4,128)S(1)}, u32[]{:S(2)}, u32[]{:S(2)}) async-start(f32[32,4,128]{2,1,0:T(4,128)} %bitcast.5), calls=%async_computation.4 | async-start | bytes 131072 | tf_op jit(solution)/shard_map/all_to_all | solution.py:533
  108.6 2.2 %copy-start.4 = (f32[64,128,128]{2,1,0:T(8,128)S(1)}, f32[64,128,128]{2,1,0:T(8,128)}, u32[]{:S(2)}) copy-start(f32[64,128,128]{2,1,0:T(8,128)} %copy-done.3) | copy-start | bytes 12582916

commit v2 on v1

--- a/solution.py
+++ b/solution.py
@@ -432,7 +432,9 @@
             row_ref[i] = raw
 
 
-def taps_kernel(nb, grad_ref, x_ref, pay_ref, out_ref):
+def taps_kernel(nb, grad_ref, x_ref, pay_ref, out_ref, rows_ref):
+    step = pl.program_id(0)
+    steps = pl.num_programs(0)
     row, lane = iotas((B, B))
     lower = row >= lane
 
@@ -449,10 +451,19 @@
         held = nxt
     mirror = jnp.concatenate([mirror_matrix()] * 3, axis=0)
     taps = mm(fine(jnp.concatenate(rows, axis=0)), mirror, NN)
-    blank = jnp.zeros((2, B), f32)
-    out_ref[...] = pay_ref[...] + jnp.concatenate(
-        [taps[0:2], blank, taps[2:4], blank, taps[4:6], blank, taps[6:8], blank], axis=0
-    )
+    rows_ref[pl.ds(pl.multiple_of(GB * step, GB), GB), :] = taps
+    first = GB * 8
+    for at, row in ((first + step, 2), (first + 8 + step, 6), (first + 16 + 2 * step, 10)):
+        rows_ref[pl.ds(at, 1), :] = pay_ref[pl.ds(row, 1), :]
+    rows_ref[pl.ds(first + 17 + 2 * step, 1), :] = pay_ref[pl.ds(14, 1), :]
+
+    @pl.when(step == steps - 1)
+    def _():
+        rows = rows_ref[...]
+        hi, lo = split(rows[first + 16 :])
+        rows = jnp.concatenate([rows.astype(bf16), lo], axis=0)
+        for i in range(out_ref.shape[0]):
+            out_ref[i] = rows
 
 
 def final_kernel(nb, width, ig_ref, h_ref, sq_ref, gain_ref, raw_ref, out_ref, rms_ref):
@@ -493,25 +504,17 @@
         out_ref[i] = found[i] + jnp.where(ones, v, 0.0)
 
 
-def sum_kernel(in_ref, out_ref):
-    total = in_ref[0]
+def outs_kernel(scale, in_ref, tap_ref, gain_ref, skip_ref, mom_ref):
+    total = in_ref[0].astype(f32)
     for i in range(1, in_ref.shape[0]):
-        total = total + in_ref[i]
-    for i in range(out_ref.shape[0]):
-        out_ref[i] = total
-
-
-def outs_kernel(scale, in_ref, tap_ref, gain_ref, skip_ref, mom_ref):
-    owners = tap_ref.shape[0] // 2
-    steps = gain_ref.shape[0]
-    for r in range(2):
-        tap_ref[pl.ds(r, owners, stride=2), :] = in_ref[pl.ds(r, owners, stride=4), :] * scale
-    gain_ref[...] = in_ref[pl.ds(2, steps, stride=16), :] * scale
-    skip_ref[...] = in_ref[pl.ds(6, steps, stride=16), :] * scale
-    for r in range(2):
-        mom_ref[pl.ds(r, steps, stride=2), :] = (
-            in_ref[pl.ds(10 + 4 * r, steps, stride=16), :] * scale
-        )
+        total = total + in_ref[i].astype(f32)
+    total = total * scale
+    start = 0
+    for ref in (tap_ref, gain_ref, skip_ref, mom_ref):
+        size = ref.shape[0]
+        ref[...] = total[start : start + size]
+        start += size
+    mom_ref[...] += total[start:]
 
 
 def call(kernel, name, grid, ins, outs, args, flops=0, moved=0, scratch=(), aliases={}):
@@ -529,6 +532,10 @@
     )(*args)
 
 
+def in_hbm(*arrays):
+    return tuple(pltpu.with_memory_space_constraint(x, pltpu.HBM) for x in arrays)
+
+
 def exchange(x, axis):
     return lax.all_to_all(x, axis, 0, 0, tiled=True)
 
@@ -545,9 +552,7 @@
     steps = groups // GB
     grid = (steps,)
     shape = jax.ShapeDtypeStruct
-    hidden, cotangent, mr_filter = (
-        pltpu.with_memory_space_constraint(x, pltpu.HBM) for x in (hidden, cotangent, mr_filter)
-    )
+    hidden, cotangent, mr_filter = in_hbm(hidden, cotangent, mr_filter)
 
     wide = pl.BlockSpec((16 * GB, tokens), lambda i: (i, 0))
     thin = pl.BlockSpec((16 * GB, B), lambda i: (i, 0))
@@ -605,8 +610,8 @@
         (
             [tall, pair_tall, quad],
             [
-                shape((groups, 16 * (nb + 1), B), f32),
-                shape((groups // 2, 16 * (nb + 1), B), f32),
+                pltpu.HBM((groups, 16 * (nb + 1), B), f32),
+                pltpu.HBM((groups // 2, 16 * (nb + 1), B), f32),
                 shape((groups // 4, 16, B), f32),
             ],
         ),
@@ -634,7 +639,7 @@
             (
                 [at(tall), at(pay), at(quad_two)],
                 [
-                    shape((groups, 16 * (nb + 1), B), bf16),
+                    pltpu.HBM((groups, 16 * (nb + 1), B), bf16),
                     shape((16 * steps, B), f32),
                     shape((groups // 4, 32, B), f32),
                 ],
@@ -649,8 +654,10 @@
             aliases={9 + i: i for i in range(len(before))},
         )
 
+    grad_local, after_local = in_hbm(grad_local, after_local)
     arrived = exchange(packed.reshape(n_ctx, 8, B), "ctx")
     early = moments(0, (), h_prev)
+    early = in_hbm(early[0]) + tuple(early[1:])
     arrived, early = lax.optimization_barrier((arrived, tuple(early)))
     scanned = call(
         functools.partial(scan_kernel, n_ctx, tokens),
@@ -664,6 +671,7 @@
     scanned, edge_rows = lax.optimization_barrier((scanned, h_prev))
     after = exchange(scanned, "ctx").reshape(groups // 4, 16, B)
     units, part, ends = moments(steps // 2, early, edge_rows)
+    (units,) = in_hbm(units)
 
     ig, row_part, mostly, grad_mixed = call(
         functools.partial(inputs_kernel, nb, width),
@@ -676,10 +684,10 @@
         (
             [body, full(n_ch, nb, B), pay, body],
             [
-                shape((groups, 16 * nb, B), f32),
+                pltpu.HBM((groups, 16 * nb, B), f32),
                 shape((n_ch, nb, B), f32),
                 shape((16 * steps, B), f32),
-                shape((groups, 16 * nb, B), bf16),
+                pltpu.HBM((groups, 16 * nb, B), bf16),
             ],
         ),
         (
@@ -691,19 +699,23 @@
         scratch=[pltpu.VMEM((8 * nb, B), f32), pltpu.VMEM((groups, B), f32)],
     )
 
+    ig, grad_mixed = in_hbm(ig, grad_mixed)
     raw = exchange(row_part, "ch")
+    extra = groups // 4
+    lines = groups + 2 * steps + 2 * extra
     payload = call(
         functools.partial(taps_kernel, nb),
         "taps",
         grid,
         [body, tall, pay],
-        (pay, shape((16 * steps, B), f32)),
+        (full(n_ctx, lines, B), shape((n_ctx, lines, B), bf16)),
         (grad_mixed, units, mostly),
         flops=groups * 2 * 128 * 128 * 256,
         moved=5 * 2**20,
+        scratch=[pltpu.VMEM((lines - extra, B), f32)],
     )
     raw, payload = lax.optimization_barrier((raw, payload))
-    landed = exchange(payload.reshape(n_ctx, 4, B), "ctx")
+    landed = exchange(payload, "ctx")
     grad_hidden, grad_inv_rms = call(
         functools.partial(final_kernel, nb, width),
         "final",
@@ -717,17 +729,11 @@
         moved=8 * 2**20,
     )
     landed, grad_inv_rms = lax.optimization_barrier((landed, grad_inv_rms))
-    chunk = full(n_ctx, 4, B)
-    summed = call(
-        sum_kernel, "sum", (), [chunk], (chunk, shape((n_ctx, 4, B), f32)), (landed,),
-        moved=2**17,
-    )
-    total = exchange(summed, "ctx").reshape(4 * n_ctx, B)
     grad_mr, grad_gain, grad_skip, both = call(
         functools.partial(outs_kernel, scale),
         "outs",
         (),
-        [full(4 * n_ctx, B)],
+        [full(n_ctx, lines, B)],
         (
             [full(groups, taps), full(steps, B), full(steps, B), full(groups // 4, B)],
             [
@@ -737,8 +743,8 @@
                 shape((groups // 4, B), f32),
             ],
         ),
-        (total,),
-        moved=2**17,
+        (landed,),
+        moved=2**20,
     )
     both = both.reshape(groups, 2 * modes)
     first, second = both[:, :modes], both[:, modes:]

time: 134 us -> 120 us (0.90)
  local copies, waits for them, and re-layouts: 17.3 us -> 0.99 us
  blocking collectives: 14.5 us -> 0 us
  waiting for transfers between devices: 4.49 us -> 13.4 us
  Pallas kernels: 50.1 us -> 57.9 us
    unnamed x30 -> x12, local copies, waits for them, and re-layouts: 16.6 us -> 0.31 us
    all_to_all x1 -> x0, blocking collectives: 14.5 us -> none  [exchange(): return lax.all_to_all(x, axis, 0, 0, tiled=True)]
    all_to_all x5, waiting for transfers between devices: 0.01 us -> 8.91 us  [exchange(): return lax.all_to_all(x, axis, 0, 0, tiled=True)]
    pallas_call x11 -> x10, Pallas kernels: 50.1 us -> 57.9 us  [call(): pl.pallas_call(kernel, name=name, grid=grid, in_specs=ins, out_specs=outs...]
  transfers between devices with their start and end apart: 7 -> 7, of which waited for: 2 -> 3; matrix products, arithmetic and copies ran while one was open for 1% -> 1% of each run, Pallas kernels for 27% -> 35%
where the time goes in v2:
time: 120 us; the launch traced here: 119 us
  Pallas kernels  57.9 us (48%)
  starting transfers between devices  45.1 us (38%)
  waiting for transfers between devices  13.4 us (11%)
    pallas_call x10, Pallas kernels, call(): pl.pallas_call(kernel, name=name, grid=grid, in_specs=ins, out_specs=outs...  57.9 us
    all_to_all x5, starting transfers between devices, exchange(): return lax.all_to_all(x, axis, 0, 0, tiled=True)  38.6 us
    all_to_all x5, waiting for transfers between devices, exchange(): return lax.all_to_all(x, axis, 0, 0, tiled=True)  8.91 us
    ppermute x1, starting transfers between devices, local(): h_prev = lax.ppermute(tail, 'ctx', [(i, i + 1) for i in range(n_ctx - 1)])  4.51 us
    ppermute x1, waiting for transfers between devices, local(): ct_next = lax.ppermute(head, 'ctx', [(i, i - 1) for i in range(1, n_ctx)])  3.63 us
  transfers between devices with their start and end apart: 7, of which 3 were waited for; matrix products, arithmetic and copies ran while one was open for 1% of the time, Pallas kernels for 35%

profile of v2, /device:TPU:1, one launch (start us, length us, event | category | flops | bytes accessed | tf_op | source)
XLA Modules:
  0.0 118.8 jit_solution(7558092798634475674)
XLA Ops:
  0.6 0.0 copy-start.2
  0.6 0.0 copy-start.3
  0.7 0.0 copy-start.1
  0.7 4.1 %prep.1 = (bf16[1024,128]{1,0:T(8,128)(2,1)S(1)}, bf16[1024,128]{1,0:T(8,128)(2,1)S(1)}, f32[8,128]{1,0:T(8,128)S(1)}) custom-call(bf16[1024,1024]{1,0:T(8,128)(2,1)} %h_ref.9, bf16[1024,1024]{1,0:T(8,128)(2,1)} %ct_ref.7), custom_call_target="tpu_custom_call" | custom-call | bytes 3145728 | tf_op jit(solution)/shard_map/prep/pallas_call | solution.py:521
  4.8 4.5 %collective-permute-start = (bf16[1024,128]{1,0:T(8,128)(2,1)S(1)}, bf16[1024,128]{1,0:T(8,128)(2,1)S(1)}, u32[]{:S(2)}, u32[]{:S(2)}) collective-permute-start(bf16[1024,128]{1,0:T(8,128)(2,1)S(1)} %get-tuple-element.41), channel_id=1, source_target_pairs={{0,8},{8,16},{16,24},{24,32},{32,40},{40,48},{48,56},{56,64},{64,7... | collective-permute-start | bytes 786440 | tf_op jit(solution)/shard_map/ppermute | solution.py:584
  9.3 1.9 %collective-permute-start.1 = (bf16[1024,128]{1,0:T(8,128)(2,1)S(1)}, bf16[1024,128]{1,0:T(8,128)(2,1)S(1)}, u32[]{:S(2)}, u32[]{:S(2)}) collective-permute-start(bf16[1024,128]{1,0:T(8,128)(2,1)S(1)} %get-tuple-element.43), channel_id=1, source_target_pairs={{8,0},{16,8},{24,16},{32,24},{40,32},{48,40},{56,48},{64,56},{72,6... | collective-permute-start | bytes 786440 | tf_op jit(solution)/shard_map/ppermute | solution.py:583
  11.3 0.0 copy-done.2
  11.3 0.1 copy.35
  11.4 0.1 reshape.51.rate_ref
  11.4 0.0 copy-done.3
  11.4 0.1 copy.36
  11.5 0.1 reshape.52.res_ref
  11.6 0.1 tile.9.four_ref
  11.8 0.8 collective-permute-done.h_ref.hp_ref
  12.6 0.8 edge.1
  13.4 3.6 %collective-permute-done.1.ctn_ref = bf16[1024,128]{1,0:T(8,128)(2,1)S(1)} collective-permute-done((bf16[1024,128]{1,0:T(8,128)(2,1)S(1)}, bf16[1024,128]{1,0:T(8,128)(2,1)S(1)}, u32[]{:S(2)}, u32[]{:S(2)}) %collective-permute-start.1) | collective-permute-done | bytes 262176 | tf_op jit(solution)/shard_map/ppermute | solution.py:583
  17.0 8.2 %all-to-all-start.1 = ((f32[8,16,128]{2,1,0:T(8,128)}), f32[8,16,128]{2,1,0:T(8,128)S(1)}, u32[]{:S(2)}, u32[]{:S(2)}) async-start(f32[8,16,128]{2,1,0:T(8,128)} %edge.1), calls=%async_computation.1 | async-start | bytes 131072 | tf_op jit(solution)/shard_map/all_to_all | solution.py:540
  25.2 0.0 copy-done.1
  25.2 0.0 copy-start
  25.2 10.0 %grads.1 = (f32[64,144,128]{2,1,0:T(8,128)}, f32[32,144,128]{2,1,0:T(8,128)}, f32[16,16,128]{2,1,0:T(8,128)}) custom-call(bf16[1024,1024]{1,0:T(8,128)(2,1)} %ct_ref.7, bf16[1024,128]{1,0:T(8,128)(2,1)S(1)} %collective-permute-done.1.ctn_ref, f32[8,128]{1,0:T(8,128)S(1)} %reshape.51.rate_ref, f32[8,128]{1,0:T(8,128)S(1)} %reshape.52.res_ref, ...), custom_call_target="tpu_custom_call" | custom-call | flops 1811939328 | bytes 14680064 | tf_op jit(solution)/shard_map/grads/pallas_call | solution.py:521
  35.2 0.0 all-to-all-done.1.sq_ref
  35.2 8.8 %all-to-all-start = ((f32[32,8,128]{2,1,0:T(8,128)}), f32[32,8,128]{2,1,0:T(8,128)S(1)}, u32[]{:S(2)}, u32[]{:S(2)}) async-start(f32[32,8,128]{2,1,0:T(8,128)} %bitcast.1), calls=%async_computation | async-start | bytes 262144 | tf_op jit(solution)/shard_map/all_to_all | solution.py:540
  44.0 0.1 copy.38
  44.1 0.1 reshape.56.r_ref
  44.2 0.0 copy-done
  44.2 7.6 %moments.2 = (bf16[64,144,128]{2,1,0:T(8,128)(2,1)}, f32[128,128]{1,0:T(8,128)S(1)}, f32[16,32,128]{2,1,0:T(8,128)S(1)}) custom-call(bf16[1024,1024]{1,0:T(8,128)(2,1)} %h_ref.9, bf16[1024,128]{1,0:T(8,128)(2,1)S(1)} %collective-permute-done.h_ref.hp_ref, f32[8,16,128]{2,1,0:T(8,128)S(1)} %all-to-all-done.1.sq_ref, f32[8,128]{1,0:T(8,128)S(1)} %bitcast.9, ...), custom_call_target="tpu_custom_call" | custom-call | flops 805306368 | bytes 7340032 | tf_op jit(solution)/shard_map/moments/pallas_call | solution.py:521
  51.8 0.0 all-to-all-done.s_ref
  51.8 0.8 scan.1
  52.6 7.4 %all-to-all-start.2 = ((f32[32,8,128]{2,1,0:T(8,128)}), f32[32,8,128]{2,1,0:T(8,128)S(1)}, u32[]{:S(2)}, u32[]{:S(2)}) async-start(f32[32,8,128]{2,1,0:T(8,128)} %scan.1), calls=%async_computation.2 | async-start | bytes 262144 | tf_op jit(solution)/shard_map/all_to_all | solution.py:540
  60.0 0.1 reshape_reshape.3
  60.0 7.5 %moments.3 = (bf16[64,144,128]{2,1,0:T(8,128)(2,1)}, f32[128,128]{1,0:T(8,128)S(1)}, f32[16,32,128]{2,1,0:T(8,128)S(1)}) custom-call(bf16[1024,1024]{1,0:T(8,128)(2,1)} %h_ref.9, bf16[1024,128]{1,0:T(8,128)(2,1)S(1)} %collective-permute-done.h_ref.hp_ref, ...), custom_call_target="tpu_custom_call", output_to_operand_aliasing={{0}: (9, {}), {1}: (10, {}), {2}: (11, {})} | custom-call | flops 805306368 | bytes 7340032 | tf_op jit(solution)/shard_map/moments/pallas_call | solution.py:521
  67.6 0.0 all-to-all-done.2
  67.6 10.5 %inputs.1 = (f32[64,128,128]{2,1,0:T(8,128)}, f32[8,8,128]{2,1,0:T(8,128)}, f32[128,128]{1,0:T(8,128)S(1)}, bf16[64,128,128]{2,1,0:T(8,128)(2,1)}) custom-call(f32[64,144,128]{2,1,0:T(8,128)} %get-tuple-element.45.gml_ref, f32[16,16,128]{2,1,0:T(8,128)S(1)} %bitcast.8, f32[8,128]{1,0:T(8,128)S(1)} %reshape.51.rate_ref, f32[8,128]{1,0:T(8,128)S(1)} %reshape.52.res_ref, ...), custom_call_target="tpu_custom_call" | custom-call | flops 2415919104 | bytes 14680064 | tf_op jit(solution)/shard_map/inputs/pallas_call | solution.py:521
  78.1 6.6 %all-to-all-start.3 = ((f32[8,8,128]{2,1,0:T(8,128)}), f32[8,8,128]{2,1,0:T(8,128)S(1)}, u32[]{:S(2)}, u32[]{:S(2)}) async-start(f32[8,8,128]{2,1,0:T(8,128)} %get-tuple-element.61), calls=%async_computation.3 | async-start | bytes 65536 | tf_op jit(solution)/shard_map/all_to_all | solution.py:540
  84.8 8.9 %taps.1 = bf16[32,112,128]{2,1,0:T(8,128)(2,1)} custom-call(bf16[64,128,128]{2,1,0:T(8,128)(2,1)} %get-tuple-element.62.grad_ref, bf16[64,144,128]{2,1,0:T(8,128)(2,1)} %get-tuple-element.63.x_ref, f32[128,128]{1,0:T(8,128)S(1)} %get-tuple-element.64.pay_ref), custom_call_target="tpu_custom_call" | custom-call | flops 536870912 | bytes 5242880 | tf_op jit(solution)/shard_map/taps/pallas_call | solution.py:521
  93.7 0.0 all-to-all-done.3.raw_ref
  93.7 7.7 %all-to-all-start.4 = ((bf16[32,112,128]{2,1,0:T(8,128)(2,1)}), bf16[32,112,128]{2,1,0:T(8,128)(2,1)S(1)}, u32[]{:S(2)}, u32[]{:S(2)}) async-start(bf16[32,112,128]{2,1,0:T(8,128)(2,1)} %taps.1), calls=%async_computation.4 | async-start | bytes 1835008 | tf_op jit(solution)/shard_map/all_to_all | solution.py:540
  101.4 6.9 %final.1 = (bf16[1024,1024]{1,0:T(8,128)(2,1)}, f32[8,128]{1,0:T(8,128)}) custom-call(f32[64,128,128]{2,1,0:T(8,128)} %get-tuple-element.60.ig_ref, bf16[1024,1024]{1,0:T(8,128)(2,1)} %h_ref.9, f32[8,16,128]{2,1,0:T(8,128)S(1)} %all-to-all-done.1.sq_ref, f32[8,128]{1,0:T(8,128)S(1)} %bitcast.12, f32[8,8,128]{2,1,0:T(8,128)S(1)} %all-to-all-done.3.raw_ref), custom_call_target="tpu_custom_call" | custom-call | bytes 8388608 | tf_op jit(solution)/shard_map/final/pallas_call | solution.py:521
  108.3 8.9 %all-to-all-done.4.in_ref = bf16[32,112,128]{2,1,0:T(8,128)(2,1)S(1)} async-done(((bf16[32,112,128]{2,1,0:T(8,128)(2,1)}), bf16[32,112,128]{2,1,0:T(8,128)(2,1)S(1)}, u32[]{:S(2)}, u32[]{:S(2)}) %all-to-all-start.4) | async-done | bytes 917536 | tf_op jit(solution)/shard_map/all_to_all | solution.py:540
  117.2 0.7 outs.1
  117.9 0.1 reshape.59
  118.0 0.1 fusion.1
  118.1 0.1 copy.44
  118.1 0.1 copy.43
  118.2 0.6 subtract_multiply_fusion
  (2 shorter events, 0.0 us)
Async XLA Ops:
  0.6 10.6 %copy-start.2 = (f32[64,16]{0,1:T(8,128)S(1)}, f32[64,16]{0,1:T(8,128)}, u32[]{:S(2)}) copy-start(f32[64,16]{0,1:T(8,128)} %param.12) | copy-start | bytes 12292
  0.6 10.8 %copy-start.3 = (f32[64,16]{0,1:T(8,128)S(1)}, f32[64,16]{0,1:T(8,128)}, u32[]{:S(2)}) copy-start(f32[64,16]{0,1:T(8,128)} %param.11) | copy-start | bytes 12292
  0.7 24.5 %copy-start.1 = (f32[1024]{0:T(1024)S(1)}, f32[1024]{0:T(1024)}, u32[]{:S(2)}) copy-start(f32[1024]{0:T(1024)} %param.13) | copy-start | bytes 12292
  4.8 7.8 %collective-permute-start = (bf16[1024,128]{1,0:T(8,128)(2,1)S(1)}, bf16[1024,128]{1,0:T(8,128)(2,1)S(1)}, u32[]{:S(2)}, u32[]{:S(2)}) collective-permute-start(bf16[1024,128]{1,0:T(8,128)(2,1)S(1)} %get-tuple-element.41), channel_id=1, source_target_pairs={{0,8},{8,16},{16,24},{24,32},{32,40},{40,48},{48,56},{56,64},{64,7... | collective-permute-start | bytes 786440 | tf_op jit(solution)/shard_map/ppermute | solution.py:584
  9.3 7.7 %collective-permute-start.1 = (bf16[1024,128]{1,0:T(8,128)(2,1)S(1)}, bf16[1024,128]{1,0:T(8,128)(2,1)S(1)}, u32[]{:S(2)}, u32[]{:S(2)}) collective-permute-start(bf16[1024,128]{1,0:T(8,128)(2,1)S(1)} %get-tuple-element.43), channel_id=1, source_target_pairs={{8,0},{16,8},{24,16},{32,24},{40,32},{48,40},{56,48},{64,56},{72,6... | collective-permute-start | bytes 786440 | tf_op jit(solution)/shard_map/ppermute | solution.py:583
  17.0 18.2 %all-to-all-start.1 = ((f32[8,16,128]{2,1,0:T(8,128)}), f32[8,16,128]{2,1,0:T(8,128)S(1)}, u32[]{:S(2)}, u32[]{:S(2)}) async-start(f32[8,16,128]{2,1,0:T(8,128)} %edge.1), calls=%async_computation.1 | async-start | bytes 131072 | tf_op jit(solution)/shard_map/all_to_all | solution.py:540
  25.2 19.0 %copy-start = (f32[1024]{0:T(1024)S(1)}, f32[1024]{0:T(1024)}, u32[]{:S(2)}) copy-start(f32[1024]{0:T(1024)} %param.9) | copy-start | bytes 12292
  35.2 16.5 %all-to-all-start = ((f32[32,8,128]{2,1,0:T(8,128)}), f32[32,8,128]{2,1,0:T(8,128)S(1)}, u32[]{:S(2)}, u32[]{:S(2)}) async-start(f32[32,8,128]{2,1,0:T(8,128)} %bitcast.1), calls=%async_computation | async-start | bytes 262144 | tf_op jit(solution)/shard_map/all_to_all | solution.py:540
  52.6 15.0 %all-to-all-start.2 = ((f32[32,8,128]{2,1,0:T(8,128)}), f32[32,8,128]{2,1,0:T(8,128)S(1)}, u32[]{:S(2)}, u32[]{:S(2)}) async-start(f32[32,8,128]{2,1,0:T(8,128)} %scan.1), calls=%async_computation.2 | async-start | bytes 262144 | tf_op jit(solution)/shard_map/all_to_all | solution.py:540
  78.1 15.6 %all-to-all-start.3 = ((f32[8,8,128]{2,1,0:T(8,128)}), f32[8,8,128]{2,1,0:T(8,128)S(1)}, u32[]{:S(2)}, u32[]{:S(2)}) async-start(f32[8,8,128]{2,1,0:T(8,128)} %get-tuple-element.61), calls=%async_computation.3 | async-start | bytes 65536 | tf_op jit(solution)/shard_map/all_to_all | solution.py:540
  93.7 23.5 %all-to-all-start.4 = ((bf16[32,112,128]{2,1,0:T(8,128)(2,1)}), bf16[32,112,128]{2,1,0:T(8,128)(2,1)S(1)}, u32[]{:S(2)}, u32[]{:S(2)}) async-start(bf16[32,112,128]{2,1,0:T(8,128)(2,1)} %taps.1), calls=%async_computation.4 | async-start | bytes 1835008 | tf_op jit(solution)/shard_map/all_to_all | solution.py:540

commit v3 on v2

--- a/solution.py
+++ b/solution.py
@@ -10,7 +10,8 @@
 eps_norm = 1e-06
 B = 128
 GB = 8
-VMEM = 16 * 1024 * 1024
+VMEM = 30 * 1024 * 1024
+PER = {"prep": 4, "grads": 2, "moments": 1, "inputs": 4, "taps": 2, "final": 4}
 f32 = jnp.float32
 bf16 = jnp.bfloat16
 
@@ -48,6 +49,10 @@
 
 def lane_sums(x):
     return mm(jnp.ones((8, 3 * B), bf16), fine(x), NT)[:1]
+
+
+def turned_sums(x):
+    return jnp.sum(jnp.transpose(x), axis=0, keepdims=True)
 
 
 def toeplitz(row):
@@ -65,23 +70,24 @@
     return jnp.sum(total, axis=0, keepdims=True)
 
 
-def prep_kernel(h_ref, ct_ref, tail_ref, head_ref, sq_ref, acc_ref):
+def prep_kernel(at, h_ref, ct_ref, tail_ref, head_ref, sq_ref, acc_ref):
     tokens = h_ref.shape[1]
 
-    @pl.when(pl.program_id(0) == 0)
-    def _():
+    def clear():
         acc_ref[...] = jnp.zeros_like(acc_ref)
 
+    begin(at, clear)
     h = h_ref[...].astype(f32)
     acc_ref[...] += jnp.sum(jnp.square(h).reshape(h.shape[0] // 8, 8, tokens), axis=0)
     tail_ref[...] = h_ref[:, tokens - B :]
     head_ref[...] = ct_ref[...]
 
-    @pl.when(pl.program_id(0) == pl.num_programs(0) - 1)
-    def _():
+    def write():
         row = jnp.sum(acc_ref[...], axis=0, keepdims=True)
         for b in range(tokens // B):
             sq_ref[pl.ds(b, 1), :] = row[:, B * b : B * b + B]
+
+    finish(at, write)
 
 
 def edge_kernel(nb, h_ref, sq_ref, out_ref):
@@ -101,9 +107,9 @@
 
 
 def grads_kernel(
-    nb, ct_ref, ctn_ref, rate_ref, res_ref, four_ref, skip_ref, gml_ref, aft_ref, pack_ref
+    nb, at, ct_ref, ctn_ref, rate_ref, res_ref, four_ref, skip_ref, gml_ref, aft_ref, pack_ref
 ):
-    step = pl.program_id(0)
+    step = at[0]
     row, lane = iotas((B, B))
     upper = lane <= row
     back = ((B - lane) % B).astype(f32)
@@ -193,19 +199,19 @@
 
 
 def moments_kernel(
-    nb, width, offset, h_ref, hp_ref, sq_ref, gain_ref, ct_ref, w_ref, rate_ref, four_ref,
+    nb, width, at, h_ref, hp_ref, sq_ref, gain_ref, ct_ref, w_ref, pair_ref, four_ref,
     aft_ref, *refs,
 ):
     x_ref, part_ref, end_ref, w_scratch = refs[-4:]
-    step = pl.program_id(0) + offset
-
-    @pl.when(step == offset)
-    def _():
+    step = at[0]
+
+    def load():
         w_scratch[...] = w_ref[...].astype(f32)
+
+    begin(at, load)
 
     row, lane = iotas((B, B))
     upper = lane >= row
-    ahead = lane.astype(f32)
     togo = float(B) - row.astype(f32)
     slot = lane % 64
     first_half = lane < 64
@@ -299,17 +305,17 @@
         quads.append(jnp.sum(joined[0], axis=0, keepdims=True))
         end_ref[k] = jnp.concatenate(joined[1:], axis=0)
     skip_row = lane_sums(jnp.concatenate(skip_parts, axis=0))
-    corr = jnp.concatenate(corrs, axis=0)
-    fall = jnp.exp(-spread(rate_ref[pl.ds(step, 1), :]) * ahead)
-    table = []
-    for g in range(GB):
-        table += [fall[16 * g : 16 * g + 16], fall[16 * g : 16 * g + 16] * ahead[:16]]
-    t_hi, t_lo = split(jnp.concatenate(table, axis=0))
-    c_hi, c_lo = split(corr)
+    below = row.astype(f32)
+    tables = []
+    for k in range(GB // 4):
+        fall = jnp.exp(-jnp.broadcast_to(pair_ref[k], (B, B)) * below)
+        tables.append(jnp.where(lane % 32 < 16, fall, fall * below))
+    t_hi, t_lo = split(jnp.concatenate(tables, axis=1))
+    c_hi, c_lo = split(jnp.concatenate(corrs, axis=0))
     near = mm(
         jnp.concatenate([c_hi, c_lo, c_hi], axis=1),
-        jnp.concatenate([t_hi, t_hi, t_lo], axis=1),
-        NT,
+        jnp.concatenate([t_hi, t_hi, t_lo], axis=0),
+        NN,
     )
     n_row, n_lane = iotas((GB, 32 * GB))
     near = jnp.sum(jnp.where(n_lane // 32 == n_row, near, 0.0), axis=0, keepdims=True)
@@ -327,15 +333,16 @@
 
 
 def inputs_kernel(
-    nb, width, gml_ref, a_ref, rate_ref, res_ref, pair_ref, h_ref, sq_ref, gain_ref, w_ref,
+    nb, width, at, gml_ref, a_ref, rate_ref, res_ref, pair_ref, h_ref, sq_ref, gain_ref, w_ref,
     part_ref, end_ref, ig_ref, row_ref, pay_ref, grad_ref, acc_ref, w_scratch,
 ):
-    step = pl.program_id(0)
-
-    @pl.when(step == 0)
-    def _():
+    step = at[0]
+
+    def load():
         w_scratch[...] = mm(w_ref[...], mirror_matrix(), NN)
         acc_ref[...] = jnp.zeros_like(acc_ref)
+
+    begin(at, load)
 
     row, lane = iotas((B, B))
     upper = lane <= row
@@ -416,25 +423,25 @@
         held = nxt
     for b in range(nb):
         acc_ref[pl.ds(8 * b, 8), :] = sums[b]
-    gain_row = lane_sums(jnp.concatenate(gain_parts, axis=0))
+    gain_row = turned_sums(jnp.concatenate(gain_parts, axis=0))
     blank = jnp.zeros((1, B), f32)
     pay_ref[...] = part_ref[...] + jnp.concatenate(
         [blank, blank, gain_row] + [blank] * 7 + [quads[0]] + [blank] * 3 + [quads[1], blank],
         axis=0,
     )
 
-    @pl.when(step == pl.num_programs(0) - 1)
-    def _():
+    def write():
         raw = jnp.concatenate(
             [jnp.sum(sums[b], axis=0, keepdims=True) for b in range(nb)], axis=0
         )
         for i in range(row_ref.shape[0]):
             row_ref[i] = raw
 
-
-def taps_kernel(nb, grad_ref, x_ref, pay_ref, out_ref, rows_ref):
-    step = pl.program_id(0)
-    steps = pl.num_programs(0)
+    finish(at, write)
+
+
+def taps_kernel(nb, at, grad_ref, x_ref, pay_ref, out_ref, rows_ref):
+    step = at[0]
     row, lane = iotas((B, B))
     lower = row >= lane
 
@@ -453,21 +460,22 @@
     taps = mm(fine(jnp.concatenate(rows, axis=0)), mirror, NN)
     rows_ref[pl.ds(pl.multiple_of(GB * step, GB), GB), :] = taps
     first = GB * 8
-    for at, row in ((first + step, 2), (first + 8 + step, 6), (first + 16 + 2 * step, 10)):
-        rows_ref[pl.ds(at, 1), :] = pay_ref[pl.ds(row, 1), :]
+    for line, row in ((first + step, 2), (first + 8 + step, 6), (first + 16 + 2 * step, 10)):
+        rows_ref[pl.ds(line, 1), :] = pay_ref[pl.ds(row, 1), :]
     rows_ref[pl.ds(first + 17 + 2 * step, 1), :] = pay_ref[pl.ds(14, 1), :]
 
-    @pl.when(step == steps - 1)
-    def _():
+    def write():
         rows = rows_ref[...]
         hi, lo = split(rows[first + 16 :])
         rows = jnp.concatenate([rows.astype(bf16), lo], axis=0)
         for i in range(out_ref.shape[0]):
             out_ref[i] = rows
 
-
-def final_kernel(nb, width, ig_ref, h_ref, sq_ref, gain_ref, raw_ref, out_ref, rms_ref):
-    step = pl.program_id(0)
+    finish(at, write)
+
+
+def final_kernel(nb, width, at, ig_ref, h_ref, sq_ref, gain_ref, raw_ref, out_ref, rms_ref):
+    step = at[0]
     inverse = inverse_rows(sq_ref, width)
     gains = spread(gain_ref[pl.ds(step, 1), :])
     raw = raw_ref[0]
@@ -517,19 +525,57 @@
     mom_ref[...] += total[start:]
 
 
-def call(kernel, name, grid, ins, outs, args, flops=0, moved=0, scratch=(), aliases={}):
+def call(
+    kernel, name, ins, outs, args, steps=0, per=1, offset=0, flops=0, moved=0, scratch=(),
+    aliases={},
+):
+    def spec(entry):
+        if isinstance(entry, pl.BlockSpec):
+            return entry
+        lead, rest = entry[0], tuple(entry[1:])
+        if lead is None:
+            return pl.BlockSpec(rest, lambda *i: (0,) * len(rest))
+        return pl.BlockSpec(
+            (lead * per,) + rest, lambda i: (i + offset // per,) + (0,) * len(rest)
+        )
+
+    entries = list(ins) + list(outs[0]) + [(None,)] * len(scratch)
+
+    def body(*refs):
+        if not steps:
+            kernel(*refs)
+            return
+        for sub in range(per):
+            views = []
+            for entry, ref in zip(entries, refs):
+                if isinstance(entry, pl.BlockSpec) or entry[0] is None or per == 1:
+                    views.append(ref)
+                else:
+                    views.append(ref.at[pl.ds(sub * entry[0], entry[0])])
+            kernel((pl.program_id(0) * per + sub + offset, sub == 0, sub == per - 1), *views)
+
     return pl.pallas_call(
-        kernel,
+        body,
         name=name,
-        grid=grid,
-        in_specs=ins,
-        out_specs=outs[0],
-        out_shape=outs[1],
+        grid=(steps // per,) if steps else (),
+        in_specs=[spec(entry) for entry in ins],
+        out_specs=[spec(entry) for entry in outs[0]],
+        out_shape=list(outs[1]),
         scratch_shapes=scratch,
         input_output_aliases=aliases,
         compiler_params=pltpu.CompilerParams(vmem_limit_bytes=VMEM),
         cost_estimate=pl.CostEstimate(flops=flops, bytes_accessed=moved, transcendentals=0),
     )(*args)
+
+
+def begin(at, action):
+    if at[1]:
+        pl.when(pl.program_id(0) == 0)(action)
+
+
+def finish(at, action):
+    if at[2]:
+        pl.when(pl.program_id(0) == pl.num_programs(0) - 1)(action)
 
 
 def in_hbm(*arrays):
@@ -550,44 +596,43 @@
     scale = (tokens * n_ctx) ** (-0.5)
     nb = tokens // B
     steps = groups // GB
-    grid = (steps,)
     shape = jax.ShapeDtypeStruct
     hidden, cotangent, mr_filter = in_hbm(hidden, cotangent, mr_filter)
 
-    wide = pl.BlockSpec((16 * GB, tokens), lambda i: (i, 0))
-    thin = pl.BlockSpec((16 * GB, B), lambda i: (i, 0))
-    tall = pl.BlockSpec((GB, 16 * (nb + 1), B), lambda i: (i, 0, 0))
-    pair_tall = pl.BlockSpec((GB // 2, 16 * (nb + 1), B), lambda i: (i, 0, 0))
-    body = pl.BlockSpec((GB, 16 * nb, B), lambda i: (i, 0, 0))
-    quad = pl.BlockSpec((GB // 4, 16, B), lambda i: (i, 0, 0))
-    quad_two = pl.BlockSpec((GB // 4, 32, B), lambda i: (i, 0, 0))
-    quad_row = pl.BlockSpec((GB // 4, 1, B), lambda i: (i, 0, 0))
-    pay = pl.BlockSpec((16, B), lambda i: (i, 0))
+    wide = (16 * GB, tokens)
+    thin = (16 * GB, B)
+    tall = (GB, 16 * (nb + 1), B)
+    pair_tall = (GB // 2, 16 * (nb + 1), B)
+    body = (GB, 16 * nb, B)
+    quad = (GB // 4, 16, B)
+    quad_two = (GB // 4, 32, B)
+    quad_row = (GB // 4, 1, B)
+    pay = (16, B)
 
     def full(*dims):
-        return pl.BlockSpec(dims, lambda *i: (0,) * len(dims))
+        return (None,) + dims
 
     tail, head, own_sq = call(
         prep_kernel,
         "prep",
-        grid,
         [wide, thin],
         (
             [thin, thin, full(nb, B)],
             [shape((channels, B), bf16), shape((channels, B), bf16), shape((nb, B), f32)],
         ),
         (hidden, cotangent),
+        steps=steps,
+        per=PER["prep"],
         moved=3 * 2**20,
         scratch=[pltpu.VMEM((8, tokens), f32)],
     )
     ct_next = lax.ppermute(head, "ctx", [(i, i - 1) for i in range(1, n_ctx)])
     h_prev = lax.ppermute(tail, "ctx", [(i, i + 1) for i in range(n_ctx - 1)])
-    edge = call(
+    (edge,) = call(
         functools.partial(edge_kernel, nb),
         "edge",
-        (),
         [full(channels, B), full(nb, B)],
-        (full(n_ch, 16, B), shape((n_ch, 16, B), f32)),
+        ([full(n_ch, 16, B)], [shape((n_ch, 16, B), f32)]),
         (h_prev, own_sq),
         moved=2**18,
     )
@@ -598,6 +643,7 @@
     res_flat = residue.reshape(steps, B)
     rate_four = jnp.tile(decay_rate, (1, 4)).reshape(groups // 2, B)
     rate_pair = jnp.concatenate([decay_rate, decay_rate], axis=1).reshape(groups // 4, B)
+    rate_rows = rate_pair.reshape(groups // 4, 1, B)
     gain_flat = norm_gain.reshape(steps, B)
     skip_flat = skip_weight.reshape(steps, B)
     flat = full(steps, B)
@@ -605,7 +651,6 @@
     grad_local, after_local, packed = call(
         functools.partial(grads_kernel, nb),
         "grads",
-        grid,
         [wide, thin, flat, flat, full(groups // 2, B), flat],
         (
             [tall, pair_tall, quad],
@@ -617,27 +662,23 @@
         ),
         (cotangent, ct_next, rate_flat, res_flat, rate_four, skip_flat),
         flops=groups * 2 * 144 * 256 * 384,
+        steps=steps,
+        per=PER["grads"],
         moved=14 * 2**20,
     )
 
     def moments(offset, before, x_next):
-        def at(spec):
-            return pl.BlockSpec(
-                spec.block_shape, lambda i: (i + offset,) + spec.index_map(i)[1:]
-            )
-
         held = [pl.BlockSpec(memory_space=pl.ANY)] * len(before)
         return call(
-            functools.partial(moments_kernel, nb, width, offset),
+            functools.partial(moments_kernel, nb, width),
             "moments",
-            (steps // 2,),
             [
-                at(wide), at(thin), full(n_ch, 16, B), flat, at(wide), full(groups, B), flat,
-                full(groups // 2, B), at(pair_tall),
+                wide, thin, full(n_ch, 16, B), flat, wide, full(groups, B), quad_row,
+                full(groups // 2, B), pair_tall,
             ]
             + held,
             (
-                [at(tall), at(pay), at(quad_two)],
+                [tall, pay, quad_two],
                 [
                     pltpu.HBM((groups, 16 * (nb + 1), B), bf16),
                     shape((16 * steps, B), f32),
@@ -645,9 +686,12 @@
                 ],
             ),
             (
-                hidden, x_next, squares, gain_flat, cotangent, mr_filter, rate_flat, rate_four,
+                hidden, x_next, squares, gain_flat, cotangent, mr_filter, rate_rows, rate_four,
                 after_local, *before,
             ),
+            steps=steps // 2,
+            per=PER["moments"],
+            offset=offset,
             flops=groups * 128 * 256 * 384,
             moved=7 * 2**20,
             scratch=[pltpu.VMEM((groups, B), f32)],
@@ -659,12 +703,11 @@
     early = moments(0, (), h_prev)
     early = in_hbm(early[0]) + tuple(early[1:])
     arrived, early = lax.optimization_barrier((arrived, tuple(early)))
-    scanned = call(
+    (scanned,) = call(
         functools.partial(scan_kernel, n_ctx, tokens),
         "scan",
-        (),
         [full(n_ctx, 8, B), full(groups // 4, B)],
-        (full(n_ctx, 8, B), shape((n_ctx, 8, B), f32)),
+        ([full(n_ctx, 8, B)], [shape((n_ctx, 8, B), f32)]),
         (arrived, rate_pair),
         moved=2**18,
     )
@@ -676,7 +719,6 @@
     ig, row_part, mostly, grad_mixed = call(
         functools.partial(inputs_kernel, nb, width),
         "inputs",
-        grid,
         [
             tall, quad, flat, flat, quad_row, wide, full(n_ch, 16, B), flat, full(groups, B),
             pay, quad_two,
@@ -691,10 +733,12 @@
             ],
         ),
         (
-            grad_local, after, rate_flat, res_flat, rate_pair.reshape(groups // 4, 1, B), hidden,
+            grad_local, after, rate_flat, res_flat, rate_rows, hidden,
             squares, gain_flat, mr_filter, part, ends,
         ),
         flops=groups * 2 * 144 * 256 * 512,
+        steps=steps,
+        per=PER["inputs"],
         moved=14 * 2**20,
         scratch=[pltpu.VMEM((8 * nb, B), f32), pltpu.VMEM((groups, B), f32)],
     )
@@ -703,14 +747,15 @@
     raw = exchange(row_part, "ch")
     extra = groups // 4
     lines = groups + 2 * steps + 2 * extra
-    payload = call(
+    (payload,) = call(
         functools.partial(taps_kernel, nb),
         "taps",
-        grid,
         [body, tall, pay],
-        (full(n_ctx, lines, B), shape((n_ctx, lines, B), bf16)),
+        ([full(n_ctx, lines, B)], [shape((n_ctx, lines, B), bf16)]),
         (grad_mixed, units, mostly),
         flops=groups * 2 * 128 * 128 * 256,
+        steps=steps,
+        per=PER["taps"],
         moved=5 * 2**20,
         scratch=[pltpu.VMEM((lines - extra, B), f32)],
     )
@@ -719,20 +764,20 @@
     grad_hidden, grad_inv_rms = call(
         functools.partial(final_kernel, nb, width),
         "final",
-        grid,
         [body, wide, full(n_ch, 16, B), flat, full(n_ch, nb, B)],
         (
             [wide, full(nb, B)],
             [shape((channels, tokens), bf16), shape((nb, B), f32)],
         ),
         (ig, hidden, squares, gain_flat, raw),
+        steps=steps,
+        per=PER["final"],
         moved=8 * 2**20,
     )
     landed, grad_inv_rms = lax.optimization_barrier((landed, grad_inv_rms))
     grad_mr, grad_gain, grad_skip, both = call(
         functools.partial(outs_kernel, scale),
         "outs",
-        (),
         [full(n_ctx, lines, B)],
         (
             [full(groups, taps), full(steps, B), full(steps, B), full(groups // 4, B)],

time: 120 us -> 111 us (0.925)
  Pallas kernels: 57.9 us -> 46.7 us
  waiting for transfers between devices: 13.4 us -> 16.1 us
    pallas_call x10, Pallas kernels: 57.9 us -> 46.7 us  [call(): pl.pallas_call(body, name=name, grid=(steps // per,) if steps else (), in...]
    all_to_all x5, waiting for transfers between devices: 8.91 us -> 11.7 us  [exchange(): return lax.all_to_all(x, axis, 0, 0, tiled=True)]
  transfers between devices with their start and end apart: 7 -> 7, of which waited for: 3 -> 4; matrix products, arithmetic and copies ran while one was open for 1% -> 1% of each run, Pallas kernels for 35% -> 32%
where the time goes in v3:
time: 111 us
  Pallas kernels  46.7 us (42%)
  starting transfers between devices  45.5 us (41%)
  waiting for transfers between devices  16.1 us (15%)
    pallas_call x10, Pallas kernels, call(): pl.pallas_call(body, name=name, grid=(steps // per,) if steps else (), in...  46.7 us
    all_to_all x5, starting transfers between devices, exchange(): return lax.all_to_all(x, axis, 0, 0, tiled=True)  39.1 us
    all_to_all x5, waiting for transfers between devices, exchange(): return lax.all_to_all(x, axis, 0, 0, tiled=True)  11.7 us
    ppermute x1, starting transfers between devices, local(): h_prev = lax.ppermute(tail, 'ctx', [(i, i + 1) for i in range(n_ctx - 1)])  4.51 us
    ppermute x1, waiting for transfers between devices, local(): ct_next = lax.ppermute(head, 'ctx', [(i, i - 1) for i in range(1, n_ctx)])  3.63 us
  transfers between devices with their start and end apart: 7, of which 4 were waited for; matrix products, arithmetic and copies ran while one was open for 1% of the time, Pallas kernels for 32%

profile of v3, /device:TPU:1, one launch (start us, length us, event | category | flops | bytes accessed | tf_op | source)
XLA Modules:
  0.0 110.8 jit_solution(6307011650659491400)
XLA Ops:
  0.6 0.0 copy-start.2
  0.6 0.0 copy-start.3
  0.7 0.0 copy-start.1
  0.7 1.7 %prep.1 = (bf16[1024,128]{1,0:T(8,128)(2,1)S(1)}, bf16[1024,128]{1,0:T(8,128)(2,1)S(1)}, f32[8,128]{1,0:T(8,128)S(1)}) custom-call(bf16[1024,1024]{1,0:T(8,128)(2,1)} %refs_1_.3, bf16[1024,1024]{1,0:T(8,128)(2,1)} %refs_4_.3), custom_call_target="tpu_custom_call" | custom-call | bytes 3145728 | tf_op jit(solution)/shard_map/prep/pallas_call | solution.py:557
  2.4 4.5 %collective-permute-start = (bf16[1024,128]{1,0:T(8,128)(2,1)S(1)}, bf16[1024,128]{1,0:T(8,128)(2,1)S(1)}, u32[]{:S(2)}, u32[]{:S(2)}) collective-permute-start(bf16[1024,128]{1,0:T(8,128)(2,1)S(1)} %get-tuple-element.41), channel_id=1, source_target_pairs={{0,8},{8,16},{16,24},{24,32},{32,40},{40,48},{48,56},{56,64},{64,7... | collective-permute-start | bytes 786440 | tf_op jit(solution)/shard_map/ppermute | solution.py:630
  6.9 1.9 %collective-permute-start.1 = (bf16[1024,128]{1,0:T(8,128)(2,1)S(1)}, bf16[1024,128]{1,0:T(8,128)(2,1)S(1)}, u32[]{:S(2)}, u32[]{:S(2)}) collective-permute-start(bf16[1024,128]{1,0:T(8,128)(2,1)S(1)} %get-tuple-element.43), channel_id=1, source_target_pairs={{8,0},{16,8},{24,16},{32,24},{40,32},{48,40},{56,48},{64,56},{72,6... | collective-permute-start | bytes 786440 | tf_op jit(solution)/shard_map/ppermute | solution.py:629
  8.9 0.0 copy-done.2
  8.9 0.1 copy.37
  8.9 0.1 reshape.51.refs_2_
  9.0 0.0 copy-done.3
  9.0 0.1 copy.38
  9.1 0.1 reshape.52.refs_3_
  9.2 0.1 tile.9.refs_4_.refs_7_
  9.4 0.8 collective-permute-done.refs_0_.refs_1_
  10.2 0.8 edge.1
  11.0 3.6 %collective-permute-done.1.refs_1_ = bf16[1024,128]{1,0:T(8,128)(2,1)S(1)} collective-permute-done((bf16[1024,128]{1,0:T(8,128)(2,1)S(1)}, bf16[1024,128]{1,0:T(8,128)(2,1)S(1)}, u32[]{:S(2)}, u32[]{:S(2)}) %collective-permute-start.1) | collective-permute-done | bytes 262176 | tf_op jit(solution)/shard_map/ppermute | solution.py:629
  14.6 8.2 %all-to-all-start.1 = ((f32[8,16,128]{2,1,0:T(8,128)}), f32[8,16,128]{2,1,0:T(8,128)S(1)}, u32[]{:S(2)}, u32[]{:S(2)}) async-start(f32[8,16,128]{2,1,0:T(8,128)} %edge.1), calls=%async_computation.1 | async-start | bytes 131072 | tf_op jit(solution)/shard_map/all_to_all | solution.py:586
  22.8 0.0 copy-done.1
  22.8 0.0 copy-start
  22.8 8.2 %grads.1 = (f32[64,144,128]{2,1,0:T(8,128)}, f32[32,144,128]{2,1,0:T(8,128)}, f32[16,16,128]{2,1,0:T(8,128)}) custom-call(bf16[1024,1024]{1,0:T(8,128)(2,1)} %refs_4_.3, bf16[1024,128]{1,0:T(8,128)(2,1)S(1)} %collective-permute-done.1.refs_1_, f32[8,128]{1,0:T(8,128)S(1)} %reshape.51.refs_2_, f32[8,128]{1,0:T(8,128)S(1)} %reshape.52.refs_3_, ...), custom_call_target="tpu_custom_call" | custom-call | flops 1811939328 | bytes 14680064 | tf_op jit(solution)/shard_map/grads/pallas_call | solution.py:557
  31.0 0.0 all-to-all-done.1.refs_2_.refs_6_
  31.0 8.8 %all-to-all-start = ((f32[32,8,128]{2,1,0:T(8,128)}), f32[32,8,128]{2,1,0:T(8,128)S(1)}, u32[]{:S(2)}, u32[]{:S(2)}) async-start(f32[32,8,128]{2,1,0:T(8,128)} %bitcast.1), calls=%async_computation | async-start | bytes 262144 | tf_op jit(solution)/shard_map/all_to_all | solution.py:586
  39.8 0.1 copy.40
  39.8 0.1 reshape.56.refs_1_
  39.9 0.1 reshape_reshape.3
  40.0 0.0 copy-done
  40.0 7.5 %moments.2 = (bf16[64,144,128]{2,1,0:T(8,128)(2,1)}, f32[128,128]{1,0:T(8,128)S(1)}, f32[16,32,128]{2,1,0:T(8,128)S(1)}) custom-call(bf16[1024,1024]{1,0:T(8,128)(2,1)} %refs_1_.3, bf16[1024,128]{1,0:T(8,128)(2,1)S(1)} %collective-permute-done.refs_0_.refs_1_, f32[8,16,128]{2,1,0:T(8,128)S(1)} %all-to-all-done.1.refs_2_.refs_6_, f32[8,128]{1,0:T(8,128)S(1)} %bitcast.12, ...), custom_call_target="tpu_custom_call" | custom-call | flops 805306368 | bytes 7340032 | tf_op jit(solution)/shard_map/moments/pallas_call | solution.py:557
  47.5 0.0 all-to-all-done.refs_0_
  47.5 0.8 scan.1
  48.3 7.4 %all-to-all-start.2 = ((f32[32,8,128]{2,1,0:T(8,128)}), f32[32,8,128]{2,1,0:T(8,128)S(1)}, u32[]{:S(2)}, u32[]{:S(2)}) async-start(f32[32,8,128]{2,1,0:T(8,128)} %scan.1), calls=%async_computation.2 | async-start | bytes 262144 | tf_op jit(solution)/shard_map/all_to_all | solution.py:586
  55.7 7.5 %moments.3 = (bf16[64,144,128]{2,1,0:T(8,128)(2,1)}, f32[128,128]{1,0:T(8,128)S(1)}, f32[16,32,128]{2,1,0:T(8,128)S(1)}) custom-call(bf16[1024,1024]{1,0:T(8,128)(2,1)} %refs_1_.3, bf16[1024,128]{1,0:T(8,128)(2,1)S(1)} %collective-permute-done.refs_0_.refs_1_, ...), custom_call_target="tpu_custom_call", output_to_operand_aliasing={{0}: (9, {}), {1}: (10, {}), {2}: (11, {})} | custom-call | flops 805306368 | bytes 7340032 | tf_op jit(solution)/shard_map/moments/pallas_call | solution.py:557
  63.2 0.1 all-to-all-done.2
  63.4 7.8 %inputs.1 = (f32[64,128,128]{2,1,0:T(8,128)}, f32[8,8,128]{2,1,0:T(8,128)}, f32[128,128]{1,0:T(8,128)S(1)}, bf16[64,128,128]{2,1,0:T(8,128)(2,1)}) custom-call(f32[64,144,128]{2,1,0:T(8,128)} %get-tuple-element.45.refs_0_, f32[16,16,128]{2,1,0:T(8,128)S(1)} %bitcast.8, f32[8,128]{1,0:T(8,128)S(1)} %reshape.51.refs_2_, f32[8,128]{1,0:T(8,128)S(1)} %reshape.52.refs_3_, ...), custom_call_target="tpu_custom_call" | custom-call | flops 2415919104 | bytes 14680064 | tf_op jit(solution)/shard_map/inputs/pallas_call | solution.py:557
  71.1 6.6 %all-to-all-start.3 = ((f32[8,8,128]{2,1,0:T(8,128)}), f32[8,8,128]{2,1,0:T(8,128)S(1)}, u32[]{:S(2)}, u32[]{:S(2)}) async-start(f32[8,8,128]{2,1,0:T(8,128)} %get-tuple-element.61), calls=%async_computation.3 | async-start | bytes 65536 | tf_op jit(solution)/shard_map/all_to_all | solution.py:586
  77.8 7.4 %taps.1 = bf16[32,112,128]{2,1,0:T(8,128)(2,1)} custom-call(bf16[64,128,128]{2,1,0:T(8,128)(2,1)} %get-tuple-element.62.refs_0_, bf16[64,144,128]{2,1,0:T(8,128)(2,1)} %get-tuple-element.63.refs_1_, f32[128,128]{1,0:T(8,128)S(1)} %get-tuple-element.64.refs_2_), custom_call_target="tpu_custom_call" | custom-call | flops 536870912 | bytes 5242880 | tf_op jit(solution)/shard_map/taps/pallas_call | solution.py:557
  85.2 0.0 all-to-all-done.3.refs_4_
  85.2 8.1 %all-to-all-start.4 = ((bf16[32,112,128]{2,1,0:T(8,128)(2,1)}), bf16[32,112,128]{2,1,0:T(8,128)(2,1)S(1)}, u32[]{:S(2)}, u32[]{:S(2)}) async-start(bf16[32,112,128]{2,1,0:T(8,128)(2,1)} %taps.1), calls=%async_computation.4 | async-start | bytes 1835008 | tf_op jit(solution)/shard_map/all_to_all | solution.py:586
  93.3 4.2 %final.1 = (bf16[1024,1024]{1,0:T(8,128)(2,1)}, f32[8,128]{1,0:T(8,128)}) custom-call(f32[64,128,128]{2,1,0:T(8,128)} %get-tuple-element.60.refs_0_, bf16[1024,1024]{1,0:T(8,128)(2,1)} %refs_1_.3, f32[8,16,128]{2,1,0:T(8,128)S(1)} %all-to-all-done.1.refs_2_.refs_6_, f32[8,128]{1,0:T(8,128)S(1)} %bitcast.15, f32[8,8,128]{2,1,0:T(8,128)S(1)} %all-to-all-done.3.refs_4_), custom_call_target="tpu_custom_call" | custom-call | bytes 8388608 | tf_op jit(solution)/shard_map/final/pallas_call | solution.py:557
  97.6 11.5 %all-to-all-done.4.refs_0_ = bf16[32,112,128]{2,1,0:T(8,128)(2,1)S(1)} async-done(((bf16[32,112,128]{2,1,0:T(8,128)(2,1)}), bf16[32,112,128]{2,1,0:T(8,128)(2,1)S(1)}, u32[]{:S(2)}, u32[]{:S(2)}) %all-to-all-start.4) | async-done | bytes 917536 | tf_op jit(solution)/shard_map/all_to_all | solution.py:586
  109.1 0.7 outs.1
  109.8 0.1 reshape.59
  109.9 0.1 fusion.1
  110.0 0.1 copy.48
  110.1 0.1 copy.47
  110.1 0.6 subtract_multiply_fusion
  (2 shorter events, 0.0 us)
Async XLA Ops:
  0.6 8.2 %copy-start.2 = (f32[64,16]{0,1:T(8,128)S(1)}, f32[64,16]{0,1:T(8,128)}, u32[]{:S(2)}) copy-start(f32[64,16]{0,1:T(8,128)} %param.12) | copy-start | bytes 12292
  0.6 8.4 %copy-start.3 = (f32[64,16]{0,1:T(8,128)S(1)}, f32[64,16]{0,1:T(8,128)}, u32[]{:S(2)}) copy-start(f32[64,16]{0,1:T(8,128)} %param.11) | copy-start | bytes 12292
  0.7 22.1 %copy-start.1 = (f32[1024]{0:T(1024)S(1)}, f32[1024]{0:T(1024)}, u32[]{:S(2)}) copy-start(f32[1024]{0:T(1024)} %param.13) | copy-start | bytes 12292
  2.4 7.8 %collective-permute-start = (bf16[1024,128]{1,0:T(8,128)(2,1)S(1)}, bf16[1024,128]{1,0:T(8,128)(2,1)S(1)}, u32[]{:S(2)}, u32[]{:S(2)}) collective-permute-start(bf16[1024,128]{1,0:T(8,128)(2,1)S(1)} %get-tuple-element.41), channel_id=1, source_target_pairs={{0,8},{8,16},{16,24},{24,32},{32,40},{40,48},{48,56},{56,64},{64,7... | collective-permute-start | bytes 786440 | tf_op jit(solution)/shard_map/ppermute | solution.py:630
  6.9 7.7 %collective-permute-start.1 = (bf16[1024,128]{1,0:T(8,128)(2,1)S(1)}, bf16[1024,128]{1,0:T(8,128)(2,1)S(1)}, u32[]{:S(2)}, u32[]{:S(2)}) collective-permute-start(bf16[1024,128]{1,0:T(8,128)(2,1)S(1)} %get-tuple-element.43), channel_id=1, source_target_pairs={{8,0},{16,8},{24,16},{32,24},{40,32},{48,40},{56,48},{64,56},{72,6... | collective-permute-start | bytes 786440 | tf_op jit(solution)/shard_map/ppermute | solution.py:629
  14.6 16.4 %all-to-all-start.1 = ((f32[8,16,128]{2,1,0:T(8,128)}), f32[8,16,128]{2,1,0:T(8,128)S(1)}, u32[]{:S(2)}, u32[]{:S(2)}) async-start(f32[8,16,128]{2,1,0:T(8,128)} %edge.1), calls=%async_computation.1 | async-start | bytes 131072 | tf_op jit(solution)/shard_map/all_to_all | solution.py:586
  22.8 17.2 %copy-start = (f32[1024]{0:T(1024)S(1)}, f32[1024]{0:T(1024)}, u32[]{:S(2)}) copy-start(f32[1024]{0:T(1024)} %param.9) | copy-start | bytes 12292
  31.0 16.5 %all-to-all-start = ((f32[32,8,128]{2,1,0:T(8,128)}), f32[32,8,128]{2,1,0:T(8,128)S(1)}, u32[]{:S(2)}, u32[]{:S(2)}) async-start(f32[32,8,128]{2,1,0:T(8,128)} %bitcast.1), calls=%async_computation | async-start | bytes 262144 | tf_op jit(solution)/shard_map/all_to_all | solution.py:586
  48.3 15.0 %all-to-all-start.2 = ((f32[32,8,128]{2,1,0:T(8,128)}), f32[32,8,128]{2,1,0:T(8,128)S(1)}, u32[]{:S(2)}, u32[]{:S(2)}) async-start(f32[32,8,128]{2,1,0:T(8,128)} %scan.1), calls=%async_computation.2 | async-start | bytes 262144 | tf_op jit(solution)/shard_map/all_to_all | solution.py:586
  71.1 14.1 %all-to-all-start.3 = ((f32[8,8,128]{2,1,0:T(8,128)}), f32[8,8,128]{2,1,0:T(8,128)S(1)}, u32[]{:S(2)}, u32[]{:S(2)}) async-start(f32[8,8,128]{2,1,0:T(8,128)} %get-tuple-element.61), calls=%async_computation.3 | async-start | bytes 65536 | tf_op jit(solution)/shard_map/all_to_all | solution.py:586
  85.2 23.9 %all-to-all-start.4 = ((bf16[32,112,128]{2,1,0:T(8,128)(2,1)}), bf16[32,112,128]{2,1,0:T(8,128)(2,1)S(1)}, u32[]{:S(2)}, u32[]{:S(2)}) async-start(bf16[32,112,128]{2,1,0:T(8,128)(2,1)} %taps.1), calls=%async_computation.4 | async-start | bytes 1835008 | tf_op jit(solution)/shard_map/all_to_all | solution.py:586

commit v4 on v3

--- a/solution.py
+++ b/solution.py
@@ -440,7 +440,7 @@
     finish(at, write)
 
 
-def taps_kernel(nb, at, grad_ref, x_ref, pay_ref, out_ref, rows_ref):
+def taps_kernel(nb, steps, at, grad_ref, x_ref, pay_ref, keep_ref, send_ref, rows_ref):
     step = at[0]
     row, lane = iotas((B, B))
     lower = row >= lane
@@ -458,20 +458,30 @@
         held = nxt
     mirror = jnp.concatenate([mirror_matrix()] * 3, axis=0)
     taps = mm(fine(jnp.concatenate(rows, axis=0)), mirror, NN)
-    rows_ref[pl.ds(pl.multiple_of(GB * step, GB), GB), :] = taps
-    first = GB * 8
-    for line, row in ((first + step, 2), (first + 8 + step, 6), (first + 16 + 2 * step, 10)):
-        rows_ref[pl.ds(line, 1), :] = pay_ref[pl.ds(row, 1), :]
-    rows_ref[pl.ds(first + 17 + 2 * step, 1), :] = pay_ref[pl.ds(14, 1), :]
+    half = keep_ref.shape[0]
+    span = steps // 2
+    base = (step // span) * half
+    step = step % span
+    rows_ref[pl.ds(pl.multiple_of(base + GB * step, GB), GB), :] = taps
+    first = base + GB * span
+    for line, row in ((step, 2), (span + step, 6), (2 * span + 2 * step, 10)):
+        rows_ref[pl.ds(first + line, 1), :] = pay_ref[pl.ds(row, 1), :]
+    rows_ref[pl.ds(first + 2 * span + 2 * step + 1, 1), :] = pay_ref[pl.ds(14, 1), :]
 
     def write():
-        rows = rows_ref[...]
-        hi, lo = split(rows[first + 16 :])
-        rows = jnp.concatenate([rows.astype(bf16), lo], axis=0)
-        for i in range(out_ref.shape[0]):
-            out_ref[i] = rows
+        side = lax.axis_index("ctx") % 2
+        keep_ref[...] = rows_ref[pl.ds(pl.multiple_of(half * side, GB), half), :]
+        send_ref[...] = rows_ref[pl.ds(pl.multiple_of(half * (1 - side), GB), half), :]
 
     finish(at, write)
+
+
+def copies_kernel(fine_rows, keep_ref, got_ref, out_ref):
+    rows = keep_ref[...] + got_ref[...]
+    hi, lo = split(rows[rows.shape[0] - fine_rows :])
+    rows = jnp.concatenate([rows.astype(bf16), lo], axis=0)
+    for i in range(out_ref.shape[0]):
+        out_ref[i] = rows
 
 
 def final_kernel(nb, width, at, ig_ref, h_ref, sq_ref, gain_ref, raw_ref, out_ref, rms_ref):
@@ -513,16 +523,19 @@
 
 
 def outs_kernel(scale, in_ref, tap_ref, gain_ref, skip_ref, mom_ref):
-    total = in_ref[0].astype(f32)
-    for i in range(1, in_ref.shape[0]):
-        total = total + in_ref[i].astype(f32)
-    total = total * scale
-    start = 0
-    for ref in (tap_ref, gain_ref, skip_ref, mom_ref):
-        size = ref.shape[0]
-        ref[...] = total[start : start + size]
-        start += size
-    mom_ref[...] += total[start:]
+    for side in range(2):
+        total = in_ref[side].astype(f32)
+        for i in range(side + 2, in_ref.shape[0], 2):
+            total = total + in_ref[i].astype(f32)
+        total = total * scale
+        start = 0
+        for ref in (tap_ref, gain_ref, skip_ref, mom_ref):
+            size = ref.shape[0] // 2
+            found = total[start : start + size]
+            start += size
+            if ref is mom_ref:
+                found = found + total[start:]
+            ref[pl.ds(side * size, size), :] = found
 
 
 def call(
@@ -745,21 +758,31 @@
 
     ig, grad_mixed = in_hbm(ig, grad_mixed)
     raw = exchange(row_part, "ch")
-    extra = groups // 4
-    lines = groups + 2 * steps + 2 * extra
-    (payload,) = call(
-        functools.partial(taps_kernel, nb),
+    extra = groups // 8
+    half = groups // 2 + steps + extra
+    lines = half + extra
+    keep, send = call(
+        functools.partial(taps_kernel, nb, steps),
         "taps",
         [body, tall, pay],
-        ([full(n_ctx, lines, B)], [shape((n_ctx, lines, B), bf16)]),
+        ([full(half, B), full(half, B)], [shape((half, B), f32), shape((half, B), f32)]),
         (grad_mixed, units, mostly),
         flops=groups * 2 * 128 * 128 * 256,
         steps=steps,
         per=PER["taps"],
         moved=5 * 2**20,
-        scratch=[pltpu.VMEM((lines - extra, B), f32)],
-    )
-    raw, payload = lax.optimization_barrier((raw, payload))
+        scratch=[pltpu.VMEM((2 * half, B), f32)],
+    )
+    got = lax.ppermute(send, "ctx", [(i, i ^ 1) for i in range(n_ctx)])
+    (payload,) = call(
+        functools.partial(copies_kernel, extra),
+        "copies",
+        [full(half, B), full(half, B)],
+        ([full(n_ctx, lines, B)], [shape((n_ctx, lines, B), bf16)]),
+        (keep, got),
+        moved=2**19,
+    )
+    raw, payload, gain_late = lax.optimization_barrier((raw, payload, gain_flat))
     landed = exchange(payload, "ctx")
     grad_hidden, grad_inv_rms = call(
         functools.partial(final_kernel, nb, width),
@@ -769,7 +792,7 @@
             [wide, full(nb, B)],
             [shape((channels, tokens), bf16), shape((nb, B), f32)],
         ),
-        (ig, hidden, squares, gain_flat, raw),
+        (ig, hidden, squares, gain_late, raw),
         steps=steps,
         per=PER["final"],
         moved=8 * 2**20,

time: 111 us -> 107 us (0.964)
  waiting for transfers between devices: 16.1 us -> 12.1 us
    all_to_all x5, waiting for transfers between devices: 11.7 us -> 6.76 us  [exchange(): return lax.all_to_all(x, axis, 0, 0, tiled=True)]
    pallas_call x10 -> x11, Pallas kernels: 46.7 us -> 46.5 us  [call(): pl.pallas_call(body, name=name, grid=(steps // per,) if steps else (), in...]
  transfers between devices with their start and end apart: 7 -> 8, of which waited for: 4 -> 5; matrix products, arithmetic and copies ran while one was open for 1% -> 1% of each run, Pallas kernels for 32% -> 33%
where the time goes in v4:
time: 107 us; the launch traced here: 106 us
  Pallas kernels  46.5 us (43%)
  starting transfers between devices  45.4 us (42%)
  waiting for transfers between devices  12.1 us (11%)
    pallas_call x11, Pallas kernels, call(): pl.pallas_call(body, name=name, grid=(steps // per,) if steps else (), in...  46.5 us
    all_to_all x5, starting transfers between devices, exchange(): return lax.all_to_all(x, axis, 0, 0, tiled=True)  38.1 us
    all_to_all x5, waiting for transfers between devices, exchange(): return lax.all_to_all(x, axis, 0, 0, tiled=True)  6.76 us
    ppermute x1, starting transfers between devices, local(): h_prev = lax.ppermute(tail, 'ctx', [(i, i + 1) for i in range(n_ctx - 1)])  4.51 us
    ppermute x1, waiting for transfers between devices, local(): ct_next = lax.ppermute(head, 'ctx', [(i, i - 1) for i in range(1, n_ctx)])  3.63 us
  transfers between devices with their start and end apart: 8, of which 5 were waited for; matrix products, arithmetic and copies ran while one was open for 1% of the time, Pallas kernels for 33%

profile of v4, /device:TPU:1, one launch (start us, length us, event | category | flops | bytes accessed | tf_op | source)
XLA Modules:
  0.0 106.3 jit_solution(1961483556598065891)
XLA Ops:
  0.6 0.0 copy-start.2
  0.6 0.0 copy-start.3
  0.7 0.0 copy-start.1
  0.7 1.7 %prep.1 = (bf16[1024,128]{1,0:T(8,128)(2,1)S(1)}, bf16[1024,128]{1,0:T(8,128)(2,1)S(1)}, f32[8,128]{1,0:T(8,128)S(1)}) custom-call(bf16[1024,1024]{1,0:T(8,128)(2,1)} %refs_1_.3, bf16[1024,1024]{1,0:T(8,128)(2,1)} %refs_4_.3), custom_call_target="tpu_custom_call" | custom-call | bytes 3145728 | tf_op jit(solution)/shard_map/prep/pallas_call | solution.py:570
  2.4 4.5 %collective-permute-start = (bf16[1024,128]{1,0:T(8,128)(2,1)S(1)}, bf16[1024,128]{1,0:T(8,128)(2,1)S(1)}, u32[]{:S(2)}, u32[]{:S(2)}) collective-permute-start(bf16[1024,128]{1,0:T(8,128)(2,1)S(1)} %get-tuple-element.44), channel_id=1, source_target_pairs={{0,8},{8,16},{16,24},{24,32},{32,40},{40,48},{48,56},{56,64},{64,7... | collective-permute-start | bytes 786440 | tf_op jit(solution)/shard_map/ppermute | solution.py:643
  6.9 1.9 %collective-permute-start.1 = (bf16[1024,128]{1,0:T(8,128)(2,1)S(1)}, bf16[1024,128]{1,0:T(8,128)(2,1)S(1)}, u32[]{:S(2)}, u32[]{:S(2)}) collective-permute-start(bf16[1024,128]{1,0:T(8,128)(2,1)S(1)} %get-tuple-element.46), channel_id=1, source_target_pairs={{8,0},{16,8},{24,16},{32,24},{40,32},{48,40},{56,48},{64,56},{72,6... | collective-permute-start | bytes 786440 | tf_op jit(solution)/shard_map/ppermute | solution.py:642
  8.9 0.0 copy-done.2
  8.9 0.1 copy.37
  8.9 0.1 reshape.51.refs_2_
  9.0 0.0 copy-done.3
  9.0 0.1 copy.38
  9.1 0.1 reshape.52.refs_3_
  9.2 0.1 tile.9.refs_4_.refs_7_
  9.4 0.8 collective-permute-done.refs_0_.refs_1_
  10.2 0.8 edge.1
  11.0 3.6 %collective-permute-done.1.refs_1_ = bf16[1024,128]{1,0:T(8,128)(2,1)S(1)} collective-permute-done((bf16[1024,128]{1,0:T(8,128)(2,1)S(1)}, bf16[1024,128]{1,0:T(8,128)(2,1)S(1)}, u32[]{:S(2)}, u32[]{:S(2)}) %collective-permute-start.1) | collective-permute-done | bytes 262176 | tf_op jit(solution)/shard_map/ppermute | solution.py:642
  14.6 8.2 %all-to-all-start.1 = ((f32[8,16,128]{2,1,0:T(8,128)}), f32[8,16,128]{2,1,0:T(8,128)S(1)}, u32[]{:S(2)}, u32[]{:S(2)}) async-start(f32[8,16,128]{2,1,0:T(8,128)} %edge.1), calls=%async_computation.1 | async-start | bytes 131072 | tf_op jit(solution)/shard_map/all_to_all | solution.py:599
  22.8 0.0 copy-done.1
  22.8 0.0 copy-start
  22.8 8.2 %grads.1 = (f32[64,144,128]{2,1,0:T(8,128)}, f32[32,144,128]{2,1,0:T(8,128)}, f32[16,16,128]{2,1,0:T(8,128)}) custom-call(bf16[1024,1024]{1,0:T(8,128)(2,1)} %refs_4_.3, bf16[1024,128]{1,0:T(8,128)(2,1)S(1)} %collective-permute-done.1.refs_1_, f32[8,128]{1,0:T(8,128)S(1)} %reshape.51.refs_2_, f32[8,128]{1,0:T(8,128)S(1)} %reshape.52.refs_3_, ...), custom_call_target="tpu_custom_call" | custom-call | flops 1811939328 | bytes 14680064 | tf_op jit(solution)/shard_map/grads/pallas_call | solution.py:570
  31.0 0.0 all-to-all-done.1.refs_2_.refs_6_
  31.0 8.8 %all-to-all-start = ((f32[32,8,128]{2,1,0:T(8,128)}), f32[32,8,128]{2,1,0:T(8,128)S(1)}, u32[]{:S(2)}, u32[]{:S(2)}) async-start(f32[32,8,128]{2,1,0:T(8,128)} %bitcast.1), calls=%async_computation | async-start | bytes 262144 | tf_op jit(solution)/shard_map/all_to_all | solution.py:599
  39.8 0.1 copy.40
  39.8 0.1 reshape.56.refs_1_
  39.9 0.1 reshape_reshape.3
  40.0 0.0 copy-done
  40.0 7.5 %moments.2 = (bf16[64,144,128]{2,1,0:T(8,128)(2,1)}, f32[128,128]{1,0:T(8,128)S(1)}, f32[16,32,128]{2,1,0:T(8,128)S(1)}) custom-call(bf16[1024,1024]{1,0:T(8,128)(2,1)} %refs_1_.3, bf16[1024,128]{1,0:T(8,128)(2,1)S(1)} %collective-permute-done.refs_0_.refs_1_, f32[8,16,128]{2,1,0:T(8,128)S(1)} %all-to-all-done.1.refs_2_.refs_6_, f32[8,128]{1,0:T(8,128)S(1)} %bitcast.12, ...), custom_call_target="tpu_custom_call" | custom-call | flops 805306368 | bytes 7340032 | tf_op jit(solution)/shard_map/moments/pallas_call | solution.py:570
  47.5 0.0 all-to-all-done.refs_0_
  47.5 0.8 scan.1
  48.4 7.4 %all-to-all-start.2 = ((f32[32,8,128]{2,1,0:T(8,128)}), f32[32,8,128]{2,1,0:T(8,128)S(1)}, u32[]{:S(2)}, u32[]{:S(2)}) async-start(f32[32,8,128]{2,1,0:T(8,128)} %scan.1), calls=%async_computation.2 | async-start | bytes 262144 | tf_op jit(solution)/shard_map/all_to_all | solution.py:599
  55.7 7.5 %moments.3 = (bf16[64,144,128]{2,1,0:T(8,128)(2,1)}, f32[128,128]{1,0:T(8,128)S(1)}, f32[16,32,128]{2,1,0:T(8,128)S(1)}) custom-call(bf16[1024,1024]{1,0:T(8,128)(2,1)} %refs_1_.3, bf16[1024,128]{1,0:T(8,128)(2,1)S(1)} %collective-permute-done.refs_0_.refs_1_, ...), custom_call_target="tpu_custom_call", output_to_operand_aliasing={{0}: (9, {}), {1}: (10, {}), {2}: (11, {})} | custom-call | flops 805306368 | bytes 7340032 | tf_op jit(solution)/shard_map/moments/pallas_call | solution.py:570
  63.2 0.1 all-to-all-done.2
  63.4 7.8 %inputs.1 = (f32[64,128,128]{2,1,0:T(8,128)}, f32[8,8,128]{2,1,0:T(8,128)}, f32[128,128]{1,0:T(8,128)S(1)}, bf16[64,128,128]{2,1,0:T(8,128)(2,1)}) custom-call(f32[64,144,128]{2,1,0:T(8,128)} %get-tuple-element.48.refs_0_, f32[16,16,128]{2,1,0:T(8,128)S(1)} %bitcast.8, f32[8,128]{1,0:T(8,128)S(1)} %reshape.51.refs_2_, f32[8,128]{1,0:T(8,128)S(1)} %reshape.52.refs_3_, ...), custom_call_target="tpu_custom_call" | custom-call | flops 2415919104 | bytes 14680064 | tf_op jit(solution)/shard_map/inputs/pallas_call | solution.py:570
  71.2 6.6 %all-to-all-start.3 = ((f32[8,8,128]{2,1,0:T(8,128)}), f32[8,8,128]{2,1,0:T(8,128)S(1)}, u32[]{:S(2)}, u32[]{:S(2)}) async-start(f32[8,8,128]{2,1,0:T(8,128)} %get-tuple-element.64), calls=%async_computation.3 | async-start | bytes 65536 | tf_op jit(solution)/shard_map/all_to_all | solution.py:599
  77.8 6.4 %taps.1 = (f32[48,128]{1,0:T(8,128)S(1)}, f32[48,128]{1,0:T(8,128)S(1)}) custom-call(bf16[64,128,128]{2,1,0:T(8,128)(2,1)} %get-tuple-element.65.refs_0_, bf16[64,144,128]{2,1,0:T(8,128)(2,1)} %get-tuple-element.66.refs_1_, f32[128,128]{1,0:T(8,128)S(1)} %get-tuple-element.67.refs_2_), custom_call_target="tpu_custom_call" | custom-call | flops 536870912 | bytes 5242880 | tf_op jit(solution)/shard_map/taps/pallas_call | solution.py:570
  84.2 0.8 collective-permute-start.2
  85.0 0.8 collective-permute-done.2.refs_1_
  85.9 0.8 copies.1
  86.7 0.0 all-to-all-done.3.refs_4_
  86.7 7.2 %all-to-all-start.4 = ((bf16[32,56,128]{2,1,0:T(8,128)(2,1)}), bf16[32,56,128]{2,1,0:T(8,128)(2,1)S(1)}, u32[]{:S(2)}, u32[]{:S(2)}) async-start(bf16[32,56,128]{2,1,0:T(8,128)(2,1)} %copies.1), calls=%async_computation.4 | async-start | bytes 917504 | tf_op jit(solution)/shard_map/all_to_all | solution.py:599
  93.9 4.2 %final.1 = (bf16[1024,1024]{1,0:T(8,128)(2,1)}, f32[8,128]{1,0:T(8,128)}) custom-call(f32[64,128,128]{2,1,0:T(8,128)} %get-tuple-element.63.refs_0_, bf16[1024,1024]{1,0:T(8,128)(2,1)} %refs_1_.3, f32[8,16,128]{2,1,0:T(8,128)S(1)} %all-to-all-done.1.refs_2_.refs_6_, f32[8,128]{1,0:T(8,128)S(1)} %bitcast.15, f32[8,8,128]{2,1,0:T(8,128)S(1)} %all-to-all-done.3.refs_4_), custom_call_target="tpu_custom_call" | custom-call | bytes 8388608 | tf_op jit(solution)/shard_map/final/pallas_call | solution.py:570
  98.1 6.6 %all-to-all-done.4.refs_0_ = bf16[32,56,128]{2,1,0:T(8,128)(2,1)S(1)} async-done(((bf16[32,56,128]{2,1,0:T(8,128)(2,1)}), bf16[32,56,128]{2,1,0:T(8,128)(2,1)S(1)}, u32[]{:S(2)}, u32[]{:S(2)}) %all-to-all-start.4) | async-done | bytes 458784 | tf_op jit(solution)/shard_map/all_to_all | solution.py:599
  104.7 0.7 outs.1
  105.4 0.1 reshape.59
  105.5 0.1 fusion.1
  105.5 0.1 copy.48
  105.6 0.1 copy.47
  105.7 0.6 subtract_multiply_fusion
  (2 shorter events, 0.0 us)
Async XLA Ops:
  0.6 8.2 %copy-start.2 = (f32[64,16]{0,1:T(8,128)S(1)}, f32[64,16]{0,1:T(8,128)}, u32[]{:S(2)}) copy-start(f32[64,16]{0,1:T(8,128)} %param.12) | copy-start | bytes 12292
  0.6 8.4 %copy-start.3 = (f32[64,16]{0,1:T(8,128)S(1)}, f32[64,16]{0,1:T(8,128)}, u32[]{:S(2)}) copy-start(f32[64,16]{0,1:T(8,128)} %param.11) | copy-start | bytes 12292
  0.7 22.1 %copy-start.1 = (f32[1024]{0:T(1024)S(1)}, f32[1024]{0:T(1024)}, u32[]{:S(2)}) copy-start(f32[1024]{0:T(1024)} %param.13) | copy-start | bytes 12292
  2.4 7.8 %collective-permute-start = (bf16[1024,128]{1,0:T(8,128)(2,1)S(1)}, bf16[1024,128]{1,0:T(8,128)(2,1)S(1)}, u32[]{:S(2)}, u32[]{:S(2)}) collective-permute-start(bf16[1024,128]{1,0:T(8,128)(2,1)S(1)} %get-tuple-element.44), channel_id=1, source_target_pairs={{0,8},{8,16},{16,24},{24,32},{32,40},{40,48},{48,56},{56,64},{64,7... | collective-permute-start | bytes 786440 | tf_op jit(solution)/shard_map/ppermute | solution.py:643
  6.9 7.7 %collective-permute-start.1 = (bf16[1024,128]{1,0:T(8,128)(2,1)S(1)}, bf16[1024,128]{1,0:T(8,128)(2,1)S(1)}, u32[]{:S(2)}, u32[]{:S(2)}) collective-permute-start(bf16[1024,128]{1,0:T(8,128)(2,1)S(1)} %get-tuple-element.46), channel_id=1, source_target_pairs={{8,0},{16,8},{24,16},{32,24},{40,32},{48,40},{56,48},{64,56},{72,6... | collective-permute-start | bytes 786440 | tf_op jit(solution)/shard_map/ppermute | solution.py:642
  14.6 16.4 %all-to-all-start.1 = ((f32[8,16,128]{2,1,0:T(8,128)}), f32[8,16,128]{2,1,0:T(8,128)S(1)}, u32[]{:S(2)}, u32[]{:S(2)}) async-start(f32[8,16,128]{2,1,0:T(8,128)} %edge.1), calls=%async_computation.1 | async-start | bytes 131072 | tf_op jit(solution)/shard_map/all_to_all | solution.py:599
  22.8 17.2 %copy-start = (f32[1024]{0:T(1024)S(1)}, f32[1024]{0:T(1024)}, u32[]{:S(2)}) copy-start(f32[1024]{0:T(1024)} %param.9) | copy-start | bytes 12292
  31.0 16.5 %all-to-all-start = ((f32[32,8,128]{2,1,0:T(8,128)}), f32[32,8,128]{2,1,0:T(8,128)S(1)}, u32[]{:S(2)}, u32[]{:S(2)}) async-start(f32[32,8,128]{2,1,0:T(8,128)} %bitcast.1), calls=%async_computation | async-start | bytes 262144 | tf_op jit(solution)/shard_map/all_to_all | solution.py:599
  48.4 15.0 %all-to-all-start.2 = ((f32[32,8,128]{2,1,0:T(8,128)}), f32[32,8,128]{2,1,0:T(8,128)S(1)}, u32[]{:S(2)}, u32[]{:S(2)}) async-start(f32[32,8,128]{2,1,0:T(8,128)} %scan.1), calls=%async_computation.2 | async-start | bytes 262144 | tf_op jit(solution)/shard_map/all_to_all | solution.py:599
  71.2 15.5 %all-to-all-start.3 = ((f32[8,8,128]{2,1,0:T(8,128)}), f32[8,8,128]{2,1,0:T(8,128)S(1)}, u32[]{:S(2)}, u32[]{:S(2)}) async-start(f32[8,8,128]{2,1,0:T(8,128)} %get-tuple-element.64), calls=%async_computation.3 | async-start | bytes 65536 | tf_op jit(solution)/shard_map/all_to_all | solution.py:599
  84.2 1.6 %collective-permute-start.2 = (f32[48,128]{1,0:T(8,128)S(1)}, f32[48,128]{1,0:T(8,128)S(1)}, u32[]{:S(2)}, u32[]{:S(2)}) collective-permute-start(f32[48,128]{1,0:T(8,128)S(1)} %get-tuple-element.69), channel_id=1, source_target_pairs={{0,8},{8,0},{16,24},{24,16},{32,40},{40,32},{48,56},{56,48},{64,72... | collective-permute-start | bytes 73736 | tf_op jit(solution)/shard_map/ppermute | solution.py:776
  86.7 18.0 %all-to-all-start.4 = ((bf16[32,56,128]{2,1,0:T(8,128)(2,1)}), bf16[32,56,128]{2,1,0:T(8,128)(2,1)S(1)}, u32[]{:S(2)}, u32[]{:S(2)}) async-start(bf16[32,56,128]{2,1,0:T(8,128)(2,1)} %copies.1), calls=%async_computation.4 | async-start | bytes 917504 | tf_op jit(solution)/shard_map/all_to_all | solution.py:599

commit v5 on v4

--- a/solution.py
+++ b/solution.py
@@ -248,15 +248,14 @@
             )
         )
         mixes = [mix(2 * p), mix(2 * p + 1)]
-        lifted = mm(
-            jnp.concatenate(mixes, axis=1), jnp.concatenate([hi, lo], axis=1), NN
-        )
-        return mixes, lifted[:, :B] + lifted[:, B:], pair_rates
+        return mixes, jnp.concatenate([hi, lo], axis=1), pair_rates
 
     skip_parts = []
     corrs = []
 
-    def second_stage(p, mixes, lifted, pair_rates):
+    def second_stage(p, mixes, weights, pair_rates):
+        lifted = mm(jnp.concatenate(mixes, axis=1), weights, NN)
+        lifted = lifted[:, :B] + lifted[:, B:]
         for h in range(2):
             rows = pl.ds(16 * (2 * p + h), 16)
             mixed = mixes[h]

time: 107 us -> 105 us (0.981)
  Pallas kernels: 46.5 us -> 44.7 us
  starting transfers between devices: 45.4 us -> 43.8 us
  waiting for transfers between devices: 12.1 us -> 13.6 us
    pallas_call x11, Pallas kernels: 46.5 us -> 44.7 us  [call(): pl.pallas_call(body, name=name, grid=(steps // per,) if steps else (), in...]
    all_to_all x5, waiting for transfers between devices: 6.76 us -> 8.32 us  [exchange(): return lax.all_to_all(x, axis, 0, 0, tiled=True)]
    all_to_all x5, starting transfers between devices: 38.1 us -> 36.6 us  [exchange(): return lax.all_to_all(x, axis, 0, 0, tiled=True)]
  transfers between devices with their start and end apart: 8 -> 8, of which waited for: 5 -> 6; matrix products, arithmetic and copies ran while one was open for 1% -> 1% of each run, Pallas kernels for 33% -> 32%
where the time goes in v5:
time: 105 us
  Pallas kernels  44.7 us (43%)
  starting transfers between devices  43.8 us (42%)
  waiting for transfers between devices  13.6 us (13%)
    pallas_call x11, Pallas kernels, call(): pl.pallas_call(body, name=name, grid=(steps // per,) if steps else (), in...  44.7 us
    all_to_all x5, starting transfers between devices, exchange(): return lax.all_to_all(x, axis, 0, 0, tiled=True)  36.6 us
    all_to_all x5, waiting for transfers between devices, exchange(): return lax.all_to_all(x, axis, 0, 0, tiled=True)  8.32 us
    ppermute x1, starting transfers between devices, local(): h_prev = lax.ppermute(tail, 'ctx', [(i, i + 1) for i in range(n_ctx - 1)])  4.51 us
    ppermute x1, waiting for transfers between devices, local(): ct_next = lax.ppermute(head, 'ctx', [(i, i - 1) for i in range(1, n_ctx)])  3.63 us
  transfers between devices with their start and end apart: 8, of which 6 were waited for; matrix products, arithmetic and copies ran while one was open for 1% of the time, Pallas kernels for 32%

profile of v5, /device:TPU:1, one launch (start us, length us, event | category | flops | bytes accessed | tf_op | source)
XLA Modules:
  0.0 104.6 jit_solution(2232560496112069346)
XLA Ops:
  0.6 0.0 copy-start.2
  0.6 0.0 copy-start.3
  0.7 0.0 copy-start.1
  0.7 1.7 %prep.1 = (bf16[1024,128]{1,0:T(8,128)(2,1)S(1)}, bf16[1024,128]{1,0:T(8,128)(2,1)S(1)}, f32[8,128]{1,0:T(8,128)S(1)}) custom-call(bf16[1024,1024]{1,0:T(8,128)(2,1)} %refs_1_.3, bf16[1024,1024]{1,0:T(8,128)(2,1)} %refs_4_.3), custom_call_target="tpu_custom_call" | custom-call | bytes 3145728 | tf_op jit(solution)/shard_map/prep/pallas_call | solution.py:569
  2.4 4.5 %collective-permute-start = (bf16[1024,128]{1,0:T(8,128)(2,1)S(1)}, bf16[1024,128]{1,0:T(8,128)(2,1)S(1)}, u32[]{:S(2)}, u32[]{:S(2)}) collective-permute-start(bf16[1024,128]{1,0:T(8,128)(2,1)S(1)} %get-tuple-element.44), channel_id=1, source_target_pairs={{0,8},{8,16},{16,24},{24,32},{32,40},{40,48},{48,56},{56,64},{64,7... | collective-permute-start | bytes 786440 | tf_op jit(solution)/shard_map/ppermute | solution.py:642
  6.9 1.9 %collective-permute-start.1 = (bf16[1024,128]{1,0:T(8,128)(2,1)S(1)}, bf16[1024,128]{1,0:T(8,128)(2,1)S(1)}, u32[]{:S(2)}, u32[]{:S(2)}) collective-permute-start(bf16[1024,128]{1,0:T(8,128)(2,1)S(1)} %get-tuple-element.46), channel_id=1, source_target_pairs={{8,0},{16,8},{24,16},{32,24},{40,32},{48,40},{56,48},{64,56},{72,6... | collective-permute-start | bytes 786440 | tf_op jit(solution)/shard_map/ppermute | solution.py:641
  8.9 0.0 copy-done.2
  8.9 0.1 copy.37
  8.9 0.1 reshape.51.refs_2_
  9.0 0.0 copy-done.3
  9.0 0.1 copy.38
  9.1 0.1 reshape.52.refs_3_
  9.2 0.1 tile.9.refs_4_.refs_7_
  9.4 0.8 collective-permute-done.refs_0_.refs_1_
  10.2 0.8 edge.1
  11.0 3.6 %collective-permute-done.1.refs_1_ = bf16[1024,128]{1,0:T(8,128)(2,1)S(1)} collective-permute-done((bf16[1024,128]{1,0:T(8,128)(2,1)S(1)}, bf16[1024,128]{1,0:T(8,128)(2,1)S(1)}, u32[]{:S(2)}, u32[]{:S(2)}) %collective-permute-start.1) | collective-permute-done | bytes 262176 | tf_op jit(solution)/shard_map/ppermute | solution.py:641
  14.6 8.2 %all-to-all-start.1 = ((f32[8,16,128]{2,1,0:T(8,128)}), f32[8,16,128]{2,1,0:T(8,128)S(1)}, u32[]{:S(2)}, u32[]{:S(2)}) async-start(f32[8,16,128]{2,1,0:T(8,128)} %edge.1), calls=%async_computation.1 | async-start | bytes 131072 | tf_op jit(solution)/shard_map/all_to_all | solution.py:598
  22.8 0.0 copy-done.1
  22.8 0.0 copy-start
  22.8 8.2 %grads.1 = (f32[64,144,128]{2,1,0:T(8,128)}, f32[32,144,128]{2,1,0:T(8,128)}, f32[16,16,128]{2,1,0:T(8,128)}) custom-call(bf16[1024,1024]{1,0:T(8,128)(2,1)} %refs_4_.3, bf16[1024,128]{1,0:T(8,128)(2,1)S(1)} %collective-permute-done.1.refs_1_, f32[8,128]{1,0:T(8,128)S(1)} %reshape.51.refs_2_, f32[8,128]{1,0:T(8,128)S(1)} %reshape.52.refs_3_, ...), custom_call_target="tpu_custom_call" | custom-call | flops 1811939328 | bytes 14680064 | tf_op jit(solution)/shard_map/grads/pallas_call | solution.py:569
  31.0 0.0 all-to-all-done.1.refs_2_.refs_6_
  31.0 8.8 %all-to-all-start = ((f32[32,8,128]{2,1,0:T(8,128)}), f32[32,8,128]{2,1,0:T(8,128)S(1)}, u32[]{:S(2)}, u32[]{:S(2)}) async-start(f32[32,8,128]{2,1,0:T(8,128)} %bitcast.1), calls=%async_computation | async-start | bytes 262144 | tf_op jit(solution)/shard_map/all_to_all | solution.py:598
  39.8 0.1 copy.40
  39.8 0.1 reshape.56.refs_1_
  39.9 0.1 reshape_reshape.3
  40.0 0.0 copy-done
  40.0 6.5 %moments.2 = (bf16[64,144,128]{2,1,0:T(8,128)(2,1)}, f32[128,128]{1,0:T(8,128)S(1)}, f32[16,32,128]{2,1,0:T(8,128)S(1)}) custom-call(bf16[1024,1024]{1,0:T(8,128)(2,1)} %refs_1_.3, bf16[1024,128]{1,0:T(8,128)(2,1)S(1)} %collective-permute-done.refs_0_.refs_1_, f32[8,16,128]{2,1,0:T(8,128)S(1)} %all-to-all-done.1.refs_2_.refs_6_, f32[8,128]{1,0:T(8,128)S(1)} %bitcast.12, ...), custom_call_target="tpu_custom_call" | custom-call | flops 805306368 | bytes 7340032 | tf_op jit(solution)/shard_map/moments/pallas_call | solution.py:569
  46.5 0.9 all-to-all-done.refs_0_
  47.4 0.8 scan.1
  48.2 6.5 %all-to-all-start.2 = ((f32[32,8,128]{2,1,0:T(8,128)}), f32[32,8,128]{2,1,0:T(8,128)S(1)}, u32[]{:S(2)}, u32[]{:S(2)}) async-start(f32[32,8,128]{2,1,0:T(8,128)} %scan.1), calls=%async_computation.2 | async-start | bytes 262144 | tf_op jit(solution)/shard_map/all_to_all | solution.py:598
  54.7 6.8 %moments.3 = (bf16[64,144,128]{2,1,0:T(8,128)(2,1)}, f32[128,128]{1,0:T(8,128)S(1)}, f32[16,32,128]{2,1,0:T(8,128)S(1)}) custom-call(bf16[1024,1024]{1,0:T(8,128)(2,1)} %refs_1_.3, bf16[1024,128]{1,0:T(8,128)(2,1)S(1)} %collective-permute-done.refs_0_.refs_1_, ...), custom_call_target="tpu_custom_call", output_to_operand_aliasing={{0}: (9, {}), {1}: (10, {}), {2}: (11, {})} | custom-call | flops 805306368 | bytes 7340032 | tf_op jit(solution)/shard_map/moments/pallas_call | solution.py:569
  61.5 0.8 all-to-all-done.2
  62.4 7.8 %inputs.1 = (f32[64,128,128]{2,1,0:T(8,128)}, f32[8,8,128]{2,1,0:T(8,128)}, f32[128,128]{1,0:T(8,128)S(1)}, bf16[64,128,128]{2,1,0:T(8,128)(2,1)}) custom-call(f32[64,144,128]{2,1,0:T(8,128)} %get-tuple-element.48.refs_0_, f32[16,16,128]{2,1,0:T(8,128)S(1)} %bitcast.8, f32[8,128]{1,0:T(8,128)S(1)} %reshape.51.refs_2_, f32[8,128]{1,0:T(8,128)S(1)} %reshape.52.refs_3_, ...), custom_call_target="tpu_custom_call" | custom-call | flops 2415919104 | bytes 14680064 | tf_op jit(solution)/shard_map/inputs/pallas_call | solution.py:569
  70.1 6.6 %all-to-all-start.3 = ((f32[8,8,128]{2,1,0:T(8,128)}), f32[8,8,128]{2,1,0:T(8,128)S(1)}, u32[]{:S(2)}, u32[]{:S(2)}) async-start(f32[8,8,128]{2,1,0:T(8,128)} %get-tuple-element.64), calls=%async_computation.3 | async-start | bytes 65536 | tf_op jit(solution)/shard_map/all_to_all | solution.py:598
  76.8 6.4 %taps.1 = (f32[48,128]{1,0:T(8,128)S(1)}, f32[48,128]{1,0:T(8,128)S(1)}) custom-call(bf16[64,128,128]{2,1,0:T(8,128)(2,1)} %get-tuple-element.65.refs_0_, bf16[64,144,128]{2,1,0:T(8,128)(2,1)} %get-tuple-element.66.refs_1_, f32[128,128]{1,0:T(8,128)S(1)} %get-tuple-element.67.refs_2_), custom_call_target="tpu_custom_call" | custom-call | flops 536870912 | bytes 5242880 | tf_op jit(solution)/shard_map/taps/pallas_call | solution.py:569
  83.2 0.8 collective-permute-start.2
  84.0 0.8 collective-permute-done.2.refs_1_
  84.8 0.8 copies.1
  85.7 0.0 all-to-all-done.3.refs_4_
  85.7 6.5 %all-to-all-start.4 = ((bf16[32,56,128]{2,1,0:T(8,128)(2,1)}), bf16[32,56,128]{2,1,0:T(8,128)(2,1)S(1)}, u32[]{:S(2)}, u32[]{:S(2)}) async-start(bf16[32,56,128]{2,1,0:T(8,128)(2,1)} %copies.1), calls=%async_computation.4 | async-start | bytes 917504 | tf_op jit(solution)/shard_map/all_to_all | solution.py:598
  92.2 4.2 %final.1 = (bf16[1024,1024]{1,0:T(8,128)(2,1)}, f32[8,128]{1,0:T(8,128)}) custom-call(f32[64,128,128]{2,1,0:T(8,128)} %get-tuple-element.63.refs_0_, bf16[1024,1024]{1,0:T(8,128)(2,1)} %refs_1_.3, f32[8,16,128]{2,1,0:T(8,128)S(1)} %all-to-all-done.1.refs_2_.refs_6_, f32[8,128]{1,0:T(8,128)S(1)} %bitcast.15, f32[8,8,128]{2,1,0:T(8,128)S(1)} %all-to-all-done.3.refs_4_), custom_call_target="tpu_custom_call" | custom-call | bytes 8388608 | tf_op jit(solution)/shard_map/final/pallas_call | solution.py:569
  96.4 6.6 %all-to-all-done.4.refs_0_ = bf16[32,56,128]{2,1,0:T(8,128)(2,1)S(1)} async-done(((bf16[32,56,128]{2,1,0:T(8,128)(2,1)}), bf16[32,56,128]{2,1,0:T(8,128)(2,1)S(1)}, u32[]{:S(2)}, u32[]{:S(2)}) %all-to-all-start.4) | async-done | bytes 458784 | tf_op jit(solution)/shard_map/all_to_all | solution.py:598
  103.0 0.7 outs.1
  103.7 0.1 reshape.59
  103.8 0.1 fusion.1
  103.8 0.1 copy.48
  103.9 0.1 copy.47
  104.0 0.6 subtract_multiply_fusion
  (2 shorter events, 0.0 us)
Async XLA Ops:
  0.6 8.2 %copy-start.2 = (f32[64,16]{0,1:T(8,128)S(1)}, f32[64,16]{0,1:T(8,128)}, u32[]{:S(2)}) copy-start(f32[64,16]{0,1:T(8,128)} %param.12) | copy-start | bytes 12292
  0.6 8.4 %copy-start.3 = (f32[64,16]{0,1:T(8,128)S(1)}, f32[64,16]{0,1:T(8,128)}, u32[]{:S(2)}) copy-start(f32[64,16]{0,1:T(8,128)} %param.11) | copy-start | bytes 12292
  0.7 22.1 %copy-start.1 = (f32[1024]{0:T(1024)S(1)}, f32[1024]{0:T(1024)}, u32[]{:S(2)}) copy-start(f32[1024]{0:T(1024)} %param.13) | copy-start | bytes 12292
  2.4 7.8 %collective-permute-start = (bf16[1024,128]{1,0:T(8,128)(2,1)S(1)}, bf16[1024,128]{1,0:T(8,128)(2,1)S(1)}, u32[]{:S(2)}, u32[]{:S(2)}) collective-permute-start(bf16[1024,128]{1,0:T(8,128)(2,1)S(1)} %get-tuple-element.44), channel_id=1, source_target_pairs={{0,8},{8,16},{16,24},{24,32},{32,40},{40,48},{48,56},{56,64},{64,7... | collective-permute-start | bytes 786440 | tf_op jit(solution)/shard_map/ppermute | solution.py:642
  6.9 7.7 %collective-permute-start.1 = (bf16[1024,128]{1,0:T(8,128)(2,1)S(1)}, bf16[1024,128]{1,0:T(8,128)(2,1)S(1)}, u32[]{:S(2)}, u32[]{:S(2)}) collective-permute-start(bf16[1024,128]{1,0:T(8,128)(2,1)S(1)} %get-tuple-element.46), channel_id=1, source_target_pairs={{8,0},{16,8},{24,16},{32,24},{40,32},{48,40},{56,48},{64,56},{72,6... | collective-permute-start | bytes 786440 | tf_op jit(solution)/shard_map/ppermute | solution.py:641
  14.6 16.4 %all-to-all-start.1 = ((f32[8,16,128]{2,1,0:T(8,128)}), f32[8,16,128]{2,1,0:T(8,128)S(1)}, u32[]{:S(2)}, u32[]{:S(2)}) async-start(f32[8,16,128]{2,1,0:T(8,128)} %edge.1), calls=%async_computation.1 | async-start | bytes 131072 | tf_op jit(solution)/shard_map/all_to_all | solution.py:598
  22.8 17.2 %copy-start = (f32[1024]{0:T(1024)S(1)}, f32[1024]{0:T(1024)}, u32[]{:S(2)}) copy-start(f32[1024]{0:T(1024)} %param.9) | copy-start | bytes 12292
  31.0 16.4 %all-to-all-start = ((f32[32,8,128]{2,1,0:T(8,128)}), f32[32,8,128]{2,1,0:T(8,128)S(1)}, u32[]{:S(2)}, u32[]{:S(2)}) async-start(f32[32,8,128]{2,1,0:T(8,128)} %bitcast.1), calls=%async_computation | async-start | bytes 262144 | tf_op jit(solution)/shard_map/all_to_all | solution.py:598
  48.2 14.2 %all-to-all-start.2 = ((f32[32,8,128]{2,1,0:T(8,128)}), f32[32,8,128]{2,1,0:T(8,128)S(1)}, u32[]{:S(2)}, u32[]{:S(2)}) async-start(f32[32,8,128]{2,1,0:T(8,128)} %scan.1), calls=%async_computation.2 | async-start | bytes 262144 | tf_op jit(solution)/shard_map/all_to_all | solution.py:598
  70.1 15.5 %all-to-all-start.3 = ((f32[8,8,128]{2,1,0:T(8,128)}), f32[8,8,128]{2,1,0:T(8,128)S(1)}, u32[]{:S(2)}, u32[]{:S(2)}) async-start(f32[8,8,128]{2,1,0:T(8,128)} %get-tuple-element.64), calls=%async_computation.3 | async-start | bytes 65536 | tf_op jit(solution)/shard_map/all_to_all | solution.py:598
  83.2 1.6 %collective-permute-start.2 = (f32[48,128]{1,0:T(8,128)S(1)}, f32[48,128]{1,0:T(8,128)S(1)}, u32[]{:S(2)}, u32[]{:S(2)}) collective-permute-start(f32[48,128]{1,0:T(8,128)S(1)} %get-tuple-element.69), channel_id=1, source_target_pairs={{0,8},{8,0},{16,24},{24,16},{32,40},{40,32},{48,56},{56,48},{64,72... | collective-permute-start | bytes 73736 | tf_op jit(solution)/shard_map/ppermute | solution.py:775
  85.7 17.4 %all-to-all-start.4 = ((bf16[32,56,128]{2,1,0:T(8,128)(2,1)}), bf16[32,56,128]{2,1,0:T(8,128)(2,1)S(1)}, u32[]{:S(2)}, u32[]{:S(2)}) async-start(bf16[32,56,128]{2,1,0:T(8,128)(2,1)} %copies.1), calls=%async_computation.4 | async-start | bytes 917504 | tf_op jit(solution)/shard_map/all_to_all | solution.py:598
